TPU v7x, 128 devices: a whole 4x4x4 slice. The times are simulated.
128 devices in a mesh: req: 32 (over x, z, core), tp: 4 (over y).
Axes of the slice: x: 4, y: 4, z: 4, core: 2. Of those that a mesh axis runs over, the one named last changes fastest.
Arguments:
- tokens: bfloat16 [1024, 2048], P('req'), may hold values from -6 to 6
- deal_order: int32 [1024], replicated, may hold values from 0 to 1023, as said below
- page_table: int32 [1024, 6], P('req'), may hold values from 0 to 1343, as said below
- lengths: int32 [1024], P('req'), may hold values from 1 to 768, as said below
- qkv_weight: bfloat16 [2048, 3, 2048], P(None, None, 'tp'), may hold values from -0.125 to 0.125
- out_weight: bfloat16 [2048, 2048], P('tp'), may hold values from -0.125 to 0.125
- up_weight: bfloat16 [2048, 4096], P(None, 'tp'), may hold values from -0.125 to 0.125
- down_weight: bfloat16 [4096, 2048], P('tp'), may hold values from -0.09375 to 0.09375
- key_cache: bfloat16 [2, 1344, 128, 2048], P(None, 'req', None, 'tp')
- value_cache: bfloat16 [2, 1344, 128, 2048], P(None, 'req', None, 'tp'), may hold values from -6 to 6
- attn_norm: float32 [2, 2048], replicated
- mlp_norm: float32 [2, 2048], replicated
Outputs:
- output: bfloat16 [1024, 2048], P('req')
Inputs may be any that keep to these rules, and one draw needn't show every extreme that they name: `deal_order`: A permutation: every request is placed in exactly one slot. Of the 32 requests in the slots s // 32 = d of one block d, at most 2 come from one source block of rows r // 32 = j, and some pair of blocks has exactly 2. `page_table`: row s holds the pages of the request in dealt slot s: its first ceil(lengths[s] / 128) entries are pages of the block s // 32 * 42 to s // 32 * 42 + 41, no page serves two slots, and the remaining entries repeat the row's first page. `lengths`: A request fills at most 6 pages; the slots s // 32 = d of one block d fill at most 42 pages together, and some block fills exactly that many.
All inputs are finite; a program needn't handle non-finite values.
Results may differ from a plain program's by a relative error of at most 0.034.
Values may be sent and summed in bfloat16 or wider, within the bound.
No kernel may reach another device: no remote copies, remote signals or barrier semaphores. Data moves between devices by JAX's collectives and lax.ppermute only.
A program may use at most 448 MiB of HBM per device.

v0:
```python
import math

import jax
import jax.numpy as jnp
from jax import lax
from jax.sharding import PartitionSpec as P

HD = 128


epsilon = 1e-06


def layer_norm(row_total, gain_bias):
    row_mean = jnp.mean(row_total, axis=-1, keepdims=True)
    centered = row_total - row_mean
    row_var = jnp.mean(centered * centered, axis=-1, keepdims=True)
    return (centered * lax.rsqrt(row_var + epsilon) * gain_bias[0] + gain_bias[1]).astype(
        jnp.bfloat16
    )


def post_norm(partial_term, residual, gain_bias):
    row_total = lax.psum(partial_term.astype(jnp.bfloat16), "tp").astype(
        jnp.float32
    ) + residual.astype(jnp.float32)
    return layer_norm(row_total, gain_bias)


def head_masks(feat_share, head_dim):
    head_count = feat_share // head_dim
    owner = jnp.arange(feat_share, dtype=jnp.int32) // head_dim
    return owner[None, :] == jnp.arange(head_count, dtype=jnp.int32)[:, None]


def spread_query(query_flat, mask):
    return jnp.where(mask[None, :, :], query_flat[:, None, :], jnp.zeros((), query_flat.dtype))


def own_scores(query_flat, key_new, mask, score_scale):
    product = query_flat.astype(jnp.float32) * key_new.astype(jnp.float32)
    return jnp.sum(jnp.where(mask[None, :, :], product[:, None, :], 0.0), axis=-1) * score_scale


def finish_mix(scores, own_score, value_new, mask, mix_fn):
    row_max = jnp.maximum(jnp.max(scores, axis=-1), own_score)
    exp_cache = jnp.exp(scores - row_max[..., None])
    exp_own = jnp.exp(own_score - row_max)
    row_total = jnp.sum(exp_cache, axis=-1) + exp_own
    cache_weights = (exp_cache / row_total[..., None]).astype(jnp.bfloat16)
    own_weight = (exp_own / row_total).astype(jnp.bfloat16).astype(jnp.float32)
    mixed_wide = mix_fn(cache_weights)
    mixed_cache = jnp.sum(jnp.where(mask[None, :, :], mixed_wide, 0.0), axis=1)
    own_spread = jnp.sum(jnp.where(mask[None, :, :], own_weight[:, :, None], 0.0), axis=1)
    return mixed_cache + own_spread * value_new.astype(jnp.float32)


def attend_pool(
    query_flat, key_new, value_new, key_pool, value_pool, local_table, lengths, score_scale, mask
):
    req_rows, feat_share = query_flat.shape
    pool_pages, page_len = (key_pool.shape[0], key_pool.shape[1])
    slot_count = local_table.shape[1]
    page_ids = jnp.arange(pool_pages, dtype=jnp.int32)
    slot_ids = jnp.arange(slot_count, dtype=jnp.int32)
    slot_used = slot_ids[None, :] * page_len < lengths[:, None]
    page_hit = (local_table[:, :, None] == page_ids[None, None, :]) & slot_used[:, :, None]
    start_pos = jnp.sum(jnp.where(page_hit, slot_ids[None, :, None] * page_len, 0), axis=1)
    is_owned = jnp.any(page_hit, axis=1)
    position = start_pos[:, :, None] + jnp.arange(page_len, dtype=jnp.int32)[None, None, :]
    is_valid = (is_owned[:, :, None] & (position < lengths[:, None, None])).reshape(
        req_rows, pool_pages * page_len
    )
    flat_keys = key_pool.reshape(pool_pages * page_len, feat_share)
    flat_values = value_pool.reshape(pool_pages * page_len, feat_share)
    query_wide = spread_query(query_flat, mask)
    scores = (
        jnp.einsum("rhf,tf->rht", query_wide, flat_keys, preferred_element_type=jnp.float32)
        * score_scale
    )
    scores = jnp.where(is_valid[:, None, :], scores, -jnp.inf)
    own_score = own_scores(query_flat, key_new, mask, score_scale)

    def mix_pool(cache_weights):
        return jnp.einsum(
            "rht,tf->rhf", cache_weights, flat_values, preferred_element_type=jnp.float32
        )

    return finish_mix(scores, own_score, value_new, mask, mix_pool)


def local(
    tokens,
    deal_order,
    page_table,
    lengths,
    qkv_weight,
    out_weight,
    up_weight,
    down_weight,
    key_cache,
    value_cache,
    attn_norm,
    mlp_norm,
):
    req_rows, model_width = tokens.shape
    tp_count = lax.axis_size("tp")
    req_index = lax.axis_index("req")
    feat_share = model_width // tp_count
    score_scale = 1.0 / math.sqrt(HD)
    mask = head_masks(feat_share, HD)
    dealt_here = lax.dynamic_slice_in_dim(deal_order, req_index * req_rows, req_rows)
    everyone = lax.all_gather(tokens, "req", axis=0, tiled=True)
    current = jnp.take(everyone, dealt_here, axis=0)
    pool_pages = key_cache.shape[1]
    local_table = page_table - req_index * pool_pages
    qkv_flat = qkv_weight.reshape(model_width, 3 * feat_share)
    for layer_index in range(key_cache.shape[0]):
        projected = jnp.dot(current, qkv_flat, preferred_element_type=jnp.float32).astype(
            jnp.bfloat16
        )
        query_flat = projected[:, :feat_share]
        key_new = projected[:, feat_share : 2 * feat_share]
        value_new = projected[:, 2 * feat_share :]
        key_pool = key_cache[layer_index]
        value_pool = value_cache[layer_index]
        attended = attend_pool(
            query_flat,
            key_new,
            value_new,
            key_pool,
            value_pool,
            local_table,
            lengths,
            score_scale,
            mask,
        )
        attended = attended.astype(jnp.bfloat16)
        attn_term = jnp.dot(attended, out_weight, preferred_element_type=jnp.float32)
        hidden = post_norm(attn_term, current, attn_norm)
        up_proj = jnp.dot(hidden, up_weight, preferred_element_type=jnp.float32)
        activated = jax.nn.gelu(up_proj, approximate=True).astype(jnp.bfloat16)
        down_term = jnp.dot(activated, down_weight, preferred_element_type=jnp.float32)
        current = post_norm(down_term, hidden, mlp_norm)
    request_count = deal_order.shape[0]
    inverse = (
        jnp.zeros_like(deal_order).at[deal_order].set(jnp.arange(request_count, dtype=jnp.int32))
    )
    inverse_here = lax.dynamic_slice_in_dim(inverse, req_index * req_rows, req_rows)
    returned = lax.all_gather(current, "req", axis=0, tiled=True)
    result = jnp.take(returned, inverse_here, axis=0)
    return result


def solution(mesh):
    in_specs = (
        P("req", None),
        P(),
        P("req", None),
        P("req"),
        P(None, None, "tp"),
        P("tp", None),
        P(None, "tp"),
        P("tp", None),
        P(None, "req", None, "tp"),
        P(None, "req", None, "tp"),
        P(),
        P(),
    )
    out_specs = P("req", None)
    return jax.shard_map(local, mesh=mesh, in_specs=in_specs, out_specs=out_specs, check_vma=False)
```

profile of v0, /device:TPU:1, one launch (start us, length us, event | category | flops | bytes accessed | tf_op | source)
XLA Modules:
  0.0 334.8 jit_solution(1223456797249646341)
XLA Ops:
  6.5 0.7 all-gather.3.cloned.1.call-update
  7.3 8.8 %copy.16 = bf16[2048,3,512]{0,2,1:T(8,128)(2,1)} copy(bf16[2048,3,512]{2,0,1:T(8,128)(2,1)} %param.18) | data formatting | bytes 12582912 | tf_op args[4]
  16.4 0.1 fusion.41
  16.5 0.1 select_reduce_fusion.4
  16.7 9.8 %fusion.77 = (bf16[1,42,128,512]{3,2,1,0:T(8,128)(2,1)}, bf16[1,42,128,512]{3,2,1,0:T(8,128)(2,1)}) fusion(bf16[2,42,128,512]{3,2,1,0:T(8,128)(2,1)} %param.22), kind=kLoop, calls=%fused_computation.147 | loop fusion | bytes 22020096 | tf_op jit(solution)/shard_map/slice | solution.py:125
  26.4 9.7 %fusion.78 = (bf16[1,42,128,512]{3,2,1,0:T(8,128)(2,1)}, bf16[1,42,128,512]{3,2,1,0:T(8,128)(2,1)}) fusion(bf16[2,42,128,512]{3,2,1,0:T(8,128)(2,1)} %param.23), kind=kLoop, calls=%fused_computation.148 | loop fusion | bytes 22020096 | tf_op jit(solution)/shard_map/slice | solution.py:126
  36.2 0.3 add.173
  36.4 0.3 and.65
  36.7 0.3 fusion.11
  37.0 22.6 %all-gather.3.cloned.1.call-done = bf16[1024,2048]{1,0:T(8,128)(2,1)} async-done(((bf16[32,2048]{1,0:T(8,128)(2,1)}), bf16[1024,2048]{1,0:T(8,128)(2,1)}) %all-gather.3.cloned.1.call-update) | async-done | bytes 4194320 | tf_op jit(solution)/shard_map/all_gather | solution.py:113
  59.7 3.5 %gather_fusion = bf16[32,2048]{1,0:T(8,128)(2,1)S(1)} fusion(bf16[1024,2048]{1,0:T(8,128)(2,1)} %all-gather.3.cloned.1.call-done, s32[1024]{0:T(1024)S(1)} %pad_clamp_fusion.1), kind=kCustom, calls=%fused_computation.clone | custom fusion | bytes 262272 | tf_op jit(solution)/shard_map/jit(_take)/gather | solution.py:114
  63.2 4.9 %convolution_convert_fusion.1 = bf16[32,1536]{1,0:T(8,128)(2,1)S(1)} fusion(bf16[2048,1536]{0,1:T(8,128)(2,1)} %bitcast.44, bf16[32,2048]{1,0:T(8,128)(2,1)S(1)} %gather_fusion, pred[32]{0:T(512)(128)(4,1)S(1)} %get-tuple-element.8), kind=kOutput, calls=%fused_computation.14 | convolution fusion | flops 201441280 | bytes 6520864 | tf_op jit(solution)/shard_map/dot_general | solution.py:119
  68.2 0.1 select_reduce_fusion.3
  68.3 2.0 fusion.81
  70.3 0.5 fusion.2
  70.9 0.1 select_reduce_fusion.2
  71.0 1.0 fusion.8
  72.1 1.1 convolution_convert_fusion.5
  73.3 38.0 %all-reduce.5.cloned.1.call-done = bf16[32,2048]{1,0:T(8,128)(2,1)} async-done(((bf16[32,2048]{1,0:T(8,128)(2,1)}), bf16[32,2048]{1,0:T(8,128)(2,1)}) %all-reduce.5.cloned.1.call-update) | async-done | bytes 131088 | tf_op jit(solution)/shard_map/psum | solution.py:24
  111.3 1.1 fusion.13
  112.5 1.1 multiply_reduce_fusion.3
  113.6 1.1 add_convert_fusion.3
  114.7 5.7 %convolution_convert_fusion.4 = bf16[32,2048]{1,0:T(8,128)(2,1)} fusion(bf16[1024,2048]{1,0:T(8,128)(2,1)} %param.21, bf16[32,2048]{1,0:T(8,128)(2,1)S(1)} %add_convert_fusion.3, bf16[2048,1024]{1,0:T(8,128)(2,1)} %param.20), kind=kOutput, calls=%fused_computation.17 | convolution fusion | flops 268795904 | bytes 8650752 | tf_op jit(solution)/shard_map/dot_general | solution.py:143
  120.5 0.2 all-reduce.9.cloned.1.call-start
  120.7 41.5 %all-reduce.7.cloned.1.call-done = bf16[32,2048]{1,0:T(8,128)(2,1)} async-done(((bf16[32,2048]{1,0:T(8,128)(2,1)}), bf16[32,2048]{1,0:T(8,128)(2,1)}) %all-reduce.7.cloned.1.call-update) | async-done | bytes 131088 | tf_op jit(solution)/shard_map/psum | solution.py:24
  162.2 1.0 fusion.15
  163.3 1.1 multiply_reduce_fusion.2
  164.4 1.0 add_convert_fusion.2
  165.4 4.9 %convolution_convert_fusion = bf16[32,1536]{1,0:T(8,128)(2,1)S(1)} fusion(bf16[32,2048]{1,0:T(8,128)(2,1)S(1)} %add_convert_fusion.2, bf16[2048,1536]{0,1:T(8,128)(2,1)} %bitcast.45), kind=kOutput, calls=%fused_computation.13 | convolution fusion | flops 201375744 | bytes 6520832 | tf_op jit(solution)/shard_map/dot_general | solution.py:119
  170.3 0.1 select_reduce_fusion.1
  170.5 4.7 %fusion.82 = (f32[32,4]{0,1:T(4,128)S(1)}, f32[32,4,5376]{2,0,1:T(8,128)S(1)}) fusion(bf16[5376,512,1]{1,0,2:T(8,128)(2,1)} %bitcast.46, pred[4,512]{1,0:T(4,128)(4,1)S(1)} %iota_compare_fusion.1, bf16[32,512]{1,0:T(8,128)(2,1)S(1)} %slice.67, pred[32,5376]{1,0:T(8,128)(4,1)S(1)} %fusion.11), kind=kOutput, calls=%fused_computation.152 | convolution fusion | flops 706772864 | bytes 8464896 | tf_op jit(solution)/shard_map/rhf,tf->rht/dot_general | solution.py:78
  175.1 0.5 fusion.3
  175.7 0.1 select_reduce_fusion
  175.8 1.0 fusion.9
  176.9 1.1 convolution_convert_fusion.3
  178.1 41.7 %all-reduce.9.cloned.1.call-done = bf16[32,2048]{1,0:T(8,128)(2,1)} async-done(((bf16[32,2048]{1,0:T(8,128)(2,1)}), bf16[32,2048]{1,0:T(8,128)(2,1)}) %all-reduce.9.cloned.1.call-update) | async-done | bytes 131088 | tf_op jit(solution)/shard_map/psum | solution.py:24
  219.7 1.0 fusion.17
  220.8 1.1 multiply_reduce_fusion.1
  221.9 1.0 add_convert_fusion.1
  222.9 5.7 %convolution_convert_fusion.2 = bf16[32,2048]{1,0:T(8,128)(2,1)} fusion(bf16[1024,2048]{1,0:T(8,128)(2,1)} %param.21, bf16[32,2048]{1,0:T(8,128)(2,1)S(1)} %add_convert_fusion.1, bf16[2048,1024]{1,0:T(8,128)(2,1)} %param.20), kind=kOutput, calls=%fused_computation.15 | convolution fusion | flops 268795904 | bytes 8650752 | tf_op jit(solution)/shard_map/dot_general | solution.py:143
  228.7 41.7 %all-reduce.11.cloned.1.call-done = bf16[32,2048]{1,0:T(8,128)(2,1)} async-done(((bf16[32,2048]{1,0:T(8,128)(2,1)}), bf16[32,2048]{1,0:T(8,128)(2,1)}) %all-reduce.11.cloned.1.call-update) | async-done | bytes 131088 | tf_op jit(solution)/shard_map/psum | solution.py:24
  270.4 1.0 fusion.19
  271.5 1.1 multiply_reduce_fusion
  272.6 1.7 add_convert_fusion
  274.3 4.3 %scatter_custom_fusion = s32[1024]{0:T(1024)S(1)} fusion(s32[1024]{0:T(1024)S(1)} %compare_select_fusion, s32[1024]{0:T(1024)S(1)} %iota.51, s32[]{:T(128)} %constant.32.clone.1), kind=kCustom, calls=%fused_computation.111 | custom fusion | bytes 4100 | tf_op jit(solution)/shard_map/scatter | solution.py:147
  278.7 45.0 %all-gather.5.cloned.1.call-done = bf16[1024,2048]{1,0:T(8,128)(2,1)} async-done(((bf16[32,2048]{1,0:T(8,128)(2,1)}), bf16[1024,2048]{1,0:T(8,128)(2,1)}) %all-gather.5.cloned.1.call-update) | async-done | bytes 4194320 | tf_op jit(solution)/shard_map/all_gather | solution.py:150
  323.7 3.5 %gather_fusion.1 = bf16[32,2048]{1,0:T(8,128)(2,1)S(1)} fusion(bf16[1024,2048]{1,0:T(8,128)(2,1)} %all-gather.5.cloned.1.call-done, s32[1024]{0:T(1024)S(1)} %pad_clamp_fusion), kind=kCustom, calls=%fused_computation.1.clone | custom fusion | bytes 262272 | tf_op jit(solution)/shard_map/jit(_take)/gather | solution.py:151
  327.2 0.7 broadcast_select_fusion
  (64 shorter events, 0.8 us)
Async XLA Ops:
  6.5 65.5 %copy-start = (bf16[512,2048]{1,0:T(8,128)(2,1)S(1)}, bf16[512,2048]{1,0:T(8,128)(2,1)}, u32[]{:S(2)}) copy-start(bf16[512,2048]{1,0:T(8,128)(2,1)} %param.19) | copy-start | bytes 6291460
  6.5 53.1 %all-gather.3.cloned.1.call-start = ((), (), s32[]{:S(2)}) async-start(), calls=%async_computation | async-start | bytes 4325376 | tf_op jit(solution)/shard_map/all_gather | solution.py:113
  7.3 104.1 %all-reduce.5.cloned.1.call-start = ((), (), s32[]{:S(2)}) async-start(), calls=%async_computation.1 | async-start | bytes 262144 | tf_op jit(solution)/shard_map/psum | solution.py:24
  7.3 8.9 %copy-start.4 = (s32[1024]{0:T(1024)S(1)}, s32[1024]{0:T(1024)}, u32[]{:S(2)}) copy-start(s32[1024]{0:T(1024)} %param.15) | copy-start | bytes 12292
  7.3 9.0 %copy-start.6 = (s32[32]{0:T(128)S(1)}, s32[32]{0:T(128)}, u32[]{:S(2)}) copy-start(s32[32]{0:T(128)} %param.17) | copy-start | bytes 388
  7.3 9.1 %copy-start.5 = (s32[32,6]{0,1:T(8,128)S(1)}, s32[32,6]{0,1:T(8,128)}, u32[]{:S(2)}) copy-start(s32[32,6]{0,1:T(8,128)} %param.16) | copy-start | bytes 2308
  63.2 5.1 %copy-start.1 = (bf16[1,42,128,512]{3,2,1,0:T(8,128)(2,1)S(1)}, bf16[1,42,128,512]{3,2,1,0:T(8,128)(2,1)}, u32[]{:S(2)}) copy-start(bf16[1,42,128,512]{3,2,1,0:T(8,128)(2,1)} %get-tuple-element.11) | copy-start | bytes 16515076
  68.1 2.9 slice-start.2
  68.3 2.7 slice-start.3
  71.0 2.3 copy-start.2
  73.2 89.0 %all-reduce.7.cloned.1.call-start = ((), (), s32[]{:S(2)}) async-start(), calls=%async_computation.2 | async-start | bytes 262144 | tf_op jit(solution)/shard_map/psum | solution.py:24
  114.7 6.0 %copy-start.3 = (f32[2,2048]{1,0:T(2,128)S(1)}, f32[2,2048]{1,0:T(2,128)}, u32[]{:S(2)}) copy-start(f32[2,2048]{1,0:T(2,128)} %param.25) | copy-start | bytes 49156
  120.5 99.3 %all-reduce.9.cloned.1.call-start = ((), (), s32[]{:S(2)}) async-start(), calls=%async_computation.3 | async-start | bytes 262144 | tf_op jit(solution)/shard_map/psum | solution.py:24
  165.4 10.4 %slice-start = ((s8[5505024]{0:T(1024)(128)(4,1)}), s8[4194304]{0:T(1024)(128)(4,1)S(1)}, s32[]{:S(2)}) async-start(s8[5505024]{0:T(1024)(128)(4,1)} %bitcast.48), calls=%async_computation.6 | async-start | bytes 8388608
  170.5 5.4 %slice-start.1 = ((s8[5505024]{0:T(1024)(128)(4,1)}), s8[1310720]{0:T(1024)(128)(4,1)S(1)}, s32[]{:S(2)}) async-start(s8[5505024]{0:T(1024)(128)(4,1)} %bitcast.48), calls=%async_computation.7 | async-start | bytes 2621440
  178.0 92.4 %all-reduce.11.cloned.1.call-start = ((), (), s32[]{:S(2)}) async-start(), calls=%async_computation.4 | async-start | bytes 262144 | tf_op jit(solution)/shard_map/psum | solution.py:24
  228.7 95.1 %all-gather.5.cloned.1.call-start = ((), (), s32[]{:S(2)}) async-start(), calls=%async_computation.5 | async-start | bytes 4325376 | tf_op jit(solution)/shard_map/all_gather | solution.py:150
Sparse Core Ops, SparseCore 0:
  9.6 50.0 all-gather.2
  73.3 37.9 all-reduce.4
  120.6 41.5 all-reduce.6
  178.1 41.5 all-reduce.8
  228.8 41.5 all-reduce.10
  274.4 49.2 all-gather.4
where the time goes:
time: 335 us
  waiting for transfers between devices  231 us (69%)
  local copies, waits for them, and re-layouts  40.3 us (12%)
  matrix products  32.2 us (10%)
  other arithmetic  16.7 us (5%)
  between operations  13.9 us (4%)
    psum x4, waiting for transfers between devices, post_norm(): lax.psum(partial_term.astype(jnp.bfloat16), 'tp').astype(jnp.float32)  163 us
    all_gather x1, waiting for transfers between devices, local(): returned = lax.all_gather(current, 'req', axis=0, tiled=True)  45 us
    all_gather x1, waiting for transfers between devices, local(): everyone = lax.all_gather(tokens, 'req', axis=0, tiled=True)  22.6 us
    dot_general x2, matrix products, local(): jnp.dot(activated, down_weight, preferred_element_type=jnp.float32)  11.4 us
    dot_general x2, matrix products, local(): jnp.dot(current, qkv_flat, preferred_element_type=jnp.float32)  9.8 us
    slice x1, local copies, waits for them, and re-layouts, local(): key_pool = key_cache[layer_index]  9.76 us
    slice x1, local copies, waits for them, and re-layouts, local(): value_pool = value_cache[layer_index]  9.75 us
    unnamed x23, local copies, waits for them, and re-layouts  8.92 us
  transfers between devices with their start and end apart: 6, of which 6 were waited for; matrix products, arithmetic and copies ran while one was open for 10% of the time, Pallas kernels for 0%

commit v1 on v0

--- a/solution.py
+++ b/solution.py
@@ -6,25 +6,54 @@
 from jax.sharding import PartitionSpec as P
 
 HD = 128
-
-
-epsilon = 1e-06
+CAP = 2
+EPS = 1e-6
+BF = jnp.bfloat16
+F32 = jnp.float32
 
 
 def layer_norm(row_total, gain_bias):
     row_mean = jnp.mean(row_total, axis=-1, keepdims=True)
     centered = row_total - row_mean
     row_var = jnp.mean(centered * centered, axis=-1, keepdims=True)
-    return (centered * lax.rsqrt(row_var + epsilon) * gain_bias[0] + gain_bias[1]).astype(
-        jnp.bfloat16
-    )
+    return (centered * lax.rsqrt(row_var + EPS) * gain_bias[0] + gain_bias[1]).astype(BF)
 
 
 def post_norm(partial_term, residual, gain_bias):
-    row_total = lax.psum(partial_term.astype(jnp.bfloat16), "tp").astype(
-        jnp.float32
-    ) + residual.astype(jnp.float32)
-    return layer_norm(row_total, gain_bias)
+    part = partial_term.astype(BF)
+    size = lax.axis_size("tp")
+    total = part.astype(F32)
+    for step in range(1, size):
+        moved = lax.ppermute(part, "tp", [(i, (i + step) % size) for i in range(size)])
+        total = total + moved.astype(F32)
+    return layer_norm(total + residual.astype(F32), gain_bias)
+
+
+def deal_maps(deal_order, req_index, rows, blocks):
+    here = deal_order.reshape(blocks, rows) - req_index * rows
+    row_ids = jnp.arange(rows, dtype=jnp.int32)
+    sent = jnp.any(here[:, :, None] == row_ids[None, None, :], axis=1)
+    sent_f = sent.astype(F32)
+    earlier = (row_ids[:, None] < row_ids[None, :]).astype(F32)
+    rank = jnp.dot(sent_f, earlier, precision=lax.Precision.HIGHEST)
+    ranks = jnp.arange(CAP, dtype=F32)
+    send = (sent[:, None, :] & (rank[:, None, :] == ranks[None, :, None])).astype(BF)
+    mine = lax.dynamic_slice_in_dim(deal_order, req_index * rows, rows)
+    source = mine // rows
+    order = jnp.sum(
+        (source[:, None] == source[None, :]) & (mine[None, :] < mine[:, None]), axis=1
+    )
+    place = source * CAP + order
+    take = (place[:, None] == jnp.arange(blocks * CAP, dtype=jnp.int32)[None, :]).astype(BF)
+    return send.reshape(blocks * CAP, rows), take
+
+
+def exchange(rows_here, send, take, blocks):
+    width = rows_here.shape[1]
+    outgoing = jnp.dot(send, rows_here, preferred_element_type=F32).astype(BF)
+    outgoing = outgoing.reshape(blocks, CAP, width)
+    incoming = lax.all_to_all(outgoing, "req", 0, 0).reshape(blocks * CAP, width)
+    return jnp.dot(take, incoming, preferred_element_type=F32).astype(BF)
 
 
 def head_masks(feat_share, head_dim):
@@ -109,9 +138,9 @@
     feat_share = model_width // tp_count
     score_scale = 1.0 / math.sqrt(HD)
     mask = head_masks(feat_share, HD)
-    dealt_here = lax.dynamic_slice_in_dim(deal_order, req_index * req_rows, req_rows)
-    everyone = lax.all_gather(tokens, "req", axis=0, tiled=True)
-    current = jnp.take(everyone, dealt_here, axis=0)
+    blocks = lax.axis_size("req")
+    send, take = deal_maps(deal_order, req_index, req_rows, blocks)
+    current = exchange(tokens, send, take, blocks)
     pool_pages = key_cache.shape[1]
     local_table = page_table - req_index * pool_pages
     qkv_flat = qkv_weight.reshape(model_width, 3 * feat_share)
@@ -142,14 +171,7 @@
         activated = jax.nn.gelu(up_proj, approximate=True).astype(jnp.bfloat16)
         down_term = jnp.dot(activated, down_weight, preferred_element_type=jnp.float32)
         current = post_norm(down_term, hidden, mlp_norm)
-    request_count = deal_order.shape[0]
-    inverse = (
-        jnp.zeros_like(deal_order).at[deal_order].set(jnp.arange(request_count, dtype=jnp.int32))
-    )
-    inverse_here = lax.dynamic_slice_in_dim(inverse, req_index * req_rows, req_rows)
-    returned = lax.all_gather(current, "req", axis=0, tiled=True)
-    result = jnp.take(returned, inverse_here, axis=0)
-    return result
+    return exchange(current, take.T, send.T, blocks)
 
 
 def solution(mesh):

time: 335 us -> 140 us (0.42)
  waiting for transfers between devices: 231 us -> 27.8 us
  starting transfers between devices: 0.39 us -> 37.5 us
  between operations: 13.9 us -> 0.39 us
  local copies, waits for them, and re-layouts: 40.3 us -> 31 us
  other arithmetic: 16.7 us -> 7.41 us
    psum x4 -> x0, waiting for transfers between devices: 163 us -> none  [post_norm(): lax.psum(partial_term.astype(jnp.bfloat16), 'tp').astype(jnp.float32)]
    all_gather x2 -> x0, waiting for transfers between devices: 67.6 us -> none  [the longest x1 45 us: local(): returned = lax.all_gather(current, 'req', axis=0, tiled=True)]
    all_to_all x0 -> x2, starting transfers between devices: none -> 19.6 us  [exchange(): lax.all_to_all(outgoing, 'req', 0, 0).reshape(blocks * CAP, width)]
    ppermute x0 -> x12, waiting for transfers between devices: none -> 18.8 us  [post_norm(): lax.ppermute(part, 'tp', [(i, (i + step) % size) for i in range(size)])]
    ppermute x0 -> x12, starting transfers between devices: none -> 17.9 us  [post_norm(): lax.ppermute(part, 'tp', [(i, (i + step) % size) for i in range(size)])]
    all_to_all x0 -> x2, waiting for transfers between devices: none -> 8.95 us  [exchange(): lax.all_to_all(outgoing, 'req', 0, 0).reshape(blocks * CAP, width)]
    gather x2 -> x0, local copies, waits for them, and re-layouts: 6.99 us -> none  [the longest x1 3.49 us: local(): current = jnp.take(everyone, dealt_here, axis=0)]
    convert_element_type x4 -> x0, other arithmetic: 4.8 us -> none  [layer_norm(): (centered * lax.rsqrt(row_var + epsilon) * gain_bias[0] + gain_bias[1]).a...]
  transfers between devices with their start and end apart: 6 -> 14, of which waited for: 6 -> 11; matrix products, arithmetic and copies ran while one was open for 10% -> 23% of each run, Pallas kernels for 0% -> 0%
where the time goes in v1:
time: 140 us; the launch traced here: 139 us
  starting transfers between devices  37.5 us (27%)
  matrix products  35 us (25%)
  local copies, waits for them, and re-layouts  31 us (22%)
  waiting for transfers between devices  27.8 us (20%)
  other arithmetic  7.41 us (5%)
    all_to_all x2, starting transfers between devices, exchange(): lax.all_to_all(outgoing, 'req', 0, 0).reshape(blocks * CAP, width)  19.6 us
    ppermute x12, waiting for transfers between devices, post_norm(): lax.ppermute(part, 'tp', [(i, (i + step) % size) for i in range(size)])  18.8 us
    ppermute x12, starting transfers between devices, post_norm(): lax.ppermute(part, 'tp', [(i, (i + step) % size) for i in range(size)])  17.9 us
    dot_general x2, matrix products, local(): jnp.dot(activated, down_weight, preferred_element_type=jnp.float32)  10.2 us
    dot_general x2, matrix products, local(): jnp.dot(current, qkv_flat, preferred_element_type=jnp.float32)  9.8 us
    slice x1, local copies, waits for them, and re-layouts, local(): value_pool = value_cache[layer_index]  9.7 us
    slice x1, local copies, waits for them, and re-layouts, local(): key_pool = key_cache[layer_index]  9.67 us
    dot_general x2, matrix products, attend_pool(): jnp.einsum('rhf,tf->rht', query_wide, flat_keys, preferred_element_type=j...  9.32 us
  transfers between devices with their start and end apart: 14, of which 11 were waited for; matrix products, arithmetic and copies ran while one was open for 23% of the time, Pallas kernels for 0%

profile of v1, /device:TPU:1, one launch (start us, length us, event | category | flops | bytes accessed | tf_op | source)
XLA Modules:
  0.0 139.1 jit_solution(3705088496645432771)
XLA Ops:
  0.0 0.8 broadcast_subtract_fusion.1
  1.5 1.2 convolution_convert_fusion.1
  2.7 0.9 reshape.234
  3.5 9.4 %all-to-all-start = ((bf16[32,2,2048]{2,1,0:T(2,128)(2,1)}), bf16[32,2,2048]{2,1,0:T(2,128)(2,1)S(1)}, u32[]{:S(2)}, u32[]{:S(2)}) async-start(bf16[32,2,2048]{2,1,0:T(2,128)(2,1)} %reshape.234), calls=%async_computation | async-start | bytes 524288 | tf_op jit(solution)/shard_map/all_to_all | solution.py:55
  13.0 0.7 broadcast_subtract_fusion
  13.7 0.7 broadcast_compare_fusion
  14.7 0.8 and_select_fusion
  15.6 9.7 %fusion.87 = (bf16[1,42,128,512]{3,2,1,0:T(8,128)(2,1)}, bf16[1,42,128,512]{3,2,1,0:T(8,128)(2,1)}) fusion(bf16[2,42,128,512]{3,2,1,0:T(8,128)(2,1)} %param.20), kind=kLoop, calls=%fused_computation.160 | loop fusion | bytes 22020096 | tf_op jit(solution)/shard_map/slice | solution.py:154
  25.3 9.7 %fusion.88 = (bf16[1,42,128,512]{3,2,1,0:T(8,128)(2,1)}, bf16[1,42,128,512]{3,2,1,0:T(8,128)(2,1)}) fusion(bf16[2,42,128,512]{3,2,1,0:T(8,128)(2,1)} %param.21), kind=kLoop, calls=%fused_computation.161 | loop fusion | bytes 22020096 | tf_op jit(solution)/shard_map/slice | solution.py:155
  35.9 8.8 %copy.24 = bf16[2048,3,512]{0,2,1:T(8,128)(2,1)} copy(bf16[2048,3,512]{2,0,1:T(8,128)(2,1)} %param.16) | data formatting | bytes 12582912 | tf_op args[4]
  45.1 4.9 %convolution_convert_fusion.3 = bf16[32,1536]{1,0:T(8,128)(2,1)S(1)} fusion(bf16[32,2048]{1,0:T(8,128)(2,1)S(1)} %convolution_convert_fusion.8, bf16[2048,1536]{0,1:T(8,128)(2,1)} %bitcast.50), kind=kOutput, calls=%fused_computation.14 | convolution fusion | flops 201375744 | bytes 6520832 | tf_op jit(solution)/shard_map/dot_general | solution.py:148
  50.2 4.7 %fusion.91 = (f32[32,4]{0,1:T(4,128)S(1)}, f32[32,4,5376]{2,0,1:T(8,128)S(1)}) fusion(bf16[5376,512,1]{1,0,2:T(8,128)(2,1)} %bitcast.53, pred[4,512]{1,0:T(4,128)(4,1)S(1)} %iota_compare_fusion.7, bf16[32,512]{1,0:T(8,128)(2,1)S(1)} %slice.60, pred[32,5376]{1,0:T(8,128)(4,1)S(1)} %fusion.12), kind=kOutput, calls=%fused_computation.164 | convolution fusion | flops 706772864 | bytes 8464896 | tf_op jit(solution)/shard_map/rhf,tf->rht/dot_general | solution.py:107
  54.8 0.5 fusion.2
  55.5 1.0 fusion.9
  56.6 0.5 convolution_convert_fusion.7
  57.1 1.3 collective-permute-start
  58.4 2.6 %collective-permute-start.1 = (bf16[32,2048]{1,0:T(8,128)(2,1)S(1)}, bf16[32,2048]{1,0:T(8,128)(2,1)S(1)}, u32[]{:S(2)}, u32[]{:S(2)}) collective-permute-start(bf16[32,2048]{1,0:T(8,128)(2,1)S(1)} %convolution_convert_fusion.7), channel_id=1, source_target_pairs={{0,2},{1,3},{2,0},{3,1},{4,6},{5,7},{6,4},{7,5},{8,10},{9,11},{10,... | collective-permute-start | bytes 393224 | tf_op jit(solution)/shard_map/ppermute | solution.py:27
  61.0 1.1 collective-permute-start.2
  62.1 1.2 collective-permute-done
  63.3 3.9 %collective-permute-done.1 = bf16[32,2048]{1,0:T(8,128)(2,1)S(1)} collective-permute-done((bf16[32,2048]{1,0:T(8,128)(2,1)S(1)}, bf16[32,2048]{1,0:T(8,128)(2,1)S(1)}, u32[]{:S(2)}, u32[]{:S(2)}) %collective-permute-start.1) | collective-permute-done | bytes 131104 | tf_op jit(solution)/shard_map/ppermute | solution.py:27
  67.6 5.1 %convolution_convert_fusion.6 = bf16[32,2048]{1,0:T(8,128)(2,1)S(1)} fusion(bf16[1024,2048]{1,0:T(8,128)(2,1)} %param.19, bf16[2048,1024]{1,0:T(8,128)(2,1)} %param.18, f32[32,2048]{1,0:T(8,128)S(1)} %get-tuple-element.12, f32[2048]{0:T(1024)S(1)} %bitcast.66, f32[2048]{0:T(1024)S(1)} %bitcast.62, f32[32]{0:T(128)S(1)} %add_rsqrt_fusion.3, ...), kind=kOutput, calls=%fused_computation.18 | convolution fusion | flops 269123584 | bytes 8798464 | tf_op jit(solution)/shard_map/dot_general | solution.py:172
  72.7 0.9 collective-permute-start.3
  73.6 2.3 %collective-permute-start.4 = (bf16[32,2048]{1,0:T(8,128)(2,1)S(1)}, bf16[32,2048]{1,0:T(8,128)(2,1)S(1)}, u32[]{:S(2)}, u32[]{:S(2)}) collective-permute-start(bf16[32,2048]{1,0:T(8,128)(2,1)S(1)} %convolution_convert_fusion.6), channel_id=1, source_target_pairs={{0,2},{1,3},{2,0},{3,1},{4,6},{5,7},{6,4},{7,5},{8,10},{9,11},{10,... | collective-permute-start | bytes 393224 | tf_op jit(solution)/shard_map/ppermute | solution.py:27
  75.9 0.9 collective-permute-start.5
  76.9 0.9 collective-permute-done.3
  77.8 3.1 %collective-permute-done.4 = bf16[32,2048]{1,0:T(8,128)(2,1)S(1)} collective-permute-done((bf16[32,2048]{1,0:T(8,128)(2,1)S(1)}, bf16[32,2048]{1,0:T(8,128)(2,1)S(1)}, u32[]{:S(2)}, u32[]{:S(2)}) %collective-permute-start.4) | collective-permute-done | bytes 131104 | tf_op jit(solution)/shard_map/ppermute | solution.py:27
  81.5 4.9 %convolution_convert_fusion.2 = bf16[32,1536]{1,0:T(8,128)(2,1)S(1)} fusion(bf16[2048,1536]{0,1:T(8,128)(2,1)} %bitcast.51, f32[32,2048]{1,0:T(8,128)S(1)} %get-tuple-element.10, f32[2048]{0:T(1024)S(1)} %bitcast.73, f32[2048]{0:T(1024)S(1)} %bitcast.70, f32[32]{0:T(128)S(1)} %add_rsqrt_fusion.2, f32[32]{0:T(128)S(1)} %broadcast_multiply_fusion.2), kind=kOutput, calls=%fused_computation.13 | convolution fusion | flops 201703424 | bytes 6668544 | tf_op jit(solution)/shard_map/dot_general | solution.py:148
  86.5 4.7 %fusion.92 = (f32[32,4]{0,1:T(4,128)S(1)}, f32[32,4,5376]{2,0,1:T(8,128)S(1)}) fusion(bf16[5376,512,1]{1,0,2:T(8,128)(2,1)} %bitcast.52, pred[4,512]{1,0:T(4,128)(4,1)S(1)} %iota_compare_fusion.7, bf16[32,512]{1,0:T(8,128)(2,1)S(1)} %slice.63, pred[32,5376]{1,0:T(8,128)(4,1)S(1)} %fusion.12), kind=kOutput, calls=%fused_computation.165 | convolution fusion | flops 706772864 | bytes 8464896 | tf_op jit(solution)/shard_map/rhf,tf->rht/dot_general | solution.py:107
  91.2 0.5 fusion.3
  91.9 1.0 fusion.10
  92.9 0.5 convolution_convert_fusion.5
  93.4 2.5 %collective-permute-start.6 = (bf16[32,2048]{1,0:T(8,128)(2,1)S(1)}, bf16[32,2048]{1,0:T(8,128)(2,1)S(1)}, u32[]{:S(2)}, u32[]{:S(2)}) collective-permute-start(bf16[32,2048]{1,0:T(8,128)(2,1)S(1)} %convolution_convert_fusion.5), channel_id=1, source_target_pairs={{0,1},{1,2},{2,3},{3,0},{4,5},{5,6},{6,7},{7,4},{8,9},{9,10},{10,1... | collective-permute-start | bytes 393224 | tf_op jit(solution)/shard_map/ppermute | solution.py:27
  95.9 1.7 %collective-permute-start.7 = (bf16[32,2048]{1,0:T(8,128)(2,1)S(1)}, bf16[32,2048]{1,0:T(8,128)(2,1)S(1)}, u32[]{:S(2)}, u32[]{:S(2)}) collective-permute-start(bf16[32,2048]{1,0:T(8,128)(2,1)S(1)} %convolution_convert_fusion.5), channel_id=1, source_target_pairs={{0,2},{1,3},{2,0},{3,1},{4,6},{5,7},{6,4},{7,5},{8,10},{9,11},{10,... | collective-permute-start | bytes 393224 | tf_op jit(solution)/shard_map/ppermute | solution.py:27
  97.6 0.8 collective-permute-start.8
  98.4 0.4 collective-permute-done.6
  98.8 3.1 %collective-permute-done.7 = bf16[32,2048]{1,0:T(8,128)(2,1)S(1)} collective-permute-done((bf16[32,2048]{1,0:T(8,128)(2,1)S(1)}, bf16[32,2048]{1,0:T(8,128)(2,1)S(1)}, u32[]{:S(2)}, u32[]{:S(2)}) %collective-permute-start.7) | collective-permute-done | bytes 131104 | tf_op jit(solution)/shard_map/ppermute | solution.py:27
  101.9 0.6 collective-permute-done.8
  103.0 5.1 %convolution_convert_fusion.4 = bf16[32,2048]{1,0:T(8,128)(2,1)S(1)} fusion(bf16[1024,2048]{1,0:T(8,128)(2,1)} %param.19, bf16[2048,1024]{1,0:T(8,128)(2,1)} %param.18, f32[32,2048]{1,0:T(8,128)S(1)} %get-tuple-element.8, f32[32]{0:T(128)S(1)} %add_rsqrt_fusion.1, f32[32]{0:T(128)S(1)} %broadcast_multiply_fusion.1, f32[2048]{0:T(1024)S(1)} %bitcast.68, ...), kind=kOutput, calls=%fused_computation.16 | convolution fusion | flops 269123584 | bytes 8798464 | tf_op jit(solution)/shard_map/dot_general | solution.py:172
  108.1 2.2 %collective-permute-start.10 = (bf16[32,2048]{1,0:T(8,128)(2,1)S(1)}, bf16[32,2048]{1,0:T(8,128)(2,1)S(1)}, u32[]{:S(2)}, u32[]{:S(2)}) collective-permute-start(bf16[32,2048]{1,0:T(8,128)(2,1)S(1)} %convolution_convert_fusion.4), channel_id=1, source_target_pairs={{0,2},{1,3},{2,0},{3,1},{4,6},{5,7},{6,4},{7,5},{8,10},{9,11},{10,... | collective-permute-start | bytes 393224 | tf_op jit(solution)/shard_map/ppermute | solution.py:27
  110.3 0.6 collective-permute-start.11
  110.9 0.9 collective-permute-start.9
  111.8 1.7 %collective-permute-done.10 = bf16[32,2048]{1,0:T(8,128)(2,1)S(1)} collective-permute-done((bf16[32,2048]{1,0:T(8,128)(2,1)S(1)}, bf16[32,2048]{1,0:T(8,128)(2,1)S(1)}, u32[]{:S(2)}, u32[]{:S(2)}) %collective-permute-start.10) | collective-permute-done | bytes 131104 | tf_op jit(solution)/shard_map/ppermute | solution.py:27
  113.5 0.6 collective-permute-done.11
  114.1 3.2 %collective-permute-done.9 = bf16[32,2048]{1,0:T(8,128)(2,1)S(1)} collective-permute-done((bf16[32,2048]{1,0:T(8,128)(2,1)S(1)}, bf16[32,2048]{1,0:T(8,128)(2,1)S(1)}, u32[]{:S(2)}, u32[]{:S(2)}) %collective-permute-start.9) | collective-permute-done | bytes 131104 | tf_op jit(solution)/shard_map/ppermute | solution.py:27
  118.1 0.9 reshape.237
  119.0 10.2 %all-to-all-start.1 = ((bf16[32,2,2048]{2,1,0:T(2,128)(2,1)}), bf16[32,2,2048]{2,1,0:T(2,128)(2,1)S(1)}, u32[]{:S(2)}, u32[]{:S(2)}) async-start(bf16[32,2,2048]{2,1,0:T(2,128)(2,1)} %reshape.237), calls=%async_computation.1 | async-start | bytes 524288 | tf_op jit(solution)/shard_map/all_to_all | solution.py:55
  129.2 8.9 %all-to-all-done.1 = bf16[32,2,2048]{2,1,0:T(2,128)(2,1)S(1)} async-done(((bf16[32,2,2048]{2,1,0:T(2,128)(2,1)}), bf16[32,2,2048]{2,1,0:T(2,128)(2,1)S(1)}, u32[]{:S(2)}, u32[]{:S(2)}) %all-to-all-start.1) | async-done | bytes 262176 | tf_op jit(solution)/shard_map/all_to_all | solution.py:55
  138.2 0.9 fusion.4
  (74 shorter events, 5.0 us)
Async XLA Ops:
  0.0 56.6 %copy-start = (bf16[512,2048]{1,0:T(8,128)(2,1)S(1)}, bf16[512,2048]{1,0:T(8,128)(2,1)}, u32[]{:S(2)}) copy-start(bf16[512,2048]{1,0:T(8,128)(2,1)} %param.17) | copy-start | bytes 6291460
  3.5 41.2 %all-to-all-start = ((bf16[32,2,2048]{2,1,0:T(2,128)(2,1)}), bf16[32,2,2048]{2,1,0:T(2,128)(2,1)S(1)}, u32[]{:S(2)}, u32[]{:S(2)}) async-start(bf16[32,2,2048]{2,1,0:T(2,128)(2,1)} %reshape.234), calls=%async_computation | async-start | bytes 524288 | tf_op jit(solution)/shard_map/all_to_all | solution.py:55
  25.3 10.2 %copy-start.3 = (s32[32]{0:T(128)S(1)}, s32[32]{0:T(128)}, u32[]{:S(2)}) copy-start(s32[32]{0:T(128)} %param.15) | copy-start | bytes 388
  45.1 10.4 %slice-start.2 = ((s8[5505024]{0:T(1024)(128)(4,1)}), s8[4194304]{0:T(1024)(128)(4,1)S(1)}, s32[]{:S(2)}) async-start(s8[5505024]{0:T(1024)(128)(4,1)} %bitcast.57), calls=%async_computation.4 | async-start | bytes 8388608
  50.1 5.4 %slice-start.3 = ((s8[5505024]{0:T(1024)(128)(4,1)}), s8[1310720]{0:T(1024)(128)(4,1)S(1)}, s32[]{:S(2)}) async-start(s8[5505024]{0:T(1024)(128)(4,1)} %bitcast.57), calls=%async_computation.5 | async-start | bytes 2621440
  55.5 6.5 %copy-start.1 = (f32[2,2048]{1,0:T(2,128)S(1)}, f32[2,2048]{1,0:T(2,128)}, u32[]{:S(2)}) copy-start(f32[2,2048]{1,0:T(2,128)} %param.22) | copy-start | bytes 49156
  57.1 6.2 %collective-permute-start = (bf16[32,2048]{1,0:T(8,128)(2,1)S(1)}, bf16[32,2048]{1,0:T(8,128)(2,1)S(1)}, u32[]{:S(2)}, u32[]{:S(2)}) collective-permute-start(bf16[32,2048]{1,0:T(8,128)(2,1)S(1)} %convolution_convert_fusion.7), channel_id=1, source_target_pairs={{0,1},{1,2},{2,3},{3,0},{4,5},{5,6},{6,7},{7,4},{8,9},{9,10},{10,1... | collective-permute-start | bytes 393224 | tf_op jit(solution)/shard_map/ppermute | solution.py:27
  58.4 8.8 %collective-permute-start.1 = (bf16[32,2048]{1,0:T(8,128)(2,1)S(1)}, bf16[32,2048]{1,0:T(8,128)(2,1)S(1)}, u32[]{:S(2)}, u32[]{:S(2)}) collective-permute-start(bf16[32,2048]{1,0:T(8,128)(2,1)S(1)} %convolution_convert_fusion.7), channel_id=1, source_target_pairs={{0,2},{1,3},{2,0},{3,1},{4,6},{5,7},{6,4},{7,5},{8,10},{9,11},{10,... | collective-permute-start | bytes 393224 | tf_op jit(solution)/shard_map/ppermute | solution.py:27
  61.0 6.2 %collective-permute-start.2 = (bf16[32,2048]{1,0:T(8,128)(2,1)S(1)}, bf16[32,2048]{1,0:T(8,128)(2,1)S(1)}, u32[]{:S(2)}, u32[]{:S(2)}) collective-permute-start(bf16[32,2048]{1,0:T(8,128)(2,1)S(1)} %convolution_convert_fusion.7), channel_id=1, source_target_pairs={{0,3},{1,0},{2,1},{3,2},{4,7},{5,4},{6,5},{7,6},{8,11},{9,8},{10,9... | collective-permute-start | bytes 393224 | tf_op jit(solution)/shard_map/ppermute | solution.py:27
  67.6 9.2 %copy-start.2 = (f32[2,2048]{1,0:T(2,128)S(1)}, f32[2,2048]{1,0:T(2,128)}, u32[]{:S(2)}) copy-start(f32[2,2048]{1,0:T(2,128)} %param.23) | copy-start | bytes 49156
  72.7 5.1 %collective-permute-start.3 = (bf16[32,2048]{1,0:T(8,128)(2,1)S(1)}, bf16[32,2048]{1,0:T(8,128)(2,1)S(1)}, u32[]{:S(2)}, u32[]{:S(2)}) collective-permute-start(bf16[32,2048]{1,0:T(8,128)(2,1)S(1)} %convolution_convert_fusion.6), channel_id=1, source_target_pairs={{0,1},{1,2},{2,3},{3,0},{4,5},{5,6},{6,7},{7,4},{8,9},{9,10},{10,1... | collective-permute-start | bytes 393224 | tf_op jit(solution)/shard_map/ppermute | solution.py:27
  73.6 7.4 %collective-permute-start.4 = (bf16[32,2048]{1,0:T(8,128)(2,1)S(1)}, bf16[32,2048]{1,0:T(8,128)(2,1)S(1)}, u32[]{:S(2)}, u32[]{:S(2)}) collective-permute-start(bf16[32,2048]{1,0:T(8,128)(2,1)S(1)} %convolution_convert_fusion.6), channel_id=1, source_target_pairs={{0,2},{1,3},{2,0},{3,1},{4,6},{5,7},{6,4},{7,5},{8,10},{9,11},{10,... | collective-permute-start | bytes 393224 | tf_op jit(solution)/shard_map/ppermute | solution.py:27
  75.9 5.1 %collective-permute-start.5 = (bf16[32,2048]{1,0:T(8,128)(2,1)S(1)}, bf16[32,2048]{1,0:T(8,128)(2,1)S(1)}, u32[]{:S(2)}, u32[]{:S(2)}) collective-permute-start(bf16[32,2048]{1,0:T(8,128)(2,1)S(1)} %convolution_convert_fusion.6), channel_id=1, source_target_pairs={{0,3},{1,0},{2,1},{3,2},{4,7},{5,4},{6,5},{7,6},{8,11},{9,8},{10,9... | collective-permute-start | bytes 393224 | tf_op jit(solution)/shard_map/ppermute | solution.py:27
  81.4 10.4 %slice-start = ((s8[5505024]{0:T(1024)(128)(4,1)}), s8[4194304]{0:T(1024)(128)(4,1)S(1)}, s32[]{:S(2)}) async-start(s8[5505024]{0:T(1024)(128)(4,1)} %bitcast.54), calls=%async_computation.2 | async-start | bytes 8388608
  86.5 5.4 %slice-start.1 = ((s8[5505024]{0:T(1024)(128)(4,1)}), s8[1310720]{0:T(1024)(128)(4,1)S(1)}, s32[]{:S(2)}) async-start(s8[5505024]{0:T(1024)(128)(4,1)} %bitcast.54), calls=%async_computation.3 | async-start | bytes 2621440
  93.4 5.4 %collective-permute-start.6 = (bf16[32,2048]{1,0:T(8,128)(2,1)S(1)}, bf16[32,2048]{1,0:T(8,128)(2,1)S(1)}, u32[]{:S(2)}, u32[]{:S(2)}) collective-permute-start(bf16[32,2048]{1,0:T(8,128)(2,1)S(1)} %convolution_convert_fusion.5), channel_id=1, source_target_pairs={{0,1},{1,2},{2,3},{3,0},{4,5},{5,6},{6,7},{7,4},{8,9},{9,10},{10,1... | collective-permute-start | bytes 393224 | tf_op jit(solution)/shard_map/ppermute | solution.py:27
  95.9 6.0 %collective-permute-start.7 = (bf16[32,2048]{1,0:T(8,128)(2,1)S(1)}, bf16[32,2048]{1,0:T(8,128)(2,1)S(1)}, u32[]{:S(2)}, u32[]{:S(2)}) collective-permute-start(bf16[32,2048]{1,0:T(8,128)(2,1)S(1)} %convolution_convert_fusion.5), channel_id=1, source_target_pairs={{0,2},{1,3},{2,0},{3,1},{4,6},{5,7},{6,4},{7,5},{8,10},{9,11},{10,... | collective-permute-start | bytes 393224 | tf_op jit(solution)/shard_map/ppermute | solution.py:27
  97.6 4.9 %collective-permute-start.8 = (bf16[32,2048]{1,0:T(8,128)(2,1)S(1)}, bf16[32,2048]{1,0:T(8,128)(2,1)S(1)}, u32[]{:S(2)}, u32[]{:S(2)}) collective-permute-start(bf16[32,2048]{1,0:T(8,128)(2,1)S(1)} %convolution_convert_fusion.5), channel_id=1, source_target_pairs={{0,3},{1,0},{2,1},{3,2},{4,7},{5,4},{6,5},{7,6},{8,11},{9,8},{10,9... | collective-permute-start | bytes 393224 | tf_op jit(solution)/shard_map/ppermute | solution.py:27
  108.1 5.4 %collective-permute-start.10 = (bf16[32,2048]{1,0:T(8,128)(2,1)S(1)}, bf16[32,2048]{1,0:T(8,128)(2,1)S(1)}, u32[]{:S(2)}, u32[]{:S(2)}) collective-permute-start(bf16[32,2048]{1,0:T(8,128)(2,1)S(1)} %convolution_convert_fusion.4), channel_id=1, source_target_pairs={{0,2},{1,3},{2,0},{3,1},{4,6},{5,7},{6,4},{7,5},{8,10},{9,11},{10,... | collective-permute-start | bytes 393224 | tf_op jit(solution)/shard_map/ppermute | solution.py:27
  110.3 3.8 %collective-permute-start.11 = (bf16[32,2048]{1,0:T(8,128)(2,1)S(1)}, bf16[32,2048]{1,0:T(8,128)(2,1)S(1)}, u32[]{:S(2)}, u32[]{:S(2)}) collective-permute-start(bf16[32,2048]{1,0:T(8,128)(2,1)S(1)} %convolution_convert_fusion.4), channel_id=1, source_target_pairs={{0,3},{1,0},{2,1},{3,2},{4,7},{5,4},{6,5},{7,6},{8,11},{9,8},{10,9... | collective-permute-start | bytes 393224 | tf_op jit(solution)/shard_map/ppermute | solution.py:27
  110.9 6.4 %collective-permute-start.9 = (bf16[32,2048]{1,0:T(8,128)(2,1)S(1)}, bf16[32,2048]{1,0:T(8,128)(2,1)S(1)}, u32[]{:S(2)}, u32[]{:S(2)}) collective-permute-start(bf16[32,2048]{1,0:T(8,128)(2,1)S(1)} %convolution_convert_fusion.4), channel_id=1, source_target_pairs={{0,1},{1,2},{2,3},{3,0},{4,5},{5,6},{6,7},{7,4},{8,9},{9,10},{10,1... | collective-permute-start | bytes 393224 | tf_op jit(solution)/shard_map/ppermute | solution.py:27
  119.0 19.2 %all-to-all-start.1 = ((bf16[32,2,2048]{2,1,0:T(2,128)(2,1)}), bf16[32,2,2048]{2,1,0:T(2,128)(2,1)S(1)}, u32[]{:S(2)}, u32[]{:S(2)}) async-start(bf16[32,2,2048]{2,1,0:T(2,128)(2,1)} %reshape.237), calls=%async_computation.1 | async-start | bytes 524288 | tf_op jit(solution)/shard_map/all_to_all | solution.py:55

commit v2 on v0

v2 whole, which is shorter than its diff:
```python
import math

import jax
import jax.numpy as jnp
from jax import lax
from jax.experimental import pallas as pl
from jax.experimental.pallas import tpu as pltpu
from jax.sharding import PartitionSpec as P

HD = 128
CAP = 2
EPS = 1e-6
BF = jnp.bfloat16
F32 = jnp.float32
MIB = 1 << 20
VMEM_SPEC = pl.BlockSpec(memory_space=pltpu.VMEM)
ANY_SPEC = pl.BlockSpec(memory_space=pl.ANY)


def kernel_call(body, out_shape, scratch, limit_mib, *operands):
    return pl.pallas_call(
        body,
        out_shape=out_shape,
        in_specs=[VMEM_SPEC] * len(operands),
        out_specs=jax.tree.map(lambda _: VMEM_SPEC, out_shape),
        scratch_shapes=scratch,
        compiler_params=pltpu.CompilerParams(vmem_limit_bytes=limit_mib * MIB),
    )(*operands)


def on_chip(array):
    return pltpu.with_memory_space_constraint(array, pltpu.VMEM)


def add_norm(parts, residual, gain_bias):
    total = residual.astype(F32)
    for part in parts:
        total = total + part.astype(F32)
    width = total.shape[-1]
    row_mean = jnp.sum(total, axis=-1, keepdims=True) * (1.0 / width)
    centered = total - row_mean
    row_var = jnp.sum(centered * centered, axis=-1, keepdims=True) * (1.0 / width)
    return (centered * lax.rsqrt(row_var + EPS) * gain_bias[0:1, :] + gain_bias[1:2, :]).astype(BF)


def attend(x, wait, w_qkv, k_ref, v_ref, w_out, bias, s_ref, p_ref):
    rows = x.shape[0]
    share = w_qkv.shape[2]
    heads = share // HD
    pages, page_len = k_ref.shape[:2]
    step = k_step(pages)
    span = step * page_len
    scale = 1.0 / math.sqrt(HD)
    projected = []
    for i in range(3):
        wait("qkv", i)
        projected.append(jnp.dot(x, w_qkv[i], preferred_element_type=F32).astype(BF))
    query, fresh_key, fresh_value = projected
    lane_head = lax.broadcasted_iota(jnp.int32, (rows, share), 1) // HD
    wide = jnp.concatenate(
        [jnp.where(lane_head == h, query.astype(F32), 0.0) for h in range(heads)], axis=0
    )
    own_key = jnp.concatenate([fresh_key.astype(F32)] * heads, axis=0)
    own = jnp.sum(wide * own_key, axis=-1, keepdims=True)
    wide = wide.astype(BF)
    peak = jnp.full((heads * rows, HD), -jnp.inf, F32)
    for c in range(pages // step):
        wait("key", c)
        keys = k_ref[c * step : (c + 1) * step].reshape(span, share)
        scores = lax.dot_general(wide, keys, (((1,), (1,)), ((), ())), preferred_element_type=F32)
        here = bias[:, c * span : (c + 1) * span]
        scores = scores + jnp.concatenate([here] * heads, axis=0)
        s_ref[:, c * span : (c + 1) * span] = scores
        for i in range(span // HD):
            peak = jnp.maximum(peak, scores[:, i * HD : (i + 1) * HD])
    peak = jnp.maximum(jnp.max(peak, axis=-1, keepdims=True), own)
    sums = jnp.zeros((heads * rows, HD), F32)
    for c in range(pages // step):
        weight = jnp.exp((s_ref[:, c * span : (c + 1) * span] - peak) * scale)
        p_ref[:, c * span : (c + 1) * span] = weight.astype(BF)
        for i in range(span // HD):
            sums = sums + weight[:, i * HD : (i + 1) * HD]
    own_weight = jnp.exp((own - peak) * scale)
    total = jnp.sum(sums, axis=-1, keepdims=True) + own_weight
    wait("value", 0)
    values = v_ref[...].reshape(pages * page_len, share)
    mixed = jnp.dot(p_ref[...], values, preferred_element_type=F32)
    fresh_value = fresh_value.astype(F32)
    own_weight = own_weight.astype(BF).astype(F32)
    attended = []
    for h in range(heads):
        r = slice(h * rows, (h + 1) * rows)
        f = slice(h * HD, (h + 1) * HD)
        attended.append((mixed[r, f] + own_weight[r] * fresh_value[:, f]) / total[r])
    attended = jnp.concatenate(attended, axis=1).astype(BF)
    wait("out", 0)
    return jnp.dot(attended, w_out[...], preferred_element_type=F32).astype(BF)


def k_step(pages):
    return math.gcd(pages, 6)


def cache_copies(k_hbm, v_hbm, layer, k_ref, v_ref, sems):
    pages = k_ref.shape[0]
    step = k_step(pages)
    copies = {}
    for c in range(pages // step):
        part = pl.ds(c * step, step)
        copies["key", c] = pltpu.make_async_copy(k_hbm.at[layer, part], k_ref.at[part], sems.at[c])
    copies["value", 0] = pltpu.make_async_copy(v_hbm.at[layer], v_ref, sems.at[pages // step])
    return copies


def attention_scratch(rows, key_cache):
    pages, page_len, share = key_cache.shape[1:]
    wide = (rows * share // HD, pages * page_len)
    pool = (pages, page_len, share)
    return [
        pltpu.VMEM(wide, F32),
        pltpu.VMEM(wide, BF),
        pltpu.VMEM(pool, BF),
        pltpu.VMEM(pool, BF),
        pltpu.SemaphoreType.DMA((pages // k_step(pages) + 1,)),
    ]


def first_attention(incoming, take, w_qkv, w_out, key_cache, value_cache, bias):
    rows = bias.shape[0]
    lines, share = incoming.shape
    cols = take.shape[0] // rows

    def body(in_ref, take_ref, b_ref, wq_hbm, wo_hbm, k_hbm, v_hbm, x_ref, out_ref, wq_ref, wo_ref,
             s_ref, p_ref, k_ref, v_ref, sems, w_sems):
        copies = {
            ("qkv", i): pltpu.make_async_copy(wq_hbm.at[i], wq_ref.at[i], w_sems.at[i]) for i in range(3)
        }
        copies.update(cache_copies(k_hbm, v_hbm, 0, k_ref, v_ref, sems))
        copies["out", 0] = pltpu.make_async_copy(wo_hbm, wo_ref, w_sems.at[3])
        for copy in copies.values():
            copy.start()
        stacked = jnp.dot(take_ref[...], in_ref[...], preferred_element_type=F32).astype(BF)
        x = jnp.concatenate([stacked[c * rows : (c + 1) * rows] for c in range(cols)], axis=1)
        x_ref[...] = x
        out_ref[...] = attend(
            x, lambda *key: copies[key].wait(), wq_ref, k_ref, v_ref, wo_ref, b_ref, s_ref, p_ref
        )

    shape = jax.ShapeDtypeStruct((rows, share * cols), BF)
    return pl.pallas_call(
        body,
        out_shape=(shape, shape, pltpu.VMEM(w_qkv.shape, BF), pltpu.VMEM(w_out.shape, BF)),
        in_specs=[VMEM_SPEC] * 3 + [ANY_SPEC] * 4,
        out_specs=(VMEM_SPEC,) * 4,
        scratch_shapes=attention_scratch(rows, key_cache) + [pltpu.SemaphoreType.DMA((4,))],
        compiler_params=pltpu.CompilerParams(vmem_limit_bytes=20 * MIB),
    )(incoming, take, bias, w_qkv, w_out, key_cache, value_cache)


def norm_attention(parts, residual, gain_bias, w_qkv, w_out, key_cache, value_cache, bias, layer):
    count = len(parts)

    def body(*refs):
        part_refs, (res_ref, norm_ref, wq_ref, wo_ref, b_ref, k_hbm, v_hbm) = refs[:count], refs[count : count + 7]
        x_ref, out_ref, s_ref, p_ref, k_ref, v_ref, sems = refs[count + 7 :]
        copies = cache_copies(k_hbm, v_hbm, layer, k_ref, v_ref, sems)
        for copy in copies.values():
            copy.start()
        x = add_norm([r[...] for r in part_refs], res_ref[...], norm_ref[...])
        x_ref[...] = x

        def wait(*key):
            if key in copies:
                copies[key].wait()

        out_ref[...] = attend(x, wait, wq_ref, k_ref, v_ref, wo_ref, b_ref, s_ref, p_ref)

    shape = jax.ShapeDtypeStruct(residual.shape, BF)
    return pl.pallas_call(
        body,
        out_shape=(shape, shape),
        in_specs=[VMEM_SPEC] * (count + 5) + [ANY_SPEC] * 2,
        out_specs=(VMEM_SPEC, VMEM_SPEC),
        scratch_shapes=attention_scratch(residual.shape[0], key_cache),
        compiler_params=pltpu.CompilerParams(vmem_limit_bytes=20 * MIB),
    )(*parts, residual, gain_bias, w_qkv, w_out, bias, key_cache, value_cache)


def norm_mlp(parts, residual, gain_bias, w_up, w_down):
    count = len(parts)

    def body(*refs):
        part_refs, (res_ref, norm_ref, up_ref, down_ref) = refs[:count], refs[count : count + 4]
        x_ref, out_ref = refs[count + 4 :]
        x = add_norm([r[...] for r in part_refs], res_ref[...], norm_ref[...])
        x_ref[...] = x
        up = jnp.dot(x, up_ref[...], preferred_element_type=F32)
        active = jax.nn.gelu(up, approximate=True).astype(BF)
        out_ref[...] = jnp.dot(active, down_ref[...], preferred_element_type=F32).astype(BF)

    shape = jax.ShapeDtypeStruct(residual.shape, BF)
    return kernel_call(body, (shape, shape), [], 8, *parts, residual, gain_bias, w_up, w_down)


def norm_send(parts, residual, gain_bias, give):
    count = len(parts)
    cols = give.shape[1] // residual.shape[0]
    share = residual.shape[1] // cols

    def body(*refs):
        res_ref, norm_ref, give_ref, out_ref = refs[count:]
        x = add_norm([r[...] for r in refs[:count]], res_ref[...], norm_ref[...])
        out_ref[...] = lay_out(give_ref[...], x, cols)

    shape = jax.ShapeDtypeStruct((give.shape[0], share), BF)
    return kernel_call(body, shape, [], 8, *parts, residual, gain_bias, give)


def lay_out(give, rows_here, cols):
    share = rows_here.shape[1] // cols
    stacked = jnp.concatenate([rows_here[:, c * share : (c + 1) * share] for c in range(cols)], axis=0)
    return jnp.dot(give, stacked, preferred_element_type=F32).astype(BF)


def gather_parts(part):
    size = lax.axis_size("tp")
    return [part] + [
        lax.ppermute(part, "tp", [(i, (i + step) % size) for i in range(size)])
        for step in range(1, size)
    ]


def iota(shape, dim):
    return lax.broadcasted_iota(jnp.int32, shape, dim)


def deal_send(order, tokens, blocks, cols):
    rows, width = tokens.shape
    lines, stack = blocks * CAP * cols, cols * rows

    def body(order_ref, tok_ref, out_ref, give_ref):
        first = lax.axis_index("req") * rows
        wanted = first + iota((stack, order.shape[1]), 0) % rows
        goes = jnp.concatenate(
            [(order_ref[r : r + 1, :] == wanted).astype(F32).astype(BF) for r in range(order.shape[0])], axis=1
        )
        slots = order.shape[0] * order.shape[1]
        block_of = (iota((blocks, slots), 1) // rows == iota((blocks, slots), 0)).astype(F32).astype(BF)
        sent = lax.dot_general(block_of, goes, (((1,), (1,)), ((), ())), preferred_element_type=F32)
        a, b = iota((stack, stack), 0), iota((stack, stack), 1)
        earlier = ((a // rows == b // rows) & (a < b)).astype(F32).astype(BF)
        rank = jnp.dot(sent.astype(BF), earlier, preferred_element_type=F32)
        line, block = iota((lines, blocks), 0), iota((lines, blocks), 1)
        give = jnp.zeros((lines, stack), F32)
        for k in range(CAP):
            spread = (line // cols == block * CAP + k).astype(F32).astype(BF)
            chosen = jnp.where(rank == k, sent, 0.0).astype(BF)
            give = give + jnp.dot(spread, chosen, preferred_element_type=F32)
        same = iota((lines, stack), 0) % cols == iota((lines, stack), 1) // rows
        give = jnp.where(same, give, 0.0)
        give_ref[...] = give
        out_ref[...] = lay_out(give.astype(BF), tok_ref[...], cols)

    out = (jax.ShapeDtypeStruct((lines, width // cols), BF), jax.ShapeDtypeStruct((lines, stack), F32))
    return kernel_call(body, out, [], 8, order, tokens)


def deal_take(order, give, table, lengths, cols, pages, page_len):
    rows = lengths.shape[1]
    lines, stack = give.shape

    def body(order_ref, give_ref, table_ref, len_ref, take_ref, back_ref, send_ref, bias_ref):
        req = lax.axis_index("req")
        slot = req * rows + iota((stack, order.shape[1]), 0) % rows
        mine = jnp.zeros((stack, order.shape[1]), F32)
        for r in range(order.shape[0]):
            here = iota((stack, order.shape[1]), 1) + r * order.shape[1]
            mine = mine + jnp.where(here == slot, order_ref[r : r + 1, :], 0).astype(F32)
        column = jnp.broadcast_to(jnp.sum(mine, axis=1, keepdims=True), (stack, stack))
        line_of = jnp.transpose(column).astype(jnp.int32)
        column = column.astype(jnp.int32)
        a, b = iota((stack, stack), 0), iota((stack, stack), 1)
        before = (b < rows) & (column // rows == line_of // rows) & (line_of < column)
        rank = jnp.sum(before.astype(F32), axis=1, keepdims=True).astype(jnp.int32)
        place = (column[:, 0:1] // rows * CAP + rank) * cols + iota((stack, 1), 0) // rows
        take = (iota((stack, lines), 1) == place).astype(F32)
        take_ref[...] = take.astype(BF)
        send_ref[...] = jnp.transpose(take).astype(BF)
        back_ref[...] = jnp.transpose(give_ref[...]).astype(BF)
        diagonal = iota((rows, rows), 0) == iota((rows, rows), 1)

        def stand(line):
            return jnp.sum(jnp.where(diagonal, line, 0).astype(F32), axis=1, keepdims=True).astype(jnp.int32)

        length = stand(len_ref[...])
        page = iota((rows, page_len), 1) + req * pages
        room = jnp.zeros((rows, page_len), jnp.int32)
        for k in range(table.shape[0]):
            left = length - k * page_len
            hit = (stand(table_ref[k : k + 1, :]) == page) & (left > 0)
            room = room + jnp.where(hit, left, 0)
        offset = iota((rows, page_len), 1)
        for p in range(pages):
            bias_ref[:, p * page_len : (p + 1) * page_len] = jnp.where(
                offset < room[:, p : p + 1], 0.0, -jnp.inf
            ).astype(F32)

    out = (
        jax.ShapeDtypeStruct((stack, lines), BF),
        jax.ShapeDtypeStruct((stack, lines), BF),
        jax.ShapeDtypeStruct((lines, stack), BF),
        jax.ShapeDtypeStruct((rows, pages * page_len), F32),
    )
    return kernel_call(body, out, [], 8, order, give, table, lengths)


def settle(incoming, back, rows):
    cols = back.shape[0] // rows

    def body(in_ref, back_ref, out_ref):
        stacked = jnp.dot(back_ref[...], in_ref[...], preferred_element_type=F32).astype(BF)
        out_ref[...] = jnp.concatenate([stacked[c * rows : (c + 1) * rows] for c in range(cols)], axis=1)

    shape = jax.ShapeDtypeStruct((rows, incoming.shape[1] * cols), BF)
    return kernel_call(body, shape, [], 8, incoming, back)


def swap(lines_out, blocks):
    lines, share = lines_out.shape
    return lax.all_to_all(lines_out.reshape(blocks, lines // blocks, share), "req", 0, 0).reshape(lines, share)


def local(
    tokens,
    deal_order,
    page_table,
    lengths,
    qkv_weight,
    out_weight,
    up_weight,
    down_weight,
    key_cache,
    value_cache,
    attn_norm,
    mlp_norm,
):
    req_rows = tokens.shape[0]
    blocks = lax.axis_size("req")
    cols = lax.axis_size("tp")
    layers, pool_pages, page_len = key_cache.shape[:3]
    order = deal_order.reshape(-1, HD)
    outgoing, give = deal_send(order, tokens, blocks, cols)
    incoming = swap(outgoing, blocks)
    take, back, send, bias = deal_take(
        order, give, page_table.T, lengths.reshape(1, -1), cols, pool_pages, page_len
    )
    w_qkv = jnp.transpose(qkv_weight, (1, 0, 2))
    w_up = on_chip(up_weight)
    w_down = on_chip(down_weight)
    current, partial, w_qkv, w_out = first_attention(
        incoming, take, w_qkv, out_weight, key_cache, value_cache, bias
    )
    for layer in range(layers):
        hidden, partial = norm_mlp(gather_parts(partial), current, attn_norm, w_up, w_down)
        if layer + 1 < layers:
            current, partial = norm_attention(
                gather_parts(partial), hidden, mlp_norm, w_qkv, w_out, key_cache, value_cache, bias, layer + 1
            )
    leaving = norm_send(gather_parts(partial), hidden, mlp_norm, send)
    return settle(swap(leaving, blocks), back, req_rows)


def solution(mesh):
    in_specs = (
        P("req", None),
        P(),
        P("req", None),
        P("req"),
        P(None, None, "tp"),
        P("tp", None),
        P(None, "tp"),
        P("tp", None),
        P(None, "req", None, "tp"),
        P(None, "req", None, "tp"),
        P(),
        P(),
    )
    out_specs = P("req", None)
    return jax.shard_map(local, mesh=mesh, in_specs=in_specs, out_specs=out_specs, check_vma=False)
```

time: 335 us -> 113 us (0.34)
  waiting for transfers between devices: 231 us -> 39.1 us
  matrix products: 32.2 us -> 0 us
  Pallas kernels: 0 us -> 22.1 us
  local copies, waits for them, and re-layouts: 40.3 us -> 20.6 us
  starting transfers between devices: 0.39 us -> 17.8 us
  other arithmetic: 16.7 us -> 0 us
  between operations: 13.9 us -> 0.1 us
  blocking collectives: 0 us -> 13.2 us
    psum x4 -> x0, waiting for transfers between devices: 163 us -> none  [post_norm(): lax.psum(partial_term.astype(jnp.bfloat16), 'tp').astype(jnp.float32)]
    all_gather x2 -> x0, waiting for transfers between devices: 67.6 us -> none  [the longest x1 45 us: local(): returned = lax.all_gather(current, 'req', axis=0, tiled=True)]
    ppermute x0 -> x12, waiting for transfers between devices: none -> 32.9 us  [gather_parts(): lax.ppermute(part, 'tp', [(i, (i + step) % size) for i in range(size)])]
    dot_general x10 -> x0, matrix products: 32.2 us -> none  [the longest x2 11.4 us: local(): jnp.dot(activated, down_weight, preferred_element_type=jnp.float32)]
    pallas_call x0 -> x8, Pallas kernels: none -> 22.1 us  [the longest x1 7.8 us: first_attention(): pl.pallas_call(body, out_shape=(shape, shape, pltpu.VMEM(w_qkv.shape, BF)...]
    slice x6 -> x0, local copies, waits for them, and re-layouts: 19.6 us -> none  [the longest x1 9.76 us: local(): key_pool = key_cache[layer_index]]
    all_to_all x0 -> x1, blocking collectives: none -> 13.2 us  [swap(): lax.all_to_all(lines_out.reshape(blocks, lines // blocks, share), 'req',...]
    unnamed x23 -> x32, local copies, waits for them, and re-layouts: 8.92 us -> 20.6 us
  transfers between devices with their start and end apart: 6 -> 13, of which waited for: 6 -> 13; matrix products, arithmetic and copies ran while one was open for 10% -> 0% of each run, Pallas kernels for 0% -> 1%
where the time goes in v2:
time: 113 us
  waiting for transfers between devices  39.1 us (35%)
  Pallas kernels  22.1 us (20%)
  local copies, waits for them, and re-layouts  20.6 us (18%)
  starting transfers between devices  17.8 us (16%)
  blocking collectives  13.2 us (12%)
    ppermute x12, waiting for transfers between devices, gather_parts(): lax.ppermute(part, 'tp', [(i, (i + step) % size) for i in range(size)])  32.9 us
    unnamed x32, local copies, waits for them, and re-layouts  20.6 us
    all_to_all x1, blocking collectives, swap(): lax.all_to_all(lines_out.reshape(blocks, lines // blocks, share), 'req',...  13.2 us
    all_to_all x1, starting transfers between devices, swap(): lax.all_to_all(lines_out.reshape(blocks, lines // blocks, share), 'req',...  9.43 us
    ppermute x12, starting transfers between devices, gather_parts(): lax.ppermute(part, 'tp', [(i, (i + step) % size) for i in range(size)])  8.34 us
    pallas_call x1, Pallas kernels, first_attention(): pl.pallas_call(body, out_shape=(shape, shape, pltpu.VMEM(w_qkv.shape, BF)...  7.8 us
    pallas_call x1, Pallas kernels, norm_attention(): pl.pallas_call(body, out_shape=(shape, shape), in_specs=[VMEM_SPEC] * (co...  7.31 us
    pallas_call x6, Pallas kernels, kernel_call(): pl.pallas_call(body, out_shape=out_shape, in_specs=[VMEM_SPEC] * len(oper...  7.03 us
  transfers between devices with their start and end apart: 13, of which 13 were waited for; matrix products, arithmetic and copies ran while one was open for 0% of the time, Pallas kernels for 1%

profile of v2, /device:TPU:1, one launch (start us, length us, event | category | flops | bytes accessed | tf_op | source)
XLA Modules:
  0.0 112.9 jit_solution(6421053248252045505)
XLA Ops:
  0.0 0.9 copy-done.9
  0.9 0.7 copy-done.12
  1.6 1.4 %shard_map.118 = (bf16[256,512]{1,0:T(8,128)(2,1)}, f32[256,128]{1,0:T(8,128)S(1)}) custom-call(s32[8,128]{1,0:T(8,128)S(1)} %bitcast.12, bf16[32,2048]{1,0:T(8,128)(2,1)S(1)} %copy-done.9), custom_call_target="tpu_custom_call" | custom-call | tf_op jit(solution)/shard_map/pallas_call | solution.py:21
  3.0 9.4 %all-to-all-start = ((bf16[32,8,512]{2,1,0:T(8,128)(2,1)}), bf16[32,8,512]{2,1,0:T(8,128)(2,1)S(1)}, u32[]{:S(2)}, u32[]{:S(2)}) async-start(bf16[32,8,512]{2,1,0:T(8,128)(2,1)} %bitcast.1), calls=%async_computation | async-start | bytes 524288 | tf_op jit(solution)/shard_map/all_to_all | solution.py:330
  12.4 0.0 copy-start.13
  12.4 0.7 copy-done.13
  13.1 0.7 copy-done.14
  13.8 0.7 copy-done.15
  14.5 0.7 shard_map.119
  15.2 6.2 %all-to-all-done = bf16[32,8,512]{2,1,0:T(8,128)(2,1)S(1)} async-done(((bf16[32,8,512]{2,1,0:T(8,128)(2,1)}), bf16[32,8,512]{2,1,0:T(8,128)(2,1)S(1)}, u32[]{:S(2)}, u32[]{:S(2)}) %all-to-all-start) | async-done | bytes 262176 | tf_op jit(solution)/shard_map/all_to_all | solution.py:330
  21.4 4.1 %copy-done = bf16[2,42,128,512]{3,2,1,0:T(8,128)(2,1)S(1)} copy-done((bf16[2,42,128,512]{3,2,1,0:T(8,128)(2,1)S(1)}, bf16[2,42,128,512]{3,2,1,0:T(8,128)(2,1)}, u32[]{:S(2)}) %copy-start) | copy-done | bytes 11010072
  25.5 2.8 %copy-done.7 = bf16[2048,3,512]{2,0,1:T(8,128)(2,1)S(1)} copy-done((bf16[2048,3,512]{2,0,1:T(8,128)(2,1)S(1)}, bf16[2048,3,512]{2,0,1:T(8,128)(2,1)}, u32[]{:S(2)}) %copy-start.7) | copy-done | bytes 6291480
  28.3 1.6 %copy-done.8 = bf16[512,2048]{1,0:T(8,128)(2,1)S(1)} copy-done((bf16[512,2048]{1,0:T(8,128)(2,1)S(1)}, bf16[512,2048]{1,0:T(8,128)(2,1)}, u32[]{:S(2)}) %copy-start.8) | copy-done | bytes 2097176
  29.9 7.8 %shard_map.120 = (bf16[32,2048]{1,0:T(8,128)(2,1)S(1)}, bf16[32,2048]{1,0:T(8,128)(2,1)S(1)}, bf16[3,2048,512]{2,1,0:T(8,128)(2,1)S(1)}, bf16[512,2048]{1,0:T(8,128)(2,1)S(1)}) custom-call(bf16[256,512]{1,0:T(8,128)(2,1)S(1)} %bitcast.9, bf16[128,256]{1,0:T(8,128)(2,1)S(1)} %get-tuple-element.23.take_ref, f32[32,5376]{1,0:T(8,128)S(1)} %get-tuple-element.24.b_ref.refs_8_, ...), custom_call_target="tpu_custom_call" | custom-call | tf_op jit(solution)/shard_map/pallas_call | solution.py:150
  37.7 2.8 %collective-permute-start.2 = (bf16[32,2048]{1,0:T(8,128)(2,1)S(1)}, bf16[32,2048]{1,0:T(8,128)(2,1)S(1)}, u32[]{:S(2)}, u32[]{:S(2)}) collective-permute-start(bf16[32,2048]{1,0:T(8,128)(2,1)S(1)} %get-tuple-element.25.refs_0_), channel_id=1, source_target_pairs={{0,3},{1,0},{2,1},{3,2},{4,7},{5,4},{6,5},{7,6},{8,11},{9,8},{10,9... | collective-permute-start | bytes 393224 | tf_op jit(solution)/shard_map/ppermute | solution.py:228
  40.5 0.3 collective-permute-start.1
  40.9 0.7 collective-permute-start
  41.6 4.3 %collective-permute-done.2.refs_3_ = bf16[32,2048]{1,0:T(8,128)(2,1)S(1)} collective-permute-done((bf16[32,2048]{1,0:T(8,128)(2,1)S(1)}, bf16[32,2048]{1,0:T(8,128)(2,1)S(1)}, u32[]{:S(2)}, u32[]{:S(2)}) %collective-permute-start.2) | collective-permute-done | bytes 131104 | tf_op jit(solution)/shard_map/ppermute | solution.py:228
  45.9 0.8 collective-permute-done.1.refs_2_
  46.7 3.6 %collective-permute-done.refs_1_ = bf16[32,2048]{1,0:T(8,128)(2,1)S(1)} collective-permute-done((bf16[32,2048]{1,0:T(8,128)(2,1)S(1)}, bf16[32,2048]{1,0:T(8,128)(2,1)S(1)}, u32[]{:S(2)}, u32[]{:S(2)}) %collective-permute-start) | collective-permute-done | bytes 131104 | tf_op jit(solution)/shard_map/ppermute | solution.py:228
  50.3 0.0 copy-done.10
  50.3 2.2 %copy-done.3 = bf16[2048,1024]{1,0:T(8,128)(2,1)S(1)} copy-done((bf16[2048,1024]{1,0:T(8,128)(2,1)S(1)}, bf16[2048,1024]{1,0:T(8,128)(2,1)}, u32[]{:S(2)}) %copy-start.3) | copy-done | bytes 4194328
  52.5 2.2 %copy-done.5 = bf16[1024,2048]{1,0:T(8,128)(2,1)S(1)} copy-done((bf16[1024,2048]{1,0:T(8,128)(2,1)S(1)}, bf16[1024,2048]{1,0:T(8,128)(2,1)}, u32[]{:S(2)}) %copy-start.5) | copy-done | bytes 4194328
  54.6 1.8 %shard_map.121 = (bf16[32,2048]{1,0:T(8,128)(2,1)S(1)}, bf16[32,2048]{1,0:T(8,128)(2,1)S(1)}) custom-call(bf16[32,2048]{1,0:T(8,128)(2,1)S(1)} %get-tuple-element.25.refs_0_, bf16[32,2048]{1,0:T(8,128)(2,1)S(1)} %collective-permute-done.refs_1_, bf16[32,2048]{1,0:T(8,128)(2,1)S(1)} %collective-permute-done.1.refs_2_, ...), custom_call_target="tpu_custom_call" | custom-call | tf_op jit(solution)/shard_map/pallas_call | solution.py:21
  56.4 0.0 collective-permute-start.5
  56.5 0.3 collective-permute-start.4
  56.8 1.1 %collective-permute-start.3 = (bf16[32,2048]{1,0:T(8,128)(2,1)S(1)}, bf16[32,2048]{1,0:T(8,128)(2,1)S(1)}, u32[]{:S(2)}, u32[]{:S(2)}) collective-permute-start(bf16[32,2048]{1,0:T(8,128)(2,1)S(1)} %get-tuple-element.27.refs_0_), channel_id=1, source_target_pairs={{0,1},{1,2},{2,3},{3,0},{4,5},{5,6},{6,7},{7,4},{8,9},{9,10},{10,1... | collective-permute-start | bytes 393224 | tf_op jit(solution)/shard_map/ppermute | solution.py:228
  57.9 3.1 %collective-permute-done.5.refs_3_ = bf16[32,2048]{1,0:T(8,128)(2,1)S(1)} collective-permute-done((bf16[32,2048]{1,0:T(8,128)(2,1)S(1)}, bf16[32,2048]{1,0:T(8,128)(2,1)S(1)}, u32[]{:S(2)}, u32[]{:S(2)}) %collective-permute-start.5) | collective-permute-done | bytes 131104 | tf_op jit(solution)/shard_map/ppermute | solution.py:228
  61.0 0.9 collective-permute-done.4.refs_2_
  61.9 4.3 %collective-permute-done.3.refs_1_ = bf16[32,2048]{1,0:T(8,128)(2,1)S(1)} collective-permute-done((bf16[32,2048]{1,0:T(8,128)(2,1)S(1)}, bf16[32,2048]{1,0:T(8,128)(2,1)S(1)}, u32[]{:S(2)}, u32[]{:S(2)}) %collective-permute-start.3) | collective-permute-done | bytes 131104 | tf_op jit(solution)/shard_map/ppermute | solution.py:228
  66.3 4.1 %copy-done.2 = bf16[2,42,128,512]{3,2,1,0:T(8,128)(2,1)S(1)} copy-done((bf16[2,42,128,512]{3,2,1,0:T(8,128)(2,1)S(1)}, bf16[2,42,128,512]{3,2,1,0:T(8,128)(2,1)}, u32[]{:S(2)}) %copy-start.2) | copy-done | bytes 11010072
  70.4 7.3 %shard_map.122 = (bf16[32,2048]{1,0:T(8,128)(2,1)S(1)}, bf16[32,2048]{1,0:T(8,128)(2,1)S(1)}) custom-call(bf16[32,2048]{1,0:T(8,128)(2,1)S(1)} %get-tuple-element.27.refs_0_, bf16[32,2048]{1,0:T(8,128)(2,1)S(1)} %collective-permute-done.3.refs_1_, bf16[32,2048]{1,0:T(8,128)(2,1)S(1)} %collective-permute-done.4.refs_2_, ...), custom_call_target="tpu_custom_call" | custom-call | tf_op jit(solution)/shard_map/pallas_call | solution.py:179
  77.7 0.1 collective-permute-start.8
  77.8 0.1 collective-permute-start.7
  77.9 1.4 %collective-permute-start.6 = (bf16[32,2048]{1,0:T(8,128)(2,1)S(1)}, bf16[32,2048]{1,0:T(8,128)(2,1)S(1)}, u32[]{:S(2)}, u32[]{:S(2)}) collective-permute-start(bf16[32,2048]{1,0:T(8,128)(2,1)S(1)} %get-tuple-element.31.refs_0_), channel_id=1, source_target_pairs={{0,1},{1,2},{2,3},{3,0},{4,5},{5,6},{6,7},{7,4},{8,9},{9,10},{10,1... | collective-permute-start | bytes 393224 | tf_op jit(solution)/shard_map/ppermute | solution.py:228
  79.2 3.1 %collective-permute-done.8.refs_3_ = bf16[32,2048]{1,0:T(8,128)(2,1)S(1)} collective-permute-done((bf16[32,2048]{1,0:T(8,128)(2,1)S(1)}, bf16[32,2048]{1,0:T(8,128)(2,1)S(1)}, u32[]{:S(2)}, u32[]{:S(2)}) %collective-permute-start.8) | collective-permute-done | bytes 131104 | tf_op jit(solution)/shard_map/ppermute | solution.py:228
  82.3 0.9 collective-permute-done.7.refs_2_
  83.3 3.8 %collective-permute-done.6.refs_1_ = bf16[32,2048]{1,0:T(8,128)(2,1)S(1)} collective-permute-done((bf16[32,2048]{1,0:T(8,128)(2,1)S(1)}, bf16[32,2048]{1,0:T(8,128)(2,1)S(1)}, u32[]{:S(2)}, u32[]{:S(2)}) %collective-permute-start.6) | collective-permute-done | bytes 131104 | tf_op jit(solution)/shard_map/ppermute | solution.py:228
  87.1 1.8 %shard_map.123 = (bf16[32,2048]{1,0:T(8,128)(2,1)S(1)}, bf16[32,2048]{1,0:T(8,128)(2,1)S(1)}) custom-call(bf16[32,2048]{1,0:T(8,128)(2,1)S(1)} %get-tuple-element.31.refs_0_, bf16[32,2048]{1,0:T(8,128)(2,1)S(1)} %collective-permute-done.6.refs_1_, bf16[32,2048]{1,0:T(8,128)(2,1)S(1)} %collective-permute-done.7.refs_2_, ...), custom_call_target="tpu_custom_call" | custom-call | tf_op jit(solution)/shard_map/pallas_call | solution.py:21
  88.9 0.5 collective-permute-start.11
  89.4 0.0 collective-permute-start.10
  89.4 1.0 collective-permute-start.9
  90.4 2.3 %collective-permute-done.11.refs_3_ = bf16[32,2048]{1,0:T(8,128)(2,1)S(1)} collective-permute-done((bf16[32,2048]{1,0:T(8,128)(2,1)S(1)}, bf16[32,2048]{1,0:T(8,128)(2,1)S(1)}, u32[]{:S(2)}, u32[]{:S(2)}) %collective-permute-start.11) | collective-permute-done | bytes 131104 | tf_op jit(solution)/shard_map/ppermute | solution.py:228
  92.7 2.1 %collective-permute-done.10.refs_2_ = bf16[32,2048]{1,0:T(8,128)(2,1)S(1)} collective-permute-done((bf16[32,2048]{1,0:T(8,128)(2,1)S(1)}, bf16[32,2048]{1,0:T(8,128)(2,1)S(1)}, u32[]{:S(2)}, u32[]{:S(2)}) %collective-permute-start.10) | collective-permute-done | bytes 131104 | tf_op jit(solution)/shard_map/ppermute | solution.py:228
  94.8 3.6 %collective-permute-done.9.refs_1_ = bf16[32,2048]{1,0:T(8,128)(2,1)S(1)} collective-permute-done((bf16[32,2048]{1,0:T(8,128)(2,1)S(1)}, bf16[32,2048]{1,0:T(8,128)(2,1)S(1)}, u32[]{:S(2)}, u32[]{:S(2)}) %collective-permute-start.9) | collective-permute-done | bytes 131104 | tf_op jit(solution)/shard_map/ppermute | solution.py:228
  98.4 0.5 shard_map.124
  98.9 13.2 %all_to_all.10 = bf16[32,8,512]{2,1,0:T(8,128)(2,1)S(1)} all-to-all(bf16[32,8,512]{2,1,0:T(8,128)(2,1)S(1)} %bitcast.11), channel_id=1, replica_groups=mesh['req'=32,'tp'=4] {'req'}, dimensions={0} | all-to-all | bytes 524288 | tf_op jit(solution)/shard_map/all_to_all | solution.py:330
  112.1 0.8 shard_map.125
  (19 shorter events, 0.0 us)
Async XLA Ops:
  0.0 0.9 copy-start.9
  0.9 0.7 copy-start.12
  3.0 18.4 %all-to-all-start = ((bf16[32,8,512]{2,1,0:T(8,128)(2,1)}), bf16[32,8,512]{2,1,0:T(8,128)(2,1)S(1)}, u32[]{:S(2)}, u32[]{:S(2)}) async-start(bf16[32,8,512]{2,1,0:T(8,128)(2,1)} %bitcast.1), calls=%async_computation | async-start | bytes 524288 | tf_op jit(solution)/shard_map/all_to_all | solution.py:330
  12.4 0.7 copy-start.13
  13.1 0.7 copy-start.14
  13.8 0.7 copy-start.15
  21.4 4.1 %copy-start = (bf16[2,42,128,512]{3,2,1,0:T(8,128)(2,1)S(1)}, bf16[2,42,128,512]{3,2,1,0:T(8,128)(2,1)}, u32[]{:S(2)}) copy-start(bf16[2,42,128,512]{3,2,1,0:T(8,128)(2,1)} %refs_9_.1) | copy-start | bytes 33030148
  25.5 2.8 %copy-start.7 = (bf16[2048,3,512]{2,0,1:T(8,128)(2,1)S(1)}, bf16[2048,3,512]{2,0,1:T(8,128)(2,1)}, u32[]{:S(2)}) copy-start(bf16[2048,3,512]{2,0,1:T(8,128)(2,1)} %param.16) | copy-start | bytes 18874372
  28.3 1.6 %copy-start.8 = (bf16[512,2048]{1,0:T(8,128)(2,1)S(1)}, bf16[512,2048]{1,0:T(8,128)(2,1)}, u32[]{:S(2)}) copy-start(bf16[512,2048]{1,0:T(8,128)(2,1)} %wo_hbm.1) | copy-start | bytes 6291460
  29.9 20.4 %copy-start.10 = (f32[2,2048]{1,0:T(2,128)S(1)}, f32[2,2048]{1,0:T(2,128)}, u32[]{:S(2)}) copy-start(f32[2,2048]{1,0:T(2,128)} %refs_5_.6) | copy-start | bytes 49156
  29.9 36.3 %copy-start.1 = (bf16[2,42,128,512]{3,2,1,0:T(8,128)(2,1)S(1)}, bf16[2,42,128,512]{3,2,1,0:T(8,128)(2,1)}, u32[]{:S(2)}) copy-start(bf16[2,42,128,512]{3,2,1,0:T(8,128)(2,1)} %refs_9_.1) | copy-start | bytes 33030148
  29.9 36.3 %copy-start.11 = (f32[2,2048]{1,0:T(2,128)S(1)}, f32[2,2048]{1,0:T(2,128)}, u32[]{:S(2)}) copy-start(f32[2,2048]{1,0:T(2,128)} %refs_5_.7) | copy-start | bytes 49156
  37.7 8.2 %collective-permute-start.2 = (bf16[32,2048]{1,0:T(8,128)(2,1)S(1)}, bf16[32,2048]{1,0:T(8,128)(2,1)S(1)}, u32[]{:S(2)}, u32[]{:S(2)}) collective-permute-start(bf16[32,2048]{1,0:T(8,128)(2,1)S(1)} %get-tuple-element.25.refs_0_), channel_id=1, source_target_pairs={{0,3},{1,0},{2,1},{3,2},{4,7},{5,4},{6,5},{7,6},{8,11},{9,8},{10,9... | collective-permute-start | bytes 393224 | tf_op jit(solution)/shard_map/ppermute | solution.py:228
  40.5 6.1 %collective-permute-start.1 = (bf16[32,2048]{1,0:T(8,128)(2,1)S(1)}, bf16[32,2048]{1,0:T(8,128)(2,1)S(1)}, u32[]{:S(2)}, u32[]{:S(2)}) collective-permute-start(bf16[32,2048]{1,0:T(8,128)(2,1)S(1)} %get-tuple-element.25.refs_0_), channel_id=1, source_target_pairs={{0,2},{1,3},{2,0},{3,1},{4,6},{5,7},{6,4},{7,5},{8,10},{9,11},{10,... | collective-permute-start | bytes 393224 | tf_op jit(solution)/shard_map/ppermute | solution.py:228
  40.9 9.4 %collective-permute-start = (bf16[32,2048]{1,0:T(8,128)(2,1)S(1)}, bf16[32,2048]{1,0:T(8,128)(2,1)S(1)}, u32[]{:S(2)}, u32[]{:S(2)}) collective-permute-start(bf16[32,2048]{1,0:T(8,128)(2,1)S(1)} %get-tuple-element.25.refs_0_), channel_id=1, source_target_pairs={{0,1},{1,2},{2,3},{3,0},{4,5},{5,6},{6,7},{7,4},{8,9},{9,10},{10,1... | collective-permute-start | bytes 393224 | tf_op jit(solution)/shard_map/ppermute | solution.py:228
  50.3 2.2 %copy-start.3 = (bf16[2048,1024]{1,0:T(8,128)(2,1)S(1)}, bf16[2048,1024]{1,0:T(8,128)(2,1)}, u32[]{:S(2)}) copy-start(bf16[2048,1024]{1,0:T(8,128)(2,1)} %refs_6_.3) | copy-start | bytes 12582916
  52.5 2.2 %copy-start.5 = (bf16[1024,2048]{1,0:T(8,128)(2,1)S(1)}, bf16[1024,2048]{1,0:T(8,128)(2,1)}, u32[]{:S(2)}) copy-start(bf16[1024,2048]{1,0:T(8,128)(2,1)} %refs_7_.3) | copy-start | bytes 12582916
  56.4 4.6 %collective-permute-start.5 = (bf16[32,2048]{1,0:T(8,128)(2,1)S(1)}, bf16[32,2048]{1,0:T(8,128)(2,1)S(1)}, u32[]{:S(2)}, u32[]{:S(2)}) collective-permute-start(bf16[32,2048]{1,0:T(8,128)(2,1)S(1)} %get-tuple-element.27.refs_0_), channel_id=1, source_target_pairs={{0,3},{1,0},{2,1},{3,2},{4,7},{5,4},{6,5},{7,6},{8,11},{9,8},{10,9... | collective-permute-start | bytes 393224 | tf_op jit(solution)/shard_map/ppermute | solution.py:228
  56.5 5.5 %collective-permute-start.4 = (bf16[32,2048]{1,0:T(8,128)(2,1)S(1)}, bf16[32,2048]{1,0:T(8,128)(2,1)S(1)}, u32[]{:S(2)}, u32[]{:S(2)}) collective-permute-start(bf16[32,2048]{1,0:T(8,128)(2,1)S(1)} %get-tuple-element.27.refs_0_), channel_id=1, source_target_pairs={{0,2},{1,3},{2,0},{3,1},{4,6},{5,7},{6,4},{7,5},{8,10},{9,11},{10,... | collective-permute-start | bytes 393224 | tf_op jit(solution)/shard_map/ppermute | solution.py:228
  56.8 9.5 %collective-permute-start.3 = (bf16[32,2048]{1,0:T(8,128)(2,1)S(1)}, bf16[32,2048]{1,0:T(8,128)(2,1)S(1)}, u32[]{:S(2)}, u32[]{:S(2)}) collective-permute-start(bf16[32,2048]{1,0:T(8,128)(2,1)S(1)} %get-tuple-element.27.refs_0_), channel_id=1, source_target_pairs={{0,1},{1,2},{2,3},{3,0},{4,5},{5,6},{6,7},{7,4},{8,9},{9,10},{10,1... | collective-permute-start | bytes 393224 | tf_op jit(solution)/shard_map/ppermute | solution.py:228
  66.3 4.1 %copy-start.2 = (bf16[2,42,128,512]{3,2,1,0:T(8,128)(2,1)S(1)}, bf16[2,42,128,512]{3,2,1,0:T(8,128)(2,1)}, u32[]{:S(2)}) copy-start(bf16[2,42,128,512]{3,2,1,0:T(8,128)(2,1)} %refs_10_.1) | copy-start | bytes 33030148
  70.4 16.7 %copy-start.4 = (bf16[2048,1024]{1,0:T(8,128)(2,1)S(1)}, bf16[2048,1024]{1,0:T(8,128)(2,1)}, u32[]{:S(2)}) copy-start(bf16[2048,1024]{1,0:T(8,128)(2,1)} %refs_6_.3) | copy-start | bytes 12582916
  70.4 16.7 %copy-start.6 = (bf16[1024,2048]{1,0:T(8,128)(2,1)S(1)}, bf16[1024,2048]{1,0:T(8,128)(2,1)}, u32[]{:S(2)}) copy-start(bf16[1024,2048]{1,0:T(8,128)(2,1)} %refs_7_.3) | copy-start | bytes 12582916
  77.7 4.6 %collective-permute-start.8 = (bf16[32,2048]{1,0:T(8,128)(2,1)S(1)}, bf16[32,2048]{1,0:T(8,128)(2,1)S(1)}, u32[]{:S(2)}, u32[]{:S(2)}) collective-permute-start(bf16[32,2048]{1,0:T(8,128)(2,1)S(1)} %get-tuple-element.31.refs_0_), channel_id=1, source_target_pairs={{0,3},{1,0},{2,1},{3,2},{4,7},{5,4},{6,5},{7,6},{8,11},{9,8},{10,9... | collective-permute-start | bytes 393224 | tf_op jit(solution)/shard_map/ppermute | solution.py:228
  77.8 5.5 %collective-permute-start.7 = (bf16[32,2048]{1,0:T(8,128)(2,1)S(1)}, bf16[32,2048]{1,0:T(8,128)(2,1)S(1)}, u32[]{:S(2)}, u32[]{:S(2)}) collective-permute-start(bf16[32,2048]{1,0:T(8,128)(2,1)S(1)} %get-tuple-element.31.refs_0_), channel_id=1, source_target_pairs={{0,2},{1,3},{2,0},{3,1},{4,6},{5,7},{6,4},{7,5},{8,10},{9,11},{10,... | collective-permute-start | bytes 393224 | tf_op jit(solution)/shard_map/ppermute | solution.py:228
  77.9 9.2 %collective-permute-start.6 = (bf16[32,2048]{1,0:T(8,128)(2,1)S(1)}, bf16[32,2048]{1,0:T(8,128)(2,1)S(1)}, u32[]{:S(2)}, u32[]{:S(2)}) collective-permute-start(bf16[32,2048]{1,0:T(8,128)(2,1)S(1)} %get-tuple-element.31.refs_0_), channel_id=1, source_target_pairs={{0,1},{1,2},{2,3},{3,0},{4,5},{5,6},{6,7},{7,4},{8,9},{9,10},{10,1... | collective-permute-start | bytes 393224 | tf_op jit(solution)/shard_map/ppermute | solution.py:228
  88.9 3.8 %collective-permute-start.11 = (bf16[32,2048]{1,0:T(8,128)(2,1)S(1)}, bf16[32,2048]{1,0:T(8,128)(2,1)S(1)}, u32[]{:S(2)}, u32[]{:S(2)}) collective-permute-start(bf16[32,2048]{1,0:T(8,128)(2,1)S(1)} %get-tuple-element.33.refs_0_), channel_id=1, source_target_pairs={{0,3},{1,0},{2,1},{3,2},{4,7},{5,4},{6,5},{7,6},{8,11},{9,8},{10,9... | collective-permute-start | bytes 393224 | tf_op jit(solution)/shard_map/ppermute | solution.py:228
  89.4 5.4 %collective-permute-start.10 = (bf16[32,2048]{1,0:T(8,128)(2,1)S(1)}, bf16[32,2048]{1,0:T(8,128)(2,1)S(1)}, u32[]{:S(2)}, u32[]{:S(2)}) collective-permute-start(bf16[32,2048]{1,0:T(8,128)(2,1)S(1)} %get-tuple-element.33.refs_0_), channel_id=1, source_target_pairs={{0,2},{1,3},{2,0},{3,1},{4,6},{5,7},{6,4},{7,5},{8,10},{9,11},{10,... | collective-permute-start | bytes 393224 | tf_op jit(solution)/shard_map/ppermute | solution.py:228
  89.4 9.0 %collective-permute-start.9 = (bf16[32,2048]{1,0:T(8,128)(2,1)S(1)}, bf16[32,2048]{1,0:T(8,128)(2,1)S(1)}, u32[]{:S(2)}, u32[]{:S(2)}) collective-permute-start(bf16[32,2048]{1,0:T(8,128)(2,1)S(1)} %get-tuple-element.33.refs_0_), channel_id=1, source_target_pairs={{0,1},{1,2},{2,3},{3,0},{4,5},{5,6},{6,7},{7,4},{8,9},{9,10},{10,1... | collective-permute-start | bytes 393224 | tf_op jit(solution)/shard_map/ppermute | solution.py:228

commit v3 on v2

--- a/solution.py
+++ b/solution.py
@@ -14,7 +14,7 @@
 F32 = jnp.float32
 MIB = 1 << 20
 VMEM_SPEC = pl.BlockSpec(memory_space=pltpu.VMEM)
-ANY_SPEC = pl.BlockSpec(memory_space=pl.ANY)
+HBM_SPEC = pl.BlockSpec(memory_space=pltpu.HBM)
 
 
 def kernel_call(body, out_shape, scratch, limit_mib, *operands):
@@ -26,6 +26,10 @@
         scratch_shapes=scratch,
         compiler_params=pltpu.CompilerParams(vmem_limit_bytes=limit_mib * MIB),
     )(*operands)
+
+
+def in_place(array):
+    return pltpu.with_memory_space_constraint(array, pltpu.HBM)
 
 
 def on_chip(array):
@@ -150,11 +154,11 @@
     return pl.pallas_call(
         body,
         out_shape=(shape, shape, pltpu.VMEM(w_qkv.shape, BF), pltpu.VMEM(w_out.shape, BF)),
-        in_specs=[VMEM_SPEC] * 3 + [ANY_SPEC] * 4,
+        in_specs=[VMEM_SPEC] * 3 + [HBM_SPEC] * 4,
         out_specs=(VMEM_SPEC,) * 4,
         scratch_shapes=attention_scratch(rows, key_cache) + [pltpu.SemaphoreType.DMA((4,))],
         compiler_params=pltpu.CompilerParams(vmem_limit_bytes=20 * MIB),
-    )(incoming, take, bias, w_qkv, w_out, key_cache, value_cache)
+    )(incoming, take, bias, *map(in_place, (w_qkv, w_out, key_cache, value_cache)))
 
 
 def norm_attention(parts, residual, gain_bias, w_qkv, w_out, key_cache, value_cache, bias, layer):
@@ -179,11 +183,11 @@
     return pl.pallas_call(
         body,
         out_shape=(shape, shape),
-        in_specs=[VMEM_SPEC] * (count + 5) + [ANY_SPEC] * 2,
+        in_specs=[VMEM_SPEC] * (count + 5) + [HBM_SPEC] * 2,
         out_specs=(VMEM_SPEC, VMEM_SPEC),
         scratch_shapes=attention_scratch(residual.shape[0], key_cache),
         compiler_params=pltpu.CompilerParams(vmem_limit_bytes=20 * MIB),
-    )(*parts, residual, gain_bias, w_qkv, w_out, bias, key_cache, value_cache)
+    )(*parts, residual, gain_bias, w_qkv, w_out, bias, in_place(key_cache), in_place(value_cache))
 
 
 def norm_mlp(parts, residual, gain_bias, w_up, w_down):
@@ -238,8 +242,13 @@
     rows, width = tokens.shape
     lines, stack = blocks * CAP * cols, cols * rows
 
-    def body(order_ref, tok_ref, out_ref, give_ref):
+    def body(order_hbm, tok_hbm, out_ref, give_ref, order_ref, tok_ref, sems):
+        order_copy = pltpu.make_async_copy(order_hbm, order_ref, sems.at[0])
+        token_copy = pltpu.make_async_copy(tok_hbm, tok_ref, sems.at[1])
+        order_copy.start()
+        token_copy.start()
         first = lax.axis_index("req") * rows
+        order_copy.wait()
         wanted = first + iota((stack, order.shape[1]), 0) % rows
         goes = jnp.concatenate(
             [(order_ref[r : r + 1, :] == wanted).astype(F32).astype(BF) for r in range(order.shape[0])], axis=1
@@ -259,10 +268,21 @@
         same = iota((lines, stack), 0) % cols == iota((lines, stack), 1) // rows
         give = jnp.where(same, give, 0.0)
         give_ref[...] = give
+        token_copy.wait()
         out_ref[...] = lay_out(give.astype(BF), tok_ref[...], cols)
 
-    out = (jax.ShapeDtypeStruct((lines, width // cols), BF), jax.ShapeDtypeStruct((lines, stack), F32))
-    return kernel_call(body, out, [], 8, order, tokens)
+    return pl.pallas_call(
+        body,
+        out_shape=(jax.ShapeDtypeStruct((lines, width // cols), BF), jax.ShapeDtypeStruct((lines, stack), F32)),
+        in_specs=[HBM_SPEC] * 2,
+        out_specs=(VMEM_SPEC,) * 2,
+        scratch_shapes=[
+            pltpu.VMEM(order.shape, order.dtype),
+            pltpu.VMEM(tokens.shape, BF),
+            pltpu.SemaphoreType.DMA((2,)),
+        ],
+        compiler_params=pltpu.CompilerParams(vmem_limit_bytes=8 * MIB),
+    )(in_place(order), in_place(tokens))
 
 
 def deal_take(order, give, table, lengths, cols, pages, page_len):

time: 113 us -> 98 us (0.87)
  local copies, waits for them, and re-layouts: 20.6 us -> 2.04 us
  Pallas kernels: 22.1 us -> 25.4 us
    unnamed x32 -> x14, local copies, waits for them, and re-layouts: 20.6 us -> 2.04 us
    pallas_call x1, Pallas kernels: 7.8 us -> 10.1 us  [first_attention(): pl.pallas_call(body, out_shape=(shape, shape, pltpu.VMEM(w_qkv.shape, BF)...]
    pallas_call x0 -> x1, Pallas kernels: none -> 2.15 us  [deal_send(): pl.pallas_call(body, out_shape=(jax.ShapeDtypeStruct((lines, width // col...]
    pallas_call x6 -> x5, Pallas kernels: 7.03 us -> 5.64 us  [kernel_call(): pl.pallas_call(body, out_shape=out_shape, in_specs=[VMEM_SPEC] * len(oper...]
where the time goes in v3:
time: 98 us; the launch traced here: 97.7 us
  waiting for transfers between devices  39 us (40%)
  Pallas kernels  25.4 us (26%)
  starting transfers between devices  17.8 us (18%)
  blocking collectives  13.3 us (14%)
  local copies, waits for them, and re-layouts  2.04 us (2%)
    ppermute x12, waiting for transfers between devices, gather_parts(): lax.ppermute(part, 'tp', [(i, (i + step) % size) for i in range(size)])  32.8 us
    all_to_all x1, blocking collectives, swap(): lax.all_to_all(lines_out.reshape(blocks, lines // blocks, share), 'req',...  13.3 us
    pallas_call x1, Pallas kernels, first_attention(): pl.pallas_call(body, out_shape=(shape, shape, pltpu.VMEM(w_qkv.shape, BF)...  10.1 us
    all_to_all x1, starting transfers between devices, swap(): lax.all_to_all(lines_out.reshape(blocks, lines // blocks, share), 'req',...  9.45 us
    ppermute x12, starting transfers between devices, gather_parts(): lax.ppermute(part, 'tp', [(i, (i + step) % size) for i in range(size)])  8.33 us
    pallas_call x1, Pallas kernels, norm_attention(): pl.pallas_call(body, out_shape=(shape, shape), in_specs=[VMEM_SPEC] * (co...  7.54 us
    all_to_all x1, waiting for transfers between devices, swap(): lax.all_to_all(lines_out.reshape(blocks, lines // blocks, share), 'req',...  6.2 us
    pallas_call x5, Pallas kernels, kernel_call(): pl.pallas_call(body, out_shape=out_shape, in_specs=[VMEM_SPEC] * len(oper...  5.64 us
  transfers between devices with their start and end apart: 13, of which 13 were waited for; matrix products, arithmetic and copies ran while one was open for 0% of the time, Pallas kernels for 1%

profile of v3, /device:TPU:1, one launch (start us, length us, event | category | flops | bytes accessed | tf_op | source)
XLA Modules:
  0.0 97.7 jit_solution(6430136710764999322)
XLA Ops:
  0.0 2.2 %shard_map.118 = (bf16[256,512]{1,0:T(8,128)(2,1)}, f32[256,128]{1,0:T(8,128)S(1)}) custom-call(s32[8,128]{1,0:T(8,128)} %bitcast.11, bf16[32,2048]{1,0:T(8,128)(2,1)} %tok_hbm.1), custom_call_target="tpu_custom_call" | custom-call | tf_op jit(solution)/shard_map/pallas_call | solution.py:274
  2.2 9.4 %all-to-all-start = ((bf16[32,8,512]{2,1,0:T(8,128)(2,1)}), bf16[32,8,512]{2,1,0:T(8,128)(2,1)S(1)}, u32[]{:S(2)}, u32[]{:S(2)}) async-start(bf16[32,8,512]{2,1,0:T(8,128)(2,1)} %bitcast.1), calls=%async_computation | async-start | bytes 524288 | tf_op jit(solution)/shard_map/all_to_all | solution.py:350
  11.6 0.0 copy-start.4
  11.6 0.7 copy-done.4
  12.3 0.0 copy-start.5
  12.3 0.7 copy-done.5
  13.0 0.7 copy-done.6
  13.7 0.7 shard_map.119
  14.4 6.2 %all-to-all-done = bf16[32,8,512]{2,1,0:T(8,128)(2,1)S(1)} async-done(((bf16[32,8,512]{2,1,0:T(8,128)(2,1)}), bf16[32,8,512]{2,1,0:T(8,128)(2,1)S(1)}, u32[]{:S(2)}, u32[]{:S(2)}) %all-to-all-start) | async-done | bytes 262176 | tf_op jit(solution)/shard_map/all_to_all | solution.py:350
  20.6 0.0 copy-start
  20.6 0.0 copy-start.1
  20.6 0.0 copy-start.2
  20.6 10.1 %shard_map.120 = (bf16[32,2048]{1,0:T(8,128)(2,1)S(1)}, bf16[32,2048]{1,0:T(8,128)(2,1)S(1)}, bf16[3,2048,512]{2,1,0:T(8,128)(2,1)S(1)}, bf16[512,2048]{1,0:T(8,128)(2,1)S(1)}) custom-call(bf16[256,512]{1,0:T(8,128)(2,1)S(1)} %bitcast.8, bf16[128,256]{1,0:T(8,128)(2,1)S(1)} %get-tuple-element.23.take_ref, f32[32,5376]{1,0:T(8,128)S(1)} %get-tuple-element.24.b_ref.refs_8_, ...), custom_call_target="tpu_custom_call" | custom-call | tf_op jit(solution)/shard_map/pallas_call | solution.py:154
  30.7 0.0 copy-start.3
  30.7 2.8 %collective-permute-start.2 = (bf16[32,2048]{1,0:T(8,128)(2,1)S(1)}, bf16[32,2048]{1,0:T(8,128)(2,1)S(1)}, u32[]{:S(2)}, u32[]{:S(2)}) collective-permute-start(bf16[32,2048]{1,0:T(8,128)(2,1)S(1)} %get-tuple-element.25.refs_0_), channel_id=1, source_target_pairs={{0,3},{1,0},{2,1},{3,2},{4,7},{5,4},{6,5},{7,6},{8,11},{9,8},{10,9... | collective-permute-start | bytes 393224 | tf_op jit(solution)/shard_map/ppermute | solution.py:232
  33.5 0.3 collective-permute-start.1
  33.9 0.7 collective-permute-start
  34.6 4.3 %collective-permute-done.2.refs_3_ = bf16[32,2048]{1,0:T(8,128)(2,1)S(1)} collective-permute-done((bf16[32,2048]{1,0:T(8,128)(2,1)S(1)}, bf16[32,2048]{1,0:T(8,128)(2,1)S(1)}, u32[]{:S(2)}, u32[]{:S(2)}) %collective-permute-start.2) | collective-permute-done | bytes 131104 | tf_op jit(solution)/shard_map/ppermute | solution.py:232
  38.9 0.8 collective-permute-done.1.refs_2_
  39.7 3.6 %collective-permute-done.refs_1_ = bf16[32,2048]{1,0:T(8,128)(2,1)S(1)} collective-permute-done((bf16[32,2048]{1,0:T(8,128)(2,1)S(1)}, bf16[32,2048]{1,0:T(8,128)(2,1)S(1)}, u32[]{:S(2)}, u32[]{:S(2)}) %collective-permute-start) | collective-permute-done | bytes 131104 | tf_op jit(solution)/shard_map/ppermute | solution.py:232
  43.3 0.0 copy-done
  43.3 0.0 copy-done.1
  43.3 0.0 copy-done.2
  43.3 1.8 %shard_map.121 = (bf16[32,2048]{1,0:T(8,128)(2,1)S(1)}, bf16[32,2048]{1,0:T(8,128)(2,1)S(1)}) custom-call(bf16[32,2048]{1,0:T(8,128)(2,1)S(1)} %get-tuple-element.25.refs_0_, bf16[32,2048]{1,0:T(8,128)(2,1)S(1)} %collective-permute-done.refs_1_, bf16[32,2048]{1,0:T(8,128)(2,1)S(1)} %collective-permute-done.1.refs_2_, ...), custom_call_target="tpu_custom_call" | custom-call | tf_op jit(solution)/shard_map/pallas_call | solution.py:21
  45.1 0.0 collective-permute-start.5
  45.1 0.3 collective-permute-start.4
  45.4 1.1 %collective-permute-start.3 = (bf16[32,2048]{1,0:T(8,128)(2,1)S(1)}, bf16[32,2048]{1,0:T(8,128)(2,1)S(1)}, u32[]{:S(2)}, u32[]{:S(2)}) collective-permute-start(bf16[32,2048]{1,0:T(8,128)(2,1)S(1)} %get-tuple-element.27.refs_0_), channel_id=1, source_target_pairs={{0,1},{1,2},{2,3},{3,0},{4,5},{5,6},{6,7},{7,4},{8,9},{9,10},{10,1... | collective-permute-start | bytes 393224 | tf_op jit(solution)/shard_map/ppermute | solution.py:232
  46.6 3.1 %collective-permute-done.5.refs_3_ = bf16[32,2048]{1,0:T(8,128)(2,1)S(1)} collective-permute-done((bf16[32,2048]{1,0:T(8,128)(2,1)S(1)}, bf16[32,2048]{1,0:T(8,128)(2,1)S(1)}, u32[]{:S(2)}, u32[]{:S(2)}) %collective-permute-start.5) | collective-permute-done | bytes 131104 | tf_op jit(solution)/shard_map/ppermute | solution.py:232
  49.7 0.9 collective-permute-done.4.refs_2_
  50.6 4.3 %collective-permute-done.3.refs_1_ = bf16[32,2048]{1,0:T(8,128)(2,1)S(1)} collective-permute-done((bf16[32,2048]{1,0:T(8,128)(2,1)S(1)}, bf16[32,2048]{1,0:T(8,128)(2,1)S(1)}, u32[]{:S(2)}, u32[]{:S(2)}) %collective-permute-start.3) | collective-permute-done | bytes 131104 | tf_op jit(solution)/shard_map/ppermute | solution.py:232
  54.9 0.0 copy-done.3
  54.9 7.5 %shard_map.122 = (bf16[32,2048]{1,0:T(8,128)(2,1)S(1)}, bf16[32,2048]{1,0:T(8,128)(2,1)S(1)}) custom-call(bf16[32,2048]{1,0:T(8,128)(2,1)S(1)} %get-tuple-element.27.refs_0_, bf16[32,2048]{1,0:T(8,128)(2,1)S(1)} %collective-permute-done.3.refs_1_, bf16[32,2048]{1,0:T(8,128)(2,1)S(1)} %collective-permute-done.4.refs_2_, ...), custom_call_target="tpu_custom_call" | custom-call | tf_op jit(solution)/shard_map/pallas_call | solution.py:183
  62.4 0.1 collective-permute-start.8
  62.5 0.1 collective-permute-start.7
  62.6 1.4 %collective-permute-start.6 = (bf16[32,2048]{1,0:T(8,128)(2,1)S(1)}, bf16[32,2048]{1,0:T(8,128)(2,1)S(1)}, u32[]{:S(2)}, u32[]{:S(2)}) collective-permute-start(bf16[32,2048]{1,0:T(8,128)(2,1)S(1)} %get-tuple-element.31.refs_0_), channel_id=1, source_target_pairs={{0,1},{1,2},{2,3},{3,0},{4,5},{5,6},{6,7},{7,4},{8,9},{9,10},{10,1... | collective-permute-start | bytes 393224 | tf_op jit(solution)/shard_map/ppermute | solution.py:232
  64.0 3.1 %collective-permute-done.8.refs_3_ = bf16[32,2048]{1,0:T(8,128)(2,1)S(1)} collective-permute-done((bf16[32,2048]{1,0:T(8,128)(2,1)S(1)}, bf16[32,2048]{1,0:T(8,128)(2,1)S(1)}, u32[]{:S(2)}, u32[]{:S(2)}) %collective-permute-start.8) | collective-permute-done | bytes 131104 | tf_op jit(solution)/shard_map/ppermute | solution.py:232
  67.1 0.9 collective-permute-done.7.refs_2_
  68.0 3.8 %collective-permute-done.6.refs_1_ = bf16[32,2048]{1,0:T(8,128)(2,1)S(1)} collective-permute-done((bf16[32,2048]{1,0:T(8,128)(2,1)S(1)}, bf16[32,2048]{1,0:T(8,128)(2,1)S(1)}, u32[]{:S(2)}, u32[]{:S(2)}) %collective-permute-start.6) | collective-permute-done | bytes 131104 | tf_op jit(solution)/shard_map/ppermute | solution.py:232
  71.8 1.8 %shard_map.123 = (bf16[32,2048]{1,0:T(8,128)(2,1)S(1)}, bf16[32,2048]{1,0:T(8,128)(2,1)S(1)}) custom-call(bf16[32,2048]{1,0:T(8,128)(2,1)S(1)} %get-tuple-element.31.refs_0_, bf16[32,2048]{1,0:T(8,128)(2,1)S(1)} %collective-permute-done.6.refs_1_, bf16[32,2048]{1,0:T(8,128)(2,1)S(1)} %collective-permute-done.7.refs_2_, ...), custom_call_target="tpu_custom_call" | custom-call | tf_op jit(solution)/shard_map/pallas_call | solution.py:21
  73.6 0.5 collective-permute-start.11
  74.1 0.0 collective-permute-start.10
  74.1 1.0 %collective-permute-start.9 = (bf16[32,2048]{1,0:T(8,128)(2,1)S(1)}, bf16[32,2048]{1,0:T(8,128)(2,1)S(1)}, u32[]{:S(2)}, u32[]{:S(2)}) collective-permute-start(bf16[32,2048]{1,0:T(8,128)(2,1)S(1)} %get-tuple-element.33.refs_0_), channel_id=1, source_target_pairs={{0,1},{1,2},{2,3},{3,0},{4,5},{5,6},{6,7},{7,4},{8,9},{9,10},{10,1... | collective-permute-start | bytes 393224 | tf_op jit(solution)/shard_map/ppermute | solution.py:232
  75.1 2.3 %collective-permute-done.11.refs_3_ = bf16[32,2048]{1,0:T(8,128)(2,1)S(1)} collective-permute-done((bf16[32,2048]{1,0:T(8,128)(2,1)S(1)}, bf16[32,2048]{1,0:T(8,128)(2,1)S(1)}, u32[]{:S(2)}, u32[]{:S(2)}) %collective-permute-start.11) | collective-permute-done | bytes 131104 | tf_op jit(solution)/shard_map/ppermute | solution.py:232
  77.4 2.1 %collective-permute-done.10.refs_2_ = bf16[32,2048]{1,0:T(8,128)(2,1)S(1)} collective-permute-done((bf16[32,2048]{1,0:T(8,128)(2,1)S(1)}, bf16[32,2048]{1,0:T(8,128)(2,1)S(1)}, u32[]{:S(2)}, u32[]{:S(2)}) %collective-permute-start.10) | collective-permute-done | bytes 131104 | tf_op jit(solution)/shard_map/ppermute | solution.py:232
  79.5 3.6 %collective-permute-done.9.refs_1_ = bf16[32,2048]{1,0:T(8,128)(2,1)S(1)} collective-permute-done((bf16[32,2048]{1,0:T(8,128)(2,1)S(1)}, bf16[32,2048]{1,0:T(8,128)(2,1)S(1)}, u32[]{:S(2)}, u32[]{:S(2)}) %collective-permute-start.9) | collective-permute-done | bytes 131104 | tf_op jit(solution)/shard_map/ppermute | solution.py:232
  83.1 0.5 shard_map.124
  83.6 13.3 %all_to_all.10 = bf16[32,8,512]{2,1,0:T(8,128)(2,1)S(1)} all-to-all(bf16[32,8,512]{2,1,0:T(8,128)(2,1)S(1)} %bitcast.10), channel_id=1, replica_groups=mesh['req'=32,'tp'=4] {'req'}, dimensions={0} | all-to-all | bytes 524288 | tf_op jit(solution)/shard_map/all_to_all | solution.py:350
  96.9 0.8 shard_map.125
  (1 shorter events, 0.0 us)
Async XLA Ops:
  2.2 18.4 %all-to-all-start = ((bf16[32,8,512]{2,1,0:T(8,128)(2,1)}), bf16[32,8,512]{2,1,0:T(8,128)(2,1)S(1)}, u32[]{:S(2)}, u32[]{:S(2)}) async-start(bf16[32,8,512]{2,1,0:T(8,128)(2,1)} %bitcast.1), calls=%async_computation | async-start | bytes 524288 | tf_op jit(solution)/shard_map/all_to_all | solution.py:350
  11.6 0.7 copy-start.4
  12.3 0.7 copy-start.5
  13.0 0.7 copy-start.6
  20.6 22.7 %copy-start = (bf16[2048,1024]{1,0:T(8,128)(2,1)S(1)}, bf16[2048,1024]{1,0:T(8,128)(2,1)}, u32[]{:S(2)}) copy-start(bf16[2048,1024]{1,0:T(8,128)(2,1)} %refs_6_.3) | copy-start | bytes 12582916
  20.6 22.7 %copy-start.1 = (bf16[1024,2048]{1,0:T(8,128)(2,1)S(1)}, bf16[1024,2048]{1,0:T(8,128)(2,1)}, u32[]{:S(2)}) copy-start(bf16[1024,2048]{1,0:T(8,128)(2,1)} %refs_7_.3) | copy-start | bytes 12582916
  20.6 22.7 %copy-start.2 = (f32[2,2048]{1,0:T(2,128)S(1)}, f32[2,2048]{1,0:T(2,128)}, u32[]{:S(2)}) copy-start(f32[2,2048]{1,0:T(2,128)} %refs_5_.6) | copy-start | bytes 49156
  30.7 24.2 %copy-start.3 = (f32[2,2048]{1,0:T(2,128)S(1)}, f32[2,2048]{1,0:T(2,128)}, u32[]{:S(2)}) copy-start(f32[2,2048]{1,0:T(2,128)} %refs_5_.7) | copy-start | bytes 49156
  30.7 8.2 %collective-permute-start.2 = (bf16[32,2048]{1,0:T(8,128)(2,1)S(1)}, bf16[32,2048]{1,0:T(8,128)(2,1)S(1)}, u32[]{:S(2)}, u32[]{:S(2)}) collective-permute-start(bf16[32,2048]{1,0:T(8,128)(2,1)S(1)} %get-tuple-element.25.refs_0_), channel_id=1, source_target_pairs={{0,3},{1,0},{2,1},{3,2},{4,7},{5,4},{6,5},{7,6},{8,11},{9,8},{10,9... | collective-permute-start | bytes 393224 | tf_op jit(solution)/shard_map/ppermute | solution.py:232
  33.5 6.1 %collective-permute-start.1 = (bf16[32,2048]{1,0:T(8,128)(2,1)S(1)}, bf16[32,2048]{1,0:T(8,128)(2,1)S(1)}, u32[]{:S(2)}, u32[]{:S(2)}) collective-permute-start(bf16[32,2048]{1,0:T(8,128)(2,1)S(1)} %get-tuple-element.25.refs_0_), channel_id=1, source_target_pairs={{0,2},{1,3},{2,0},{3,1},{4,6},{5,7},{6,4},{7,5},{8,10},{9,11},{10,... | collective-permute-start | bytes 393224 | tf_op jit(solution)/shard_map/ppermute | solution.py:232
  33.9 9.4 %collective-permute-start = (bf16[32,2048]{1,0:T(8,128)(2,1)S(1)}, bf16[32,2048]{1,0:T(8,128)(2,1)S(1)}, u32[]{:S(2)}, u32[]{:S(2)}) collective-permute-start(bf16[32,2048]{1,0:T(8,128)(2,1)S(1)} %get-tuple-element.25.refs_0_), channel_id=1, source_target_pairs={{0,1},{1,2},{2,3},{3,0},{4,5},{5,6},{6,7},{7,4},{8,9},{9,10},{10,1... | collective-permute-start | bytes 393224 | tf_op jit(solution)/shard_map/ppermute | solution.py:232
  45.1 4.6 %collective-permute-start.5 = (bf16[32,2048]{1,0:T(8,128)(2,1)S(1)}, bf16[32,2048]{1,0:T(8,128)(2,1)S(1)}, u32[]{:S(2)}, u32[]{:S(2)}) collective-permute-start(bf16[32,2048]{1,0:T(8,128)(2,1)S(1)} %get-tuple-element.27.refs_0_), channel_id=1, source_target_pairs={{0,3},{1,0},{2,1},{3,2},{4,7},{5,4},{6,5},{7,6},{8,11},{9,8},{10,9... | collective-permute-start | bytes 393224 | tf_op jit(solution)/shard_map/ppermute | solution.py:232
  45.1 5.5 %collective-permute-start.4 = (bf16[32,2048]{1,0:T(8,128)(2,1)S(1)}, bf16[32,2048]{1,0:T(8,128)(2,1)S(1)}, u32[]{:S(2)}, u32[]{:S(2)}) collective-permute-start(bf16[32,2048]{1,0:T(8,128)(2,1)S(1)} %get-tuple-element.27.refs_0_), channel_id=1, source_target_pairs={{0,2},{1,3},{2,0},{3,1},{4,6},{5,7},{6,4},{7,5},{8,10},{9,11},{10,... | collective-permute-start | bytes 393224 | tf_op jit(solution)/shard_map/ppermute | solution.py:232
  45.4 9.5 %collective-permute-start.3 = (bf16[32,2048]{1,0:T(8,128)(2,1)S(1)}, bf16[32,2048]{1,0:T(8,128)(2,1)S(1)}, u32[]{:S(2)}, u32[]{:S(2)}) collective-permute-start(bf16[32,2048]{1,0:T(8,128)(2,1)S(1)} %get-tuple-element.27.refs_0_), channel_id=1, source_target_pairs={{0,1},{1,2},{2,3},{3,0},{4,5},{5,6},{6,7},{7,4},{8,9},{9,10},{10,1... | collective-permute-start | bytes 393224 | tf_op jit(solution)/shard_map/ppermute | solution.py:232
  62.4 4.6 %collective-permute-start.8 = (bf16[32,2048]{1,0:T(8,128)(2,1)S(1)}, bf16[32,2048]{1,0:T(8,128)(2,1)S(1)}, u32[]{:S(2)}, u32[]{:S(2)}) collective-permute-start(bf16[32,2048]{1,0:T(8,128)(2,1)S(1)} %get-tuple-element.31.refs_0_), channel_id=1, source_target_pairs={{0,3},{1,0},{2,1},{3,2},{4,7},{5,4},{6,5},{7,6},{8,11},{9,8},{10,9... | collective-permute-start | bytes 393224 | tf_op jit(solution)/shard_map/ppermute | solution.py:232
  62.5 5.5 %collective-permute-start.7 = (bf16[32,2048]{1,0:T(8,128)(2,1)S(1)}, bf16[32,2048]{1,0:T(8,128)(2,1)S(1)}, u32[]{:S(2)}, u32[]{:S(2)}) collective-permute-start(bf16[32,2048]{1,0:T(8,128)(2,1)S(1)} %get-tuple-element.31.refs_0_), channel_id=1, source_target_pairs={{0,2},{1,3},{2,0},{3,1},{4,6},{5,7},{6,4},{7,5},{8,10},{9,11},{10,... | collective-permute-start | bytes 393224 | tf_op jit(solution)/shard_map/ppermute | solution.py:232
  62.6 9.2 %collective-permute-start.6 = (bf16[32,2048]{1,0:T(8,128)(2,1)S(1)}, bf16[32,2048]{1,0:T(8,128)(2,1)S(1)}, u32[]{:S(2)}, u32[]{:S(2)}) collective-permute-start(bf16[32,2048]{1,0:T(8,128)(2,1)S(1)} %get-tuple-element.31.refs_0_), channel_id=1, source_target_pairs={{0,1},{1,2},{2,3},{3,0},{4,5},{5,6},{6,7},{7,4},{8,9},{9,10},{10,1... | collective-permute-start | bytes 393224 | tf_op jit(solution)/shard_map/ppermute | solution.py:232
  73.6 3.8 %collective-permute-start.11 = (bf16[32,2048]{1,0:T(8,128)(2,1)S(1)}, bf16[32,2048]{1,0:T(8,128)(2,1)S(1)}, u32[]{:S(2)}, u32[]{:S(2)}) collective-permute-start(bf16[32,2048]{1,0:T(8,128)(2,1)S(1)} %get-tuple-element.33.refs_0_), channel_id=1, source_target_pairs={{0,3},{1,0},{2,1},{3,2},{4,7},{5,4},{6,5},{7,6},{8,11},{9,8},{10,9... | collective-permute-start | bytes 393224 | tf_op jit(solution)/shard_map/ppermute | solution.py:232
  74.1 5.4 %collective-permute-start.10 = (bf16[32,2048]{1,0:T(8,128)(2,1)S(1)}, bf16[32,2048]{1,0:T(8,128)(2,1)S(1)}, u32[]{:S(2)}, u32[]{:S(2)}) collective-permute-start(bf16[32,2048]{1,0:T(8,128)(2,1)S(1)} %get-tuple-element.33.refs_0_), channel_id=1, source_target_pairs={{0,2},{1,3},{2,0},{3,1},{4,6},{5,7},{6,4},{7,5},{8,10},{9,11},{10,... | collective-permute-start | bytes 393224 | tf_op jit(solution)/shard_map/ppermute | solution.py:232
  74.1 9.0 %collective-permute-start.9 = (bf16[32,2048]{1,0:T(8,128)(2,1)S(1)}, bf16[32,2048]{1,0:T(8,128)(2,1)S(1)}, u32[]{:S(2)}, u32[]{:S(2)}) collective-permute-start(bf16[32,2048]{1,0:T(8,128)(2,1)S(1)} %get-tuple-element.33.refs_0_), channel_id=1, source_target_pairs={{0,1},{1,2},{2,3},{3,0},{4,5},{5,6},{6,7},{7,4},{8,9},{9,10},{10,1... | collective-permute-start | bytes 393224 | tf_op jit(solution)/shard_map/ppermute | solution.py:232

commit v4 on v3

--- a/solution.py
+++ b/solution.py
@@ -32,10 +32,6 @@
     return pltpu.with_memory_space_constraint(array, pltpu.HBM)
 
 
-def on_chip(array):
-    return pltpu.with_memory_space_constraint(array, pltpu.VMEM)
-
-
 def add_norm(parts, residual, gain_bias):
     total = residual.astype(F32)
     for part in parts:
@@ -47,7 +43,7 @@
     return (centered * lax.rsqrt(row_var + EPS) * gain_bias[0:1, :] + gain_bias[1:2, :]).astype(BF)
 
 
-def attend(x, wait, w_qkv, k_ref, v_ref, w_out, bias, s_ref, p_ref):
+def attend(x, wait, w_qkv, k_ref, v_ref, w_out, bias, s_ref):
     rows = x.shape[0]
     share = w_qkv.shape[2]
     heads = share // HD
@@ -79,16 +75,16 @@
             peak = jnp.maximum(peak, scores[:, i * HD : (i + 1) * HD])
     peak = jnp.maximum(jnp.max(peak, axis=-1, keepdims=True), own)
     sums = jnp.zeros((heads * rows, HD), F32)
+    mixed = jnp.zeros((heads * rows, share), F32)
     for c in range(pages // step):
         weight = jnp.exp((s_ref[:, c * span : (c + 1) * span] - peak) * scale)
-        p_ref[:, c * span : (c + 1) * span] = weight.astype(BF)
         for i in range(span // HD):
             sums = sums + weight[:, i * HD : (i + 1) * HD]
+        wait("value", c)
+        values = v_ref[c * step : (c + 1) * step].reshape(span, share)
+        mixed = mixed + jnp.dot(weight.astype(BF), values, preferred_element_type=F32)
     own_weight = jnp.exp((own - peak) * scale)
     total = jnp.sum(sums, axis=-1, keepdims=True) + own_weight
-    wait("value", 0)
-    values = v_ref[...].reshape(pages * page_len, share)
-    mixed = jnp.dot(p_ref[...], values, preferred_element_type=F32)
     fresh_value = fresh_value.astype(F32)
     own_weight = own_weight.astype(BF).astype(F32)
     attended = []
@@ -105,28 +101,35 @@
     return math.gcd(pages, 6)
 
 
-def cache_copies(k_hbm, v_hbm, layer, k_ref, v_ref, sems):
-    pages = k_ref.shape[0]
-    step = k_step(pages)
-    copies = {}
-    for c in range(pages // step):
-        part = pl.ds(c * step, step)
-        copies["key", c] = pltpu.make_async_copy(k_hbm.at[layer, part], k_ref.at[part], sems.at[c])
-    copies["value", 0] = pltpu.make_async_copy(v_hbm.at[layer], v_ref, sems.at[pages // step])
-    return copies
-
-
-def attention_scratch(rows, key_cache):
-    pages, page_len, share = key_cache.shape[1:]
-    wide = (rows * share // HD, pages * page_len)
-    pool = (pages, page_len, share)
-    return [
-        pltpu.VMEM(wide, F32),
-        pltpu.VMEM(wide, BF),
-        pltpu.VMEM(pool, BF),
-        pltpu.VMEM(pool, BF),
-        pltpu.SemaphoreType.DMA((pages // k_step(pages) + 1,)),
-    ]
+def score_scratch(rows, pages, page_len, share):
+    return pltpu.VMEM((rows * share // HD, pages * page_len), F32)
+
+
+def load(after, *sources):
+    def body(*refs):
+        count = len(sources)
+        copies = [
+            pltpu.make_async_copy(
+                refs[1 + i] if layer is None else refs[1 + i].at[layer], refs[1 + count + i], refs[-1].at[i]
+            )
+            for i, (_, layer) in enumerate(sources)
+        ]
+        for copy in copies:
+            copy.start()
+        for copy in copies:
+            copy.wait()
+
+    shapes = [a.shape if layer is None else a.shape[1:] for a, layer in sources]
+    size = sum(2 * math.prod(shape) for shape in shapes)
+    return pl.pallas_call(
+        body,
+        out_shape=tuple(pltpu.VMEM(shape, BF) for shape in shapes),
+        in_specs=[HBM_SPEC] * (1 + len(sources)),
+        out_specs=(VMEM_SPEC,) * len(sources),
+        scratch_shapes=[pltpu.SemaphoreType.DMA((len(sources),))],
+        compiler_params=pltpu.CompilerParams(vmem_limit_bytes=MIB),
+        cost_estimate=pl.CostEstimate(flops=0, transcendentals=0, bytes_accessed=2 * size),
+    )(after, *(in_place(a) for a, _ in sources))
 
 
 def first_attention(incoming, take, w_qkv, w_out, key_cache, value_cache, bias):
@@ -134,12 +137,19 @@
     lines, share = incoming.shape
     cols = take.shape[0] // rows
 
+    pages, page_len = key_cache.shape[1:3]
+    step = k_step(pages)
+    parts = pages // step
+
     def body(in_ref, take_ref, b_ref, wq_hbm, wo_hbm, k_hbm, v_hbm, x_ref, out_ref, wq_ref, wo_ref,
-             s_ref, p_ref, k_ref, v_ref, sems, w_sems):
-        copies = {
-            ("qkv", i): pltpu.make_async_copy(wq_hbm.at[i], wq_ref.at[i], w_sems.at[i]) for i in range(3)
-        }
-        copies.update(cache_copies(k_hbm, v_hbm, 0, k_ref, v_ref, sems))
+             s_ref, k_ref, v_ref, k_sems, v_sems, w_sems):
+        copies = {}
+        for i in range(3):
+            copies["qkv", i] = pltpu.make_async_copy(wq_hbm.at[i], wq_ref.at[i], w_sems.at[i])
+        for name, hbm, ref, sems in (("key", k_hbm, k_ref, k_sems), ("value", v_hbm, v_ref, v_sems)):
+            for c in range(parts):
+                span = pl.ds(c * step, step)
+                copies[name, c] = pltpu.make_async_copy(hbm.at[0, span], ref.at[span], sems.at[c])
         copies["out", 0] = pltpu.make_async_copy(wo_hbm, wo_ref, w_sems.at[3])
         for copy in copies.values():
             copy.start()
@@ -147,7 +157,7 @@
         x = jnp.concatenate([stacked[c * rows : (c + 1) * rows] for c in range(cols)], axis=1)
         x_ref[...] = x
         out_ref[...] = attend(
-            x, lambda *key: copies[key].wait(), wq_ref, k_ref, v_ref, wo_ref, b_ref, s_ref, p_ref
+            x, lambda *key: copies[key].wait(), wq_ref, k_ref, v_ref, wo_ref, b_ref, s_ref
         )
 
     shape = jax.ShapeDtypeStruct((rows, share * cols), BF)
@@ -156,38 +166,33 @@
         out_shape=(shape, shape, pltpu.VMEM(w_qkv.shape, BF), pltpu.VMEM(w_out.shape, BF)),
         in_specs=[VMEM_SPEC] * 3 + [HBM_SPEC] * 4,
         out_specs=(VMEM_SPEC,) * 4,
-        scratch_shapes=attention_scratch(rows, key_cache) + [pltpu.SemaphoreType.DMA((4,))],
+        scratch_shapes=[
+            score_scratch(rows, pages, page_len, share),
+            pltpu.VMEM(key_cache.shape[1:], BF),
+            pltpu.VMEM(value_cache.shape[1:], BF),
+            pltpu.SemaphoreType.DMA((parts,)),
+            pltpu.SemaphoreType.DMA((parts,)),
+            pltpu.SemaphoreType.DMA((4,)),
+        ],
         compiler_params=pltpu.CompilerParams(vmem_limit_bytes=20 * MIB),
     )(incoming, take, bias, *map(in_place, (w_qkv, w_out, key_cache, value_cache)))
 
 
-def norm_attention(parts, residual, gain_bias, w_qkv, w_out, key_cache, value_cache, bias, layer):
+def norm_attention(parts, residual, gain_bias, w_qkv, w_out, keys, values, bias):
     count = len(parts)
 
     def body(*refs):
-        part_refs, (res_ref, norm_ref, wq_ref, wo_ref, b_ref, k_hbm, v_hbm) = refs[:count], refs[count : count + 7]
-        x_ref, out_ref, s_ref, p_ref, k_ref, v_ref, sems = refs[count + 7 :]
-        copies = cache_copies(k_hbm, v_hbm, layer, k_ref, v_ref, sems)
-        for copy in copies.values():
-            copy.start()
+        part_refs, (res_ref, norm_ref, wq_ref, wo_ref, k_ref, v_ref, b_ref) = refs[:count], refs[count : count + 7]
+        x_ref, out_ref, s_ref = refs[count + 7 :]
         x = add_norm([r[...] for r in part_refs], res_ref[...], norm_ref[...])
         x_ref[...] = x
-
-        def wait(*key):
-            if key in copies:
-                copies[key].wait()
-
-        out_ref[...] = attend(x, wait, wq_ref, k_ref, v_ref, wo_ref, b_ref, s_ref, p_ref)
+        out_ref[...] = attend(x, lambda *key: None, wq_ref, k_ref, v_ref, wo_ref, b_ref, s_ref)
 
     shape = jax.ShapeDtypeStruct(residual.shape, BF)
-    return pl.pallas_call(
-        body,
-        out_shape=(shape, shape),
-        in_specs=[VMEM_SPEC] * (count + 5) + [HBM_SPEC] * 2,
-        out_specs=(VMEM_SPEC, VMEM_SPEC),
-        scratch_shapes=attention_scratch(residual.shape[0], key_cache),
-        compiler_params=pltpu.CompilerParams(vmem_limit_bytes=20 * MIB),
-    )(*parts, residual, gain_bias, w_qkv, w_out, bias, in_place(key_cache), in_place(value_cache))
+    scratch = [score_scratch(residual.shape[0], *keys.shape)]
+    return kernel_call(
+        body, (shape, shape), scratch, 12, *parts, residual, gain_bias, w_qkv, w_out, keys, values, bias
+    )
 
 
 def norm_mlp(parts, residual, gain_bias, w_up, w_down):
@@ -375,17 +380,19 @@
         order, give, page_table.T, lengths.reshape(1, -1), cols, pool_pages, page_len
     )
     w_qkv = jnp.transpose(qkv_weight, (1, 0, 2))
-    w_up = on_chip(up_weight)
-    w_down = on_chip(down_weight)
     current, partial, w_qkv, w_out = first_attention(
         incoming, take, w_qkv, out_weight, key_cache, value_cache, bias
     )
+    w_up, w_down, keys = load(partial, (up_weight, None), (down_weight, None), (key_cache, 1))
     for layer in range(layers):
         hidden, partial = norm_mlp(gather_parts(partial), current, attn_norm, w_up, w_down)
         if layer + 1 < layers:
+            (values,) = load(partial, (value_cache, layer + 1))
             current, partial = norm_attention(
-                gather_parts(partial), hidden, mlp_norm, w_qkv, w_out, key_cache, value_cache, bias, layer + 1
+                gather_parts(partial), hidden, mlp_norm, w_qkv, w_out, keys, values, bias
             )
+            if layer + 2 < layers:
+                (keys,) = load(partial, (key_cache, layer + 2))
     leaving = norm_send(gather_parts(partial), hidden, mlp_norm, send)
     return settle(swap(leaving, blocks), back, req_rows)
 

time: 98 us -> 97.1 us (level)
  waiting for transfers between devices: 39 us -> 31.4 us
  Pallas kernels: 25.4 us -> 32.1 us
    ppermute x12, waiting for transfers between devices: 32.8 us -> 25.2 us  [gather_parts(): lax.ppermute(part, 'tp', [(i, (i + step) % size) for i in range(size)])]
    pallas_call x5 -> x6, Pallas kernels: 5.64 us -> 10.8 us  [kernel_call(): pl.pallas_call(body, out_shape=out_shape, in_specs=[VMEM_SPEC] * len(oper...]
    pallas_call x1, Pallas kernels: 10.1 us -> 11.6 us  [first_attention(): pl.pallas_call(body, out_shape=(shape, shape, pltpu.VMEM(w_qkv.shape, BF)...]
    pallas_call x1 -> x2, Pallas kernels: 7.54 us -> 7.63 us  [load(): pl.pallas_call(body, out_shape=tuple((pltpu.VMEM(shape, BF) for shape in...]
    unnamed x14 -> x10, local copies, waits for them, and re-layouts: 2.04 us -> 2.04 us
  transfers between devices with their start and end apart: 13 -> 13, of which waited for: 13 -> 11; matrix products, arithmetic and copies ran while one was open for 0% -> 0% of each run, Pallas kernels for 1% -> 9%
where the time goes in v4:
time: 97.1 us; the launch traced here: 96.8 us
  Pallas kernels  32.1 us (33%)
  waiting for transfers between devices  31.4 us (32%)
  starting transfers between devices  17.8 us (18%)
  blocking collectives  13.2 us (14%)
  local copies, waits for them, and re-layouts  2.04 us (2%)
    ppermute x12, waiting for transfers between devices, gather_parts(): lax.ppermute(part, 'tp', [(i, (i + step) % size) for i in range(size)])  25.2 us
    all_to_all x1, blocking collectives, swap(): lax.all_to_all(lines_out.reshape(blocks, lines // blocks, share), 'req',...  13.2 us
    pallas_call x1, Pallas kernels, first_attention(): pl.pallas_call(body, out_shape=(shape, shape, pltpu.VMEM(w_qkv.shape, BF)...  11.6 us
    pallas_call x6, Pallas kernels, kernel_call(): pl.pallas_call(body, out_shape=out_shape, in_specs=[VMEM_SPEC] * len(oper...  10.8 us
    all_to_all x1, starting transfers between devices, swap(): lax.all_to_all(lines_out.reshape(blocks, lines // blocks, share), 'req',...  9.45 us
    ppermute x12, starting transfers between devices, gather_parts(): lax.ppermute(part, 'tp', [(i, (i + step) % size) for i in range(size)])  8.35 us
    pallas_call x2, Pallas kernels, load(): pl.pallas_call(body, out_shape=tuple((pltpu.VMEM(shape, BF) for shape in...  7.63 us
    all_to_all x1, waiting for transfers between devices, swap(): lax.all_to_all(lines_out.reshape(blocks, lines // blocks, share), 'req',...  6.2 us
  transfers between devices with their start and end apart: 13, of which 11 were waited for; matrix products, arithmetic and copies ran while one was open for 0% of the time, Pallas kernels for 9%

profile of v4, /device:TPU:1, one launch (start us, length us, event | category | flops | bytes accessed | tf_op | source)
XLA Modules:
  0.0 96.8 jit_solution(16285268429281923569)
XLA Ops:
  0.0 2.1 %shard_map.118 = (bf16[256,512]{1,0:T(8,128)(2,1)}, f32[256,128]{1,0:T(8,128)S(1)}) custom-call(s32[8,128]{1,0:T(8,128)} %bitcast.11, bf16[32,2048]{1,0:T(8,128)(2,1)} %tok_hbm.1), custom_call_target="tpu_custom_call" | custom-call | tf_op jit(solution)/shard_map/pallas_call | solution.py:279
  2.2 9.4 %all-to-all-start = ((bf16[32,8,512]{2,1,0:T(8,128)(2,1)}), bf16[32,8,512]{2,1,0:T(8,128)(2,1)S(1)}, u32[]{:S(2)}, u32[]{:S(2)}) async-start(bf16[32,8,512]{2,1,0:T(8,128)(2,1)} %bitcast.1), calls=%async_computation | async-start | bytes 524288 | tf_op jit(solution)/shard_map/all_to_all | solution.py:355
  11.6 0.0 copy-start.2
  11.6 0.7 copy-done.2
  12.3 0.0 copy-start.3
  12.3 0.7 copy-done.3
  13.0 0.0 copy-start.4
  13.0 0.7 copy-done.4
  13.6 0.7 shard_map.119
  14.4 6.2 %all-to-all-done = bf16[32,8,512]{2,1,0:T(8,128)(2,1)S(1)} async-done(((bf16[32,8,512]{2,1,0:T(8,128)(2,1)}), bf16[32,8,512]{2,1,0:T(8,128)(2,1)S(1)}, u32[]{:S(2)}, u32[]{:S(2)}) %all-to-all-start) | async-done | bytes 262176 | tf_op jit(solution)/shard_map/all_to_all | solution.py:355
  20.6 11.6 %shard_map.120 = (bf16[32,2048]{1,0:T(8,128)(2,1)S(1)}, bf16[32,2048]{1,0:T(8,128)(2,1)S(1)}, bf16[3,2048,512]{2,1,0:T(8,128)(2,1)S(1)}, bf16[512,2048]{1,0:T(8,128)(2,1)S(1)}) custom-call(bf16[256,512]{1,0:T(8,128)(2,1)S(1)} %bitcast.8, bf16[128,256]{1,0:T(8,128)(2,1)S(1)} %get-tuple-element.26.take_ref, f32[32,5376]{1,0:T(8,128)S(1)} %get-tuple-element.27.b_ref.refs_10_, ...), custom_call_target="tpu_custom_call" | custom-call | tf_op jit(solution)/shard_map/pallas_call | solution.py:164
  32.2 0.0 copy-start
  32.2 2.8 %collective-permute-start.2 = (bf16[32,2048]{1,0:T(8,128)(2,1)S(1)}, bf16[32,2048]{1,0:T(8,128)(2,1)S(1)}, u32[]{:S(2)}, u32[]{:S(2)}) collective-permute-start(bf16[32,2048]{1,0:T(8,128)(2,1)S(1)} %get-tuple-element.28.refs_0_), channel_id=1, source_target_pairs={{0,3},{1,0},{2,1},{3,2},{4,7},{5,4},{6,5},{7,6},{8,11},{9,8},{10,9... | collective-permute-start | bytes 393224 | tf_op jit(solution)/shard_map/ppermute | solution.py:237
  35.0 0.4 collective-permute-start.1
  35.4 0.7 collective-permute-start
  36.0 5.1 %shard_map.121 = (bf16[2048,1024]{1,0:T(8,128)(2,1)S(1)}, bf16[1024,2048]{1,0:T(8,128)(2,1)S(1)}, bf16[42,128,512]{2,1,0:T(8,128)(2,1)S(1)}) custom-call(bf16[32,2048]{1,0:T(8,128)(2,1)S(1)} %get-tuple-element.28.refs_0_, bf16[2048,1024]{1,0:T(8,128)(2,1)} %refs_1_.2, bf16[1024,2048]{1,0:T(8,128)(2,1)} %refs_2_.1, bf16[2,42,128,512]{3,2,1,0:T(8,128)(2,1)} %refs_3_.1), custom_call_target="tpu_custom_call" | custom-call | bytes 27787264 | tf_op jit(solution)/shard_map/pallas_call | solution.py:124
  41.1 0.0 collective-permute-done.2.refs_3_
  41.1 0.0 collective-permute-done.1.refs_2_
  41.1 3.6 %collective-permute-done.refs_1_ = bf16[32,2048]{1,0:T(8,128)(2,1)S(1)} collective-permute-done((bf16[32,2048]{1,0:T(8,128)(2,1)S(1)}, bf16[32,2048]{1,0:T(8,128)(2,1)S(1)}, u32[]{:S(2)}, u32[]{:S(2)}) %collective-permute-start) | collective-permute-done | bytes 131104 | tf_op jit(solution)/shard_map/ppermute | solution.py:237
  44.7 0.0 copy-done
  44.7 1.8 %shard_map.122 = (bf16[32,2048]{1,0:T(8,128)(2,1)S(1)}, bf16[32,2048]{1,0:T(8,128)(2,1)S(1)}) custom-call(bf16[32,2048]{1,0:T(8,128)(2,1)S(1)} %get-tuple-element.28.refs_0_, bf16[32,2048]{1,0:T(8,128)(2,1)S(1)} %collective-permute-done.refs_1_, bf16[32,2048]{1,0:T(8,128)(2,1)S(1)} %collective-permute-done.1.refs_2_, ...), custom_call_target="tpu_custom_call" | custom-call | tf_op jit(solution)/shard_map/pallas_call | solution.py:21
  46.5 0.0 copy-start.1
  46.5 0.1 collective-permute-start.5
  46.6 0.3 collective-permute-start.4
  46.9 1.1 %collective-permute-start.3 = (bf16[32,2048]{1,0:T(8,128)(2,1)S(1)}, bf16[32,2048]{1,0:T(8,128)(2,1)S(1)}, u32[]{:S(2)}, u32[]{:S(2)}) collective-permute-start(bf16[32,2048]{1,0:T(8,128)(2,1)S(1)} %get-tuple-element.32.refs_0_), channel_id=1, source_target_pairs={{0,1},{1,2},{2,3},{3,0},{4,5},{5,6},{6,7},{7,4},{8,9},{9,10},{10,1... | collective-permute-start | bytes 393224 | tf_op jit(solution)/shard_map/ppermute | solution.py:237
  48.1 2.6 %shard_map.123.refs_9_ = bf16[42,128,512]{2,1,0:T(8,128)(2,1)S(1)} custom-call(bf16[32,2048]{1,0:T(8,128)(2,1)S(1)} %get-tuple-element.32.refs_0_, bf16[2,42,128,512]{3,2,1,0:T(8,128)(2,1)} %refs_1_.3), custom_call_target="tpu_custom_call" | custom-call | bytes 11010048 | tf_op jit(solution)/shard_map/pallas_call | solution.py:124
  50.6 0.5 collective-permute-done.5.refs_3_
  51.2 0.9 collective-permute-done.4.refs_2_
  52.1 4.3 %collective-permute-done.3.refs_1_ = bf16[32,2048]{1,0:T(8,128)(2,1)S(1)} collective-permute-done((bf16[32,2048]{1,0:T(8,128)(2,1)S(1)}, bf16[32,2048]{1,0:T(8,128)(2,1)S(1)}, u32[]{:S(2)}, u32[]{:S(2)}) %collective-permute-start.3) | collective-permute-done | bytes 131104 | tf_op jit(solution)/shard_map/ppermute | solution.py:237
  56.4 0.0 copy-done.1
  56.4 5.1 %shard_map.124 = (bf16[32,2048]{1,0:T(8,128)(2,1)S(1)}, bf16[32,2048]{1,0:T(8,128)(2,1)S(1)}) custom-call(bf16[32,2048]{1,0:T(8,128)(2,1)S(1)} %get-tuple-element.32.refs_0_, bf16[32,2048]{1,0:T(8,128)(2,1)S(1)} %collective-permute-done.3.refs_1_, bf16[32,2048]{1,0:T(8,128)(2,1)S(1)} %collective-permute-done.4.refs_2_, ...), custom_call_target="tpu_custom_call" | custom-call | tf_op jit(solution)/shard_map/pallas_call | solution.py:21
  61.6 0.0 collective-permute-start.8
  61.6 0.1 collective-permute-start.7
  61.7 1.4 %collective-permute-start.6 = (bf16[32,2048]{1,0:T(8,128)(2,1)S(1)}, bf16[32,2048]{1,0:T(8,128)(2,1)S(1)}, u32[]{:S(2)}, u32[]{:S(2)}) collective-permute-start(bf16[32,2048]{1,0:T(8,128)(2,1)S(1)} %get-tuple-element.37.refs_0_), channel_id=1, source_target_pairs={{0,1},{1,2},{2,3},{3,0},{4,5},{5,6},{6,7},{7,4},{8,9},{9,10},{10,1... | collective-permute-start | bytes 393224 | tf_op jit(solution)/shard_map/ppermute | solution.py:237
  63.1 3.1 %collective-permute-done.8.refs_3_ = bf16[32,2048]{1,0:T(8,128)(2,1)S(1)} collective-permute-done((bf16[32,2048]{1,0:T(8,128)(2,1)S(1)}, bf16[32,2048]{1,0:T(8,128)(2,1)S(1)}, u32[]{:S(2)}, u32[]{:S(2)}) %collective-permute-start.8) | collective-permute-done | bytes 131104 | tf_op jit(solution)/shard_map/ppermute | solution.py:237
  66.2 0.9 collective-permute-done.7.refs_2_
  67.1 3.8 %collective-permute-done.6.refs_1_ = bf16[32,2048]{1,0:T(8,128)(2,1)S(1)} collective-permute-done((bf16[32,2048]{1,0:T(8,128)(2,1)S(1)}, bf16[32,2048]{1,0:T(8,128)(2,1)S(1)}, u32[]{:S(2)}, u32[]{:S(2)}) %collective-permute-start.6) | collective-permute-done | bytes 131104 | tf_op jit(solution)/shard_map/ppermute | solution.py:237
  70.9 1.8 %shard_map.125 = (bf16[32,2048]{1,0:T(8,128)(2,1)S(1)}, bf16[32,2048]{1,0:T(8,128)(2,1)S(1)}) custom-call(bf16[32,2048]{1,0:T(8,128)(2,1)S(1)} %get-tuple-element.37.refs_0_, bf16[32,2048]{1,0:T(8,128)(2,1)S(1)} %collective-permute-done.6.refs_1_, bf16[32,2048]{1,0:T(8,128)(2,1)S(1)} %collective-permute-done.7.refs_2_, ...), custom_call_target="tpu_custom_call" | custom-call | tf_op jit(solution)/shard_map/pallas_call | solution.py:21
  72.7 0.5 collective-permute-start.11
  73.2 0.0 collective-permute-start.10
  73.2 1.0 %collective-permute-start.9 = (bf16[32,2048]{1,0:T(8,128)(2,1)S(1)}, bf16[32,2048]{1,0:T(8,128)(2,1)S(1)}, u32[]{:S(2)}, u32[]{:S(2)}) collective-permute-start(bf16[32,2048]{1,0:T(8,128)(2,1)S(1)} %get-tuple-element.39.refs_0_), channel_id=1, source_target_pairs={{0,1},{1,2},{2,3},{3,0},{4,5},{5,6},{6,7},{7,4},{8,9},{9,10},{10,1... | collective-permute-start | bytes 393224 | tf_op jit(solution)/shard_map/ppermute | solution.py:237
  74.2 2.3 %collective-permute-done.11.refs_3_ = bf16[32,2048]{1,0:T(8,128)(2,1)S(1)} collective-permute-done((bf16[32,2048]{1,0:T(8,128)(2,1)S(1)}, bf16[32,2048]{1,0:T(8,128)(2,1)S(1)}, u32[]{:S(2)}, u32[]{:S(2)}) %collective-permute-start.11) | collective-permute-done | bytes 131104 | tf_op jit(solution)/shard_map/ppermute | solution.py:237
  76.5 2.1 %collective-permute-done.10.refs_2_ = bf16[32,2048]{1,0:T(8,128)(2,1)S(1)} collective-permute-done((bf16[32,2048]{1,0:T(8,128)(2,1)S(1)}, bf16[32,2048]{1,0:T(8,128)(2,1)S(1)}, u32[]{:S(2)}, u32[]{:S(2)}) %collective-permute-start.10) | collective-permute-done | bytes 131104 | tf_op jit(solution)/shard_map/ppermute | solution.py:237
  78.6 3.6 %collective-permute-done.9.refs_1_ = bf16[32,2048]{1,0:T(8,128)(2,1)S(1)} collective-permute-done((bf16[32,2048]{1,0:T(8,128)(2,1)S(1)}, bf16[32,2048]{1,0:T(8,128)(2,1)S(1)}, u32[]{:S(2)}, u32[]{:S(2)}) %collective-permute-start.9) | collective-permute-done | bytes 131104 | tf_op jit(solution)/shard_map/ppermute | solution.py:237
  82.2 0.5 shard_map.126
  82.7 13.2 %all_to_all.10 = bf16[32,8,512]{2,1,0:T(8,128)(2,1)S(1)} all-to-all(bf16[32,8,512]{2,1,0:T(8,128)(2,1)S(1)} %bitcast.10), channel_id=1, replica_groups=mesh['req'=32,'tp'=4] {'req'}, dimensions={0} | all-to-all | bytes 524288 | tf_op jit(solution)/shard_map/all_to_all | solution.py:355
  95.9 0.8 shard_map.127
Async XLA Ops:
  2.2 18.4 %all-to-all-start = ((bf16[32,8,512]{2,1,0:T(8,128)(2,1)}), bf16[32,8,512]{2,1,0:T(8,128)(2,1)S(1)}, u32[]{:S(2)}, u32[]{:S(2)}) async-start(bf16[32,8,512]{2,1,0:T(8,128)(2,1)} %bitcast.1), calls=%async_computation | async-start | bytes 524288 | tf_op jit(solution)/shard_map/all_to_all | solution.py:355
  11.6 0.7 copy-start.2
  12.3 0.7 copy-start.3
  13.0 0.7 copy-start.4
  32.2 12.5 %copy-start = (f32[2,2048]{1,0:T(2,128)S(1)}, f32[2,2048]{1,0:T(2,128)}, u32[]{:S(2)}) copy-start(f32[2,2048]{1,0:T(2,128)} %refs_5_.6) | copy-start | bytes 49156
  32.2 8.9 %collective-permute-start.2 = (bf16[32,2048]{1,0:T(8,128)(2,1)S(1)}, bf16[32,2048]{1,0:T(8,128)(2,1)S(1)}, u32[]{:S(2)}, u32[]{:S(2)}) collective-permute-start(bf16[32,2048]{1,0:T(8,128)(2,1)S(1)} %get-tuple-element.28.refs_0_), channel_id=1, source_target_pairs={{0,3},{1,0},{2,1},{3,2},{4,7},{5,4},{6,5},{7,6},{8,11},{9,8},{10,9... | collective-permute-start | bytes 393224 | tf_op jit(solution)/shard_map/ppermute | solution.py:237
  35.0 6.1 %collective-permute-start.1 = (bf16[32,2048]{1,0:T(8,128)(2,1)S(1)}, bf16[32,2048]{1,0:T(8,128)(2,1)S(1)}, u32[]{:S(2)}, u32[]{:S(2)}) collective-permute-start(bf16[32,2048]{1,0:T(8,128)(2,1)S(1)} %get-tuple-element.28.refs_0_), channel_id=1, source_target_pairs={{0,2},{1,3},{2,0},{3,1},{4,6},{5,7},{6,4},{7,5},{8,10},{9,11},{10,... | collective-permute-start | bytes 393224 | tf_op jit(solution)/shard_map/ppermute | solution.py:237
  35.4 9.4 %collective-permute-start = (bf16[32,2048]{1,0:T(8,128)(2,1)S(1)}, bf16[32,2048]{1,0:T(8,128)(2,1)S(1)}, u32[]{:S(2)}, u32[]{:S(2)}) collective-permute-start(bf16[32,2048]{1,0:T(8,128)(2,1)S(1)} %get-tuple-element.28.refs_0_), channel_id=1, source_target_pairs={{0,1},{1,2},{2,3},{3,0},{4,5},{5,6},{6,7},{7,4},{8,9},{9,10},{10,1... | collective-permute-start | bytes 393224 | tf_op jit(solution)/shard_map/ppermute | solution.py:237
  46.5 9.9 %copy-start.1 = (f32[2,2048]{1,0:T(2,128)S(1)}, f32[2,2048]{1,0:T(2,128)}, u32[]{:S(2)}) copy-start(f32[2,2048]{1,0:T(2,128)} %refs_5_.7) | copy-start | bytes 49156
  46.5 4.6 %collective-permute-start.5 = (bf16[32,2048]{1,0:T(8,128)(2,1)S(1)}, bf16[32,2048]{1,0:T(8,128)(2,1)S(1)}, u32[]{:S(2)}, u32[]{:S(2)}) collective-permute-start(bf16[32,2048]{1,0:T(8,128)(2,1)S(1)} %get-tuple-element.32.refs_0_), channel_id=1, source_target_pairs={{0,3},{1,0},{2,1},{3,2},{4,7},{5,4},{6,5},{7,6},{8,11},{9,8},{10,9... | collective-permute-start | bytes 393224 | tf_op jit(solution)/shard_map/ppermute | solution.py:237
  46.6 5.5 %collective-permute-start.4 = (bf16[32,2048]{1,0:T(8,128)(2,1)S(1)}, bf16[32,2048]{1,0:T(8,128)(2,1)S(1)}, u32[]{:S(2)}, u32[]{:S(2)}) collective-permute-start(bf16[32,2048]{1,0:T(8,128)(2,1)S(1)} %get-tuple-element.32.refs_0_), channel_id=1, source_target_pairs={{0,2},{1,3},{2,0},{3,1},{4,6},{5,7},{6,4},{7,5},{8,10},{9,11},{10,... | collective-permute-start | bytes 393224 | tf_op jit(solution)/shard_map/ppermute | solution.py:237
  46.9 9.5 %collective-permute-start.3 = (bf16[32,2048]{1,0:T(8,128)(2,1)S(1)}, bf16[32,2048]{1,0:T(8,128)(2,1)S(1)}, u32[]{:S(2)}, u32[]{:S(2)}) collective-permute-start(bf16[32,2048]{1,0:T(8,128)(2,1)S(1)} %get-tuple-element.32.refs_0_), channel_id=1, source_target_pairs={{0,1},{1,2},{2,3},{3,0},{4,5},{5,6},{6,7},{7,4},{8,9},{9,10},{10,1... | collective-permute-start | bytes 393224 | tf_op jit(solution)/shard_map/ppermute | solution.py:237
  61.6 4.6 %collective-permute-start.8 = (bf16[32,2048]{1,0:T(8,128)(2,1)S(1)}, bf16[32,2048]{1,0:T(8,128)(2,1)S(1)}, u32[]{:S(2)}, u32[]{:S(2)}) collective-permute-start(bf16[32,2048]{1,0:T(8,128)(2,1)S(1)} %get-tuple-element.37.refs_0_), channel_id=1, source_target_pairs={{0,3},{1,0},{2,1},{3,2},{4,7},{5,4},{6,5},{7,6},{8,11},{9,8},{10,9... | collective-permute-start | bytes 393224 | tf_op jit(solution)/shard_map/ppermute | solution.py:237
  61.6 5.5 %collective-permute-start.7 = (bf16[32,2048]{1,0:T(8,128)(2,1)S(1)}, bf16[32,2048]{1,0:T(8,128)(2,1)S(1)}, u32[]{:S(2)}, u32[]{:S(2)}) collective-permute-start(bf16[32,2048]{1,0:T(8,128)(2,1)S(1)} %get-tuple-element.37.refs_0_), channel_id=1, source_target_pairs={{0,2},{1,3},{2,0},{3,1},{4,6},{5,7},{6,4},{7,5},{8,10},{9,11},{10,... | collective-permute-start | bytes 393224 | tf_op jit(solution)/shard_map/ppermute | solution.py:237
  61.7 9.2 %collective-permute-start.6 = (bf16[32,2048]{1,0:T(8,128)(2,1)S(1)}, bf16[32,2048]{1,0:T(8,128)(2,1)S(1)}, u32[]{:S(2)}, u32[]{:S(2)}) collective-permute-start(bf16[32,2048]{1,0:T(8,128)(2,1)S(1)} %get-tuple-element.37.refs_0_), channel_id=1, source_target_pairs={{0,1},{1,2},{2,3},{3,0},{4,5},{5,6},{6,7},{7,4},{8,9},{9,10},{10,1... | collective-permute-start | bytes 393224 | tf_op jit(solution)/shard_map/ppermute | solution.py:237
  72.7 3.8 %collective-permute-start.11 = (bf16[32,2048]{1,0:T(8,128)(2,1)S(1)}, bf16[32,2048]{1,0:T(8,128)(2,1)S(1)}, u32[]{:S(2)}, u32[]{:S(2)}) collective-permute-start(bf16[32,2048]{1,0:T(8,128)(2,1)S(1)} %get-tuple-element.39.refs_0_), channel_id=1, source_target_pairs={{0,3},{1,0},{2,1},{3,2},{4,7},{5,4},{6,5},{7,6},{8,11},{9,8},{10,9... | collective-permute-start | bytes 393224 | tf_op jit(solution)/shard_map/ppermute | solution.py:237
  73.2 5.4 %collective-permute-start.10 = (bf16[32,2048]{1,0:T(8,128)(2,1)S(1)}, bf16[32,2048]{1,0:T(8,128)(2,1)S(1)}, u32[]{:S(2)}, u32[]{:S(2)}) collective-permute-start(bf16[32,2048]{1,0:T(8,128)(2,1)S(1)} %get-tuple-element.39.refs_0_), channel_id=1, source_target_pairs={{0,2},{1,3},{2,0},{3,1},{4,6},{5,7},{6,4},{7,5},{8,10},{9,11},{10,... | collective-permute-start | bytes 393224 | tf_op jit(solution)/shard_map/ppermute | solution.py:237
  73.2 9.0 %collective-permute-start.9 = (bf16[32,2048]{1,0:T(8,128)(2,1)S(1)}, bf16[32,2048]{1,0:T(8,128)(2,1)S(1)}, u32[]{:S(2)}, u32[]{:S(2)}) collective-permute-start(bf16[32,2048]{1,0:T(8,128)(2,1)S(1)} %get-tuple-element.39.refs_0_), channel_id=1, source_target_pairs={{0,1},{1,2},{2,3},{3,0},{4,5},{5,6},{6,7},{7,4},{8,9},{9,10},{10,1... | collective-permute-start | bytes 393224 | tf_op jit(solution)/shard_map/ppermute | solution.py:237

commit v5 on v4

--- a/solution.py
+++ b/solution.py
@@ -13,6 +13,8 @@
 BF = jnp.bfloat16
 F32 = jnp.float32
 MIB = 1 << 20
+DEPTH = 3
+STEP = 7
 VMEM_SPEC = pl.BlockSpec(memory_space=pltpu.VMEM)
 HBM_SPEC = pl.BlockSpec(memory_space=pltpu.HBM)
 
@@ -43,12 +45,11 @@
     return (centered * lax.rsqrt(row_var + EPS) * gain_bias[0:1, :] + gain_bias[1:2, :]).astype(BF)
 
 
-def attend(x, wait, w_qkv, k_ref, v_ref, w_out, bias, s_ref):
+def attend(x, wait, w_qkv, score, v_ref, w_out, bias, s_ref, step):
     rows = x.shape[0]
     share = w_qkv.shape[2]
     heads = share // HD
-    pages, page_len = k_ref.shape[:2]
-    step = k_step(pages)
+    pages, page_len = v_ref.shape[:2]
     span = step * page_len
     scale = 1.0 / math.sqrt(HD)
     projected = []
@@ -65,9 +66,7 @@
     wide = wide.astype(BF)
     peak = jnp.full((heads * rows, HD), -jnp.inf, F32)
     for c in range(pages // step):
-        wait("key", c)
-        keys = k_ref[c * step : (c + 1) * step].reshape(span, share)
-        scores = lax.dot_general(wide, keys, (((1,), (1,)), ((), ())), preferred_element_type=F32)
+        scores = score(wide, slice(c * span, (c + 1) * span))
         here = bias[:, c * span : (c + 1) * span]
         scores = scores + jnp.concatenate([here] * heads, axis=0)
         s_ref[:, c * span : (c + 1) * span] = scores
@@ -80,7 +79,7 @@
         weight = jnp.exp((s_ref[:, c * span : (c + 1) * span] - peak) * scale)
         for i in range(span // HD):
             sums = sums + weight[:, i * HD : (i + 1) * HD]
-        wait("value", c)
+        wait("value", c * step)
         values = v_ref[c * step : (c + 1) * step].reshape(span, share)
         mixed = mixed + jnp.dot(weight.astype(BF), values, preferred_element_type=F32)
     own_weight = jnp.exp((own - peak) * scale)
@@ -98,7 +97,7 @@
 
 
 def k_step(pages):
-    return math.gcd(pages, 6)
+    return math.gcd(pages, 21)
 
 
 def score_scratch(rows, pages, page_len, share):
@@ -106,8 +105,9 @@
 
 
 def load(after, *sources):
+    count = len(sources)
+
     def body(*refs):
-        count = len(sources)
         copies = [
             pltpu.make_async_copy(
                 refs[1 + i] if layer is None else refs[1 + i].at[layer], refs[1 + count + i], refs[-1].at[i]
@@ -120,16 +120,51 @@
             copy.wait()
 
     shapes = [a.shape if layer is None else a.shape[1:] for a, layer in sources]
-    size = sum(2 * math.prod(shape) for shape in shapes)
     return pl.pallas_call(
         body,
         out_shape=tuple(pltpu.VMEM(shape, BF) for shape in shapes),
-        in_specs=[HBM_SPEC] * (1 + len(sources)),
-        out_specs=(VMEM_SPEC,) * len(sources),
-        scratch_shapes=[pltpu.SemaphoreType.DMA((len(sources),))],
+        in_specs=[HBM_SPEC] * (1 + count),
+        out_specs=(VMEM_SPEC,) * count,
+        scratch_shapes=[pltpu.SemaphoreType.DMA((count,))],
         compiler_params=pltpu.CompilerParams(vmem_limit_bytes=MIB),
-        cost_estimate=pl.CostEstimate(flops=0, transcendentals=0, bytes_accessed=2 * size),
+        cost_estimate=load_cost(shapes),
     )(after, *(in_place(a) for a, _ in sources))
+
+
+def load_cost(shapes):
+    size = sum(2 * math.prod(shape) for shape in shapes)
+    return pl.CostEstimate(flops=0, transcendentals=0, bytes_accessed=2 * size)
+
+
+def load_turned(after, key_cache, layer):
+    pages, page_len, share = key_cache.shape[1:]
+    step = math.gcd(pages, 14)
+    parts = pages // step
+    span = step * page_len
+
+    def body(after_ref, k_hbm, out_ref, k_ref, sems):
+        copies = [
+            pltpu.make_async_copy(k_hbm.at[layer, pl.ds(c * step, step)], k_ref.at[pl.ds(c * step, step)], sems.at[c])
+            for c in range(parts)
+        ]
+        for copy in copies[:3]:
+            copy.start()
+        for c in range(parts):
+            copies[c].wait()
+            if c + 3 < parts:
+                copies[c + 3].start()
+            keys = k_ref[c * step : (c + 1) * step].reshape(span, share)
+            out_ref[:, c * span : (c + 1) * span] = jnp.transpose(keys)
+
+    return pl.pallas_call(
+        body,
+        out_shape=pltpu.VMEM((share, pages * page_len), BF),
+        in_specs=[HBM_SPEC] * 2,
+        out_specs=VMEM_SPEC,
+        scratch_shapes=[pltpu.VMEM((pages, page_len, share), BF), pltpu.SemaphoreType.DMA((parts,))],
+        compiler_params=pltpu.CompilerParams(vmem_limit_bytes=10 * MIB),
+        cost_estimate=load_cost([key_cache.shape[1:]]),
+    )(after, in_place(key_cache))
 
 
 def first_attention(incoming, take, w_qkv, w_out, key_cache, value_cache, bias):
@@ -140,25 +175,43 @@
     pages, page_len = key_cache.shape[1:3]
     step = k_step(pages)
     parts = pages // step
+    span = step * page_len
 
     def body(in_ref, take_ref, b_ref, wq_hbm, wo_hbm, k_hbm, v_hbm, x_ref, out_ref, wq_ref, wo_ref,
-             s_ref, k_ref, v_ref, k_sems, v_sems, w_sems):
+             s_ref, k_ref, turned_ref, v_ref, k_sems, v_sems, w_sems):
         copies = {}
+        for c in range(parts):
+            at = pl.ds(c * step, step)
+            copies["key", c] = pltpu.make_async_copy(k_hbm.at[0, at], k_ref.at[at], k_sems.at[c])
         for i in range(3):
             copies["qkv", i] = pltpu.make_async_copy(wq_hbm.at[i], wq_ref.at[i], w_sems.at[i])
-        for name, hbm, ref, sems in (("key", k_hbm, k_ref, k_sems), ("value", v_hbm, v_ref, v_sems)):
-            for c in range(parts):
-                span = pl.ds(c * step, step)
-                copies[name, c] = pltpu.make_async_copy(hbm.at[0, span], ref.at[span], sems.at[c])
+        for c in range(parts):
+            at = pl.ds(c * step, step)
+            copies["value", c * step] = pltpu.make_async_copy(v_hbm.at[0, at], v_ref.at[at], v_sems.at[c])
         copies["out", 0] = pltpu.make_async_copy(wo_hbm, wo_ref, w_sems.at[3])
-        for copy in copies.values():
-            copy.start()
+        order = list(copies)
+        for key in order[:DEPTH]:
+            copies[key].start()
+
+        def wait(*key):
+            if key not in copies:
+                return
+            copies[key].wait()
+            later = order.index(key) + DEPTH
+            if later < len(order):
+                copies[order[later]].start()
+
+        def score(wide, at):
+            return jnp.dot(wide, turned_ref[:, at], preferred_element_type=F32)
+
         stacked = jnp.dot(take_ref[...], in_ref[...], preferred_element_type=F32).astype(BF)
         x = jnp.concatenate([stacked[c * rows : (c + 1) * rows] for c in range(cols)], axis=1)
         x_ref[...] = x
-        out_ref[...] = attend(
-            x, lambda *key: copies[key].wait(), wq_ref, k_ref, v_ref, wo_ref, b_ref, s_ref
-        )
+        for c in range(parts):
+            wait("key", c)
+            keys = k_ref[c * step : (c + 1) * step].reshape(span, share)
+            turned_ref[:, c * span : (c + 1) * span] = jnp.transpose(keys)
+        out_ref[...] = attend(x, wait, wq_ref, score, v_ref, wo_ref, b_ref, s_ref, math.gcd(step, STEP))
 
     shape = jax.ShapeDtypeStruct((rows, share * cols), BF)
     return pl.pallas_call(
@@ -169,27 +222,33 @@
         scratch_shapes=[
             score_scratch(rows, pages, page_len, share),
             pltpu.VMEM(key_cache.shape[1:], BF),
+            pltpu.VMEM((share, pages * page_len), BF),
             pltpu.VMEM(value_cache.shape[1:], BF),
             pltpu.SemaphoreType.DMA((parts,)),
             pltpu.SemaphoreType.DMA((parts,)),
             pltpu.SemaphoreType.DMA((4,)),
         ],
-        compiler_params=pltpu.CompilerParams(vmem_limit_bytes=20 * MIB),
+        compiler_params=pltpu.CompilerParams(vmem_limit_bytes=24 * MIB),
     )(incoming, take, bias, *map(in_place, (w_qkv, w_out, key_cache, value_cache)))
 
 
 def norm_attention(parts, residual, gain_bias, w_qkv, w_out, keys, values, bias):
     count = len(parts)
+    step = math.gcd(values.shape[0], 6)
 
     def body(*refs):
         part_refs, (res_ref, norm_ref, wq_ref, wo_ref, k_ref, v_ref, b_ref) = refs[:count], refs[count : count + 7]
         x_ref, out_ref, s_ref = refs[count + 7 :]
         x = add_norm([r[...] for r in part_refs], res_ref[...], norm_ref[...])
         x_ref[...] = x
-        out_ref[...] = attend(x, lambda *key: None, wq_ref, k_ref, v_ref, wo_ref, b_ref, s_ref)
+
+        def score(wide, at):
+            return jnp.dot(wide, k_ref[:, at], preferred_element_type=F32)
+
+        out_ref[...] = attend(x, lambda *key: None, wq_ref, score, v_ref, wo_ref, b_ref, s_ref, step)
 
     shape = jax.ShapeDtypeStruct(residual.shape, BF)
-    scratch = [score_scratch(residual.shape[0], *keys.shape)]
+    scratch = [score_scratch(residual.shape[0], *values.shape)]
     return kernel_call(
         body, (shape, shape), scratch, 12, *parts, residual, gain_bias, w_qkv, w_out, keys, values, bias
     )
@@ -246,39 +305,40 @@
 def deal_send(order, tokens, blocks, cols):
     rows, width = tokens.shape
     lines, stack = blocks * CAP * cols, cols * rows
-
-    def body(order_hbm, tok_hbm, out_ref, give_ref, order_ref, tok_ref, sems):
+    groups, lanes = order.shape
+    near = lanes // rows * CAP * cols
+
+    def body(order_hbm, tok_hbm, out_ref, back_ref, order_ref, tok_ref, sems):
         order_copy = pltpu.make_async_copy(order_hbm, order_ref, sems.at[0])
         token_copy = pltpu.make_async_copy(tok_hbm, tok_ref, sems.at[1])
         order_copy.start()
         token_copy.start()
-        first = lax.axis_index("req") * rows
+        wanted = lax.axis_index("req") * rows + iota((rows, lanes), 0)
+        spread = iota((lanes, lines), 0) // rows == iota((lanes, lines), 1) % near // (CAP * cols)
+        spread = spread.astype(F32).astype(BF)
+        line = iota((rows, lines), 1)
+        earlier = (iota((rows, rows), 1) < iota((rows, rows), 0)).astype(F32).astype(BF)
         order_copy.wait()
-        wanted = first + iota((stack, order.shape[1]), 0) % rows
         goes = jnp.concatenate(
-            [(order_ref[r : r + 1, :] == wanted).astype(F32).astype(BF) for r in range(order.shape[0])], axis=1
+            [(order_ref[r : r + 1, :] == wanted).astype(F32).astype(BF) for r in range(groups)], axis=0
         )
-        slots = order.shape[0] * order.shape[1]
-        block_of = (iota((blocks, slots), 1) // rows == iota((blocks, slots), 0)).astype(F32).astype(BF)
-        sent = lax.dot_general(block_of, goes, (((1,), (1,)), ((), ())), preferred_element_type=F32)
-        a, b = iota((stack, stack), 0), iota((stack, stack), 1)
-        earlier = ((a // rows == b // rows) & (a < b)).astype(F32).astype(BF)
-        rank = jnp.dot(sent.astype(BF), earlier, preferred_element_type=F32)
-        line, block = iota((lines, blocks), 0), iota((lines, blocks), 1)
-        give = jnp.zeros((lines, stack), F32)
-        for k in range(CAP):
-            spread = (line // cols == block * CAP + k).astype(F32).astype(BF)
-            chosen = jnp.where(rank == k, sent, 0.0).astype(BF)
-            give = give + jnp.dot(spread, chosen, preferred_element_type=F32)
-        same = iota((lines, stack), 0) % cols == iota((lines, stack), 1) // rows
-        give = jnp.where(same, give, 0.0)
-        give_ref[...] = give
+        sent_by_group = jnp.dot(goes, spread, preferred_element_type=F32)
+        sent = jnp.zeros((rows, lines), F32)
+        for r in range(groups):
+            sent = jnp.where(line // near == r, sent_by_group[r * rows : (r + 1) * rows], sent)
+        rank = jnp.dot(earlier, sent.astype(BF), preferred_element_type=F32).astype(jnp.int32)
+        mine = jnp.where(rank == line // cols % CAP, sent, 0.0)
+        back = jnp.concatenate([jnp.where(line % cols == c, mine, 0.0) for c in range(cols)], axis=0)
+        back_ref[...] = back.astype(BF)
         token_copy.wait()
-        out_ref[...] = lay_out(give.astype(BF), tok_ref[...], cols)
+        out_ref[...] = lay_out(jnp.transpose(back).astype(BF), tok_ref[...], cols)
 
     return pl.pallas_call(
         body,
-        out_shape=(jax.ShapeDtypeStruct((lines, width // cols), BF), jax.ShapeDtypeStruct((lines, stack), F32)),
+        out_shape=(
+            jax.ShapeDtypeStruct((lines, width // cols), BF),
+            jax.ShapeDtypeStruct((stack, lines), BF),
+        ),
         in_specs=[HBM_SPEC] * 2,
         out_specs=(VMEM_SPEC,) * 2,
         scratch_shapes=[
@@ -290,11 +350,11 @@
     )(in_place(order), in_place(tokens))
 
 
-def deal_take(order, give, table, lengths, cols, pages, page_len):
+def deal_take(order, table, lengths, blocks, cols, pages, page_len):
     rows = lengths.shape[1]
-    lines, stack = give.shape
-
-    def body(order_ref, give_ref, table_ref, len_ref, take_ref, back_ref, send_ref, bias_ref):
+    lines, stack = blocks * CAP * cols, cols * rows
+
+    def body(order_ref, table_ref, len_ref, take_ref, send_ref, bias_ref):
         req = lax.axis_index("req")
         slot = req * rows + iota((stack, order.shape[1]), 0) % rows
         mine = jnp.zeros((stack, order.shape[1]), F32)
@@ -311,7 +371,6 @@
         take = (iota((stack, lines), 1) == place).astype(F32)
         take_ref[...] = take.astype(BF)
         send_ref[...] = jnp.transpose(take).astype(BF)
-        back_ref[...] = jnp.transpose(give_ref[...]).astype(BF)
         diagonal = iota((rows, rows), 0) == iota((rows, rows), 1)
 
         def stand(line):
@@ -332,11 +391,10 @@
 
     out = (
         jax.ShapeDtypeStruct((stack, lines), BF),
-        jax.ShapeDtypeStruct((stack, lines), BF),
         jax.ShapeDtypeStruct((lines, stack), BF),
         jax.ShapeDtypeStruct((rows, pages * page_len), F32),
     )
-    return kernel_call(body, out, [], 8, order, give, table, lengths)
+    return kernel_call(body, out, [], 8, order, table, lengths)
 
 
 def settle(incoming, back, rows):
@@ -374,25 +432,25 @@
     cols = lax.axis_size("tp")
     layers, pool_pages, page_len = key_cache.shape[:3]
     order = deal_order.reshape(-1, HD)
-    outgoing, give = deal_send(order, tokens, blocks, cols)
+    outgoing, back = deal_send(order, tokens, blocks, cols)
     incoming = swap(outgoing, blocks)
-    take, back, send, bias = deal_take(
-        order, give, page_table.T, lengths.reshape(1, -1), cols, pool_pages, page_len
+    take, send, bias = deal_take(
+        order, page_table.T, lengths.reshape(1, -1), blocks, cols, pool_pages, page_len
     )
     w_qkv = jnp.transpose(qkv_weight, (1, 0, 2))
     current, partial, w_qkv, w_out = first_attention(
         incoming, take, w_qkv, out_weight, key_cache, value_cache, bias
     )
-    w_up, w_down, keys = load(partial, (up_weight, None), (down_weight, None), (key_cache, 1))
+    w_up, w_down, values = load(partial, (up_weight, None), (down_weight, None), (value_cache, 1))
     for layer in range(layers):
         hidden, partial = norm_mlp(gather_parts(partial), current, attn_norm, w_up, w_down)
         if layer + 1 < layers:
-            (values,) = load(partial, (value_cache, layer + 1))
+            keys = load_turned(partial, key_cache, layer + 1)
             current, partial = norm_attention(
                 gather_parts(partial), hidden, mlp_norm, w_qkv, w_out, keys, values, bias
             )
             if layer + 2 < layers:
-                (keys,) = load(partial, (key_cache, layer + 2))
+                (values,) = load(partial, (value_cache, layer + 2))
     leaving = norm_send(gather_parts(partial), hidden, mlp_norm, send)
     return settle(swap(leaving, blocks), back, req_rows)
 

time: 97.1 us -> 92.3 us (0.951)
  Pallas kernels: 32.1 us -> 27.9 us
    pallas_call x1, Pallas kernels: 11.6 us -> 7.94 us  [first_attention(): pl.pallas_call(body, out_shape=(shape, shape, pltpu.VMEM(w_qkv.shape, BF)...]
    pallas_call x0 -> x1, Pallas kernels: none -> 3.16 us  [load_turned(): pl.pallas_call(body, out_shape=pltpu.VMEM((share, pages * page_len), BF),...]
    pallas_call x2 -> x1, Pallas kernels: 7.63 us -> 5.06 us  [load(): pl.pallas_call(body, out_shape=tuple((pltpu.VMEM(shape, BF) for shape in...]
    pallas_call x6, Pallas kernels: 10.8 us -> 9.72 us  [kernel_call(): pl.pallas_call(body, out_shape=out_shape, in_specs=[VMEM_SPEC] * len(oper...]
  transfers between devices with their start and end apart: 13 -> 13, of which waited for: 11 -> 10; matrix products, arithmetic and copies ran while one was open for 0% -> 0% of each run, Pallas kernels for 9% -> 10%
where the time goes in v5:
time: 92.3 us; the launch traced here: 92 us
  waiting for transfers between devices  30.8 us (33%)
  Pallas kernels  27.9 us (30%)
  starting transfers between devices  17.8 us (19%)
  blocking collectives  13.3 us (14%)
  local copies, waits for them, and re-layouts  2.04 us (2%)
    ppermute x12, waiting for transfers between devices, gather_parts(): lax.ppermute(part, 'tp', [(i, (i + step) % size) for i in range(size)])  24.6 us
    all_to_all x1, blocking collectives, swap(): lax.all_to_all(lines_out.reshape(blocks, lines // blocks, share), 'req',...  13.3 us
    pallas_call x6, Pallas kernels, kernel_call(): pl.pallas_call(body, out_shape=out_shape, in_specs=[VMEM_SPEC] * len(oper...  9.72 us
    all_to_all x1, starting transfers between devices, swap(): lax.all_to_all(lines_out.reshape(blocks, lines // blocks, share), 'req',...  9.45 us
    ppermute x12, starting transfers between devices, gather_parts(): lax.ppermute(part, 'tp', [(i, (i + step) % size) for i in range(size)])  8.37 us
    pallas_call x1, Pallas kernels, first_attention(): pl.pallas_call(body, out_shape=(shape, shape, pltpu.VMEM(w_qkv.shape, BF)...  7.94 us
    all_to_all x1, waiting for transfers between devices, swap(): lax.all_to_all(lines_out.reshape(blocks, lines // blocks, share), 'req',...  6.21 us
    pallas_call x1, Pallas kernels, load(): pl.pallas_call(body, out_shape=tuple((pltpu.VMEM(shape, BF) for shape in...  5.06 us
  transfers between devices with their start and end apart: 13, of which 10 were waited for; matrix products, arithmetic and copies ran while one was open for 0% of the time, Pallas kernels for 10%

profile of v5, /device:TPU:1, one launch (start us, length us, event | category | flops | bytes accessed | tf_op | source)
XLA Modules:
  0.0 92.0 jit_solution(9432022116372609936)
XLA Ops:
  0.0 2.0 %shard_map.118 = (bf16[256,512]{1,0:T(8,128)(2,1)}, bf16[128,256]{1,0:T(8,128)(2,1)S(1)}) custom-call(s32[8,128]{1,0:T(8,128)} %bitcast.11, bf16[32,2048]{1,0:T(8,128)(2,1)} %tok_hbm.1), custom_call_target="tpu_custom_call" | custom-call | tf_op jit(solution)/shard_map/pallas_call | solution.py:336
  2.0 9.4 %all-to-all-start = ((bf16[32,8,512]{2,1,0:T(8,128)(2,1)}), bf16[32,8,512]{2,1,0:T(8,128)(2,1)S(1)}, u32[]{:S(2)}, u32[]{:S(2)}) async-start(bf16[32,8,512]{2,1,0:T(8,128)(2,1)} %bitcast.1), calls=%async_computation | async-start | bytes 524288 | tf_op jit(solution)/shard_map/all_to_all | solution.py:413
  11.5 0.0 copy-start.2
  11.5 0.7 copy-done.2
  12.2 0.0 copy-start.3
  12.2 0.7 copy-done.3
  12.9 0.0 copy-start.4
  12.9 0.7 copy-done.4
  13.5 0.7 shard_map.119
  14.3 6.2 %all-to-all-done = bf16[32,8,512]{2,1,0:T(8,128)(2,1)S(1)} async-done(((bf16[32,8,512]{2,1,0:T(8,128)(2,1)}), bf16[32,8,512]{2,1,0:T(8,128)(2,1)S(1)}, u32[]{:S(2)}, u32[]{:S(2)}) %all-to-all-start) | async-done | bytes 262176 | tf_op jit(solution)/shard_map/all_to_all | solution.py:413
  20.5 7.9 %shard_map.120 = (bf16[32,2048]{1,0:T(8,128)(2,1)S(1)}, bf16[32,2048]{1,0:T(8,128)(2,1)S(1)}, bf16[3,2048,512]{2,1,0:T(8,128)(2,1)S(1)}, bf16[512,2048]{1,0:T(8,128)(2,1)S(1)}) custom-call(bf16[256,512]{1,0:T(8,128)(2,1)S(1)} %bitcast.8, bf16[128,256]{1,0:T(8,128)(2,1)S(1)} %get-tuple-element.24.take_ref, f32[32,5376]{1,0:T(8,128)S(1)} %get-tuple-element.25.b_ref.refs_10_, ...), custom_call_target="tpu_custom_call" | custom-call | tf_op jit(solution)/shard_map/pallas_call | solution.py:217
  28.4 0.0 copy-start
  28.4 2.8 %collective-permute-start.2 = (bf16[32,2048]{1,0:T(8,128)(2,1)S(1)}, bf16[32,2048]{1,0:T(8,128)(2,1)S(1)}, u32[]{:S(2)}, u32[]{:S(2)}) collective-permute-start(bf16[32,2048]{1,0:T(8,128)(2,1)S(1)} %get-tuple-element.26.refs_0_), channel_id=1, source_target_pairs={{0,3},{1,0},{2,1},{3,2},{4,7},{5,4},{6,5},{7,6},{8,11},{9,8},{10,9... | collective-permute-start | bytes 393224 | tf_op jit(solution)/shard_map/ppermute | solution.py:296
  31.2 0.3 collective-permute-start.1
  31.6 0.7 collective-permute-start
  32.3 5.1 %shard_map.121 = (bf16[2048,1024]{1,0:T(8,128)(2,1)S(1)}, bf16[1024,2048]{1,0:T(8,128)(2,1)S(1)}, bf16[42,128,512]{2,1,0:T(8,128)(2,1)S(1)}) custom-call(bf16[32,2048]{1,0:T(8,128)(2,1)S(1)} %get-tuple-element.26.refs_0_, bf16[2048,1024]{1,0:T(8,128)(2,1)} %refs_1_.1, bf16[1024,2048]{1,0:T(8,128)(2,1)} %refs_2_.1, bf16[2,42,128,512]{3,2,1,0:T(8,128)(2,1)} %refs_3_.1), custom_call_target="tpu_custom_call" | custom-call | bytes 27787264 | tf_op jit(solution)/shard_map/pallas_call | solution.py:123
  37.4 0.0 collective-permute-done.2.refs_3_
  37.4 0.0 collective-permute-done.1.refs_2_
  37.4 3.6 %collective-permute-done.refs_1_ = bf16[32,2048]{1,0:T(8,128)(2,1)S(1)} collective-permute-done((bf16[32,2048]{1,0:T(8,128)(2,1)S(1)}, bf16[32,2048]{1,0:T(8,128)(2,1)S(1)}, u32[]{:S(2)}, u32[]{:S(2)}) %collective-permute-start) | collective-permute-done | bytes 131104 | tf_op jit(solution)/shard_map/ppermute | solution.py:296
  41.0 0.0 copy-done
  41.0 1.8 %shard_map.122 = (bf16[32,2048]{1,0:T(8,128)(2,1)S(1)}, bf16[32,2048]{1,0:T(8,128)(2,1)S(1)}) custom-call(bf16[32,2048]{1,0:T(8,128)(2,1)S(1)} %get-tuple-element.26.refs_0_, bf16[32,2048]{1,0:T(8,128)(2,1)S(1)} %collective-permute-done.refs_1_, bf16[32,2048]{1,0:T(8,128)(2,1)S(1)} %collective-permute-done.1.refs_2_, ...), custom_call_target="tpu_custom_call" | custom-call | tf_op jit(solution)/shard_map/pallas_call | solution.py:23
  42.8 0.0 copy-start.1
  42.8 0.1 collective-permute-start.5
  42.9 0.3 collective-permute-start.4
  43.2 1.1 %collective-permute-start.3 = (bf16[32,2048]{1,0:T(8,128)(2,1)S(1)}, bf16[32,2048]{1,0:T(8,128)(2,1)S(1)}, u32[]{:S(2)}, u32[]{:S(2)}) collective-permute-start(bf16[32,2048]{1,0:T(8,128)(2,1)S(1)} %get-tuple-element.30.after_ref.refs_0_), channel_id=1, source_target_pairs={{0,1},{1,2},{2,3},{3,0},{4,5},{5,6},{6,7},{7,4},{8,9},{9,10},{10,1... | collective-permute-start | bytes 393224 | tf_op jit(solution)/shard_map/ppermute | solution.py:296
  44.3 3.2 %shard_map.123.refs_8_ = bf16[512,5376]{1,0:T(8,128)(2,1)S(1)} custom-call(bf16[32,2048]{1,0:T(8,128)(2,1)S(1)} %get-tuple-element.30.after_ref.refs_0_, bf16[2,42,128,512]{3,2,1,0:T(8,128)(2,1)} %k_hbm.3), custom_call_target="tpu_custom_call" | custom-call | bytes 11010048 | tf_op jit(solution)/shard_map/pallas_call | solution.py:159
  47.5 0.0 collective-permute-done.5.refs_3_
  47.5 0.8 collective-permute-done.4.refs_2_
  48.3 4.3 %collective-permute-done.3.refs_1_ = bf16[32,2048]{1,0:T(8,128)(2,1)S(1)} collective-permute-done((bf16[32,2048]{1,0:T(8,128)(2,1)S(1)}, bf16[32,2048]{1,0:T(8,128)(2,1)S(1)}, u32[]{:S(2)}, u32[]{:S(2)}) %collective-permute-start.3) | collective-permute-done | bytes 131104 | tf_op jit(solution)/shard_map/ppermute | solution.py:296
  52.7 0.0 copy-done.1
  52.7 4.1 %shard_map.124 = (bf16[32,2048]{1,0:T(8,128)(2,1)S(1)}, bf16[32,2048]{1,0:T(8,128)(2,1)S(1)}) custom-call(bf16[32,2048]{1,0:T(8,128)(2,1)S(1)} %get-tuple-element.30.after_ref.refs_0_, bf16[32,2048]{1,0:T(8,128)(2,1)S(1)} %collective-permute-done.3.refs_1_, bf16[32,2048]{1,0:T(8,128)(2,1)S(1)} %collective-permute-done.4.refs_2_, ...), custom_call_target="tpu_custom_call" | custom-call | tf_op jit(solution)/shard_map/pallas_call | solution.py:23
  56.7 0.0 collective-permute-start.8
  56.8 0.1 collective-permute-start.7
  56.9 1.4 %collective-permute-start.6 = (bf16[32,2048]{1,0:T(8,128)(2,1)S(1)}, bf16[32,2048]{1,0:T(8,128)(2,1)S(1)}, u32[]{:S(2)}, u32[]{:S(2)}) collective-permute-start(bf16[32,2048]{1,0:T(8,128)(2,1)S(1)} %get-tuple-element.35.refs_0_), channel_id=1, source_target_pairs={{0,1},{1,2},{2,3},{3,0},{4,5},{5,6},{6,7},{7,4},{8,9},{9,10},{10,1... | collective-permute-start | bytes 393224 | tf_op jit(solution)/shard_map/ppermute | solution.py:296
  58.2 3.1 %collective-permute-done.8.refs_3_ = bf16[32,2048]{1,0:T(8,128)(2,1)S(1)} collective-permute-done((bf16[32,2048]{1,0:T(8,128)(2,1)S(1)}, bf16[32,2048]{1,0:T(8,128)(2,1)S(1)}, u32[]{:S(2)}, u32[]{:S(2)}) %collective-permute-start.8) | collective-permute-done | bytes 131104 | tf_op jit(solution)/shard_map/ppermute | solution.py:296
  61.3 0.9 %collective-permute-done.7.refs_2_ = bf16[32,2048]{1,0:T(8,128)(2,1)S(1)} collective-permute-done((bf16[32,2048]{1,0:T(8,128)(2,1)S(1)}, bf16[32,2048]{1,0:T(8,128)(2,1)S(1)}, u32[]{:S(2)}, u32[]{:S(2)}) %collective-permute-start.7) | collective-permute-done | bytes 131104 | tf_op jit(solution)/shard_map/ppermute | solution.py:296
  62.3 3.8 %collective-permute-done.6.refs_1_ = bf16[32,2048]{1,0:T(8,128)(2,1)S(1)} collective-permute-done((bf16[32,2048]{1,0:T(8,128)(2,1)S(1)}, bf16[32,2048]{1,0:T(8,128)(2,1)S(1)}, u32[]{:S(2)}, u32[]{:S(2)}) %collective-permute-start.6) | collective-permute-done | bytes 131104 | tf_op jit(solution)/shard_map/ppermute | solution.py:296
  66.1 1.8 %shard_map.125 = (bf16[32,2048]{1,0:T(8,128)(2,1)S(1)}, bf16[32,2048]{1,0:T(8,128)(2,1)S(1)}) custom-call(bf16[32,2048]{1,0:T(8,128)(2,1)S(1)} %get-tuple-element.35.refs_0_, bf16[32,2048]{1,0:T(8,128)(2,1)S(1)} %collective-permute-done.6.refs_1_, bf16[32,2048]{1,0:T(8,128)(2,1)S(1)} %collective-permute-done.7.refs_2_, ...), custom_call_target="tpu_custom_call" | custom-call | tf_op jit(solution)/shard_map/pallas_call | solution.py:23
  67.9 0.5 collective-permute-start.11
  68.3 0.0 collective-permute-start.10
  68.3 1.0 %collective-permute-start.9 = (bf16[32,2048]{1,0:T(8,128)(2,1)S(1)}, bf16[32,2048]{1,0:T(8,128)(2,1)S(1)}, u32[]{:S(2)}, u32[]{:S(2)}) collective-permute-start(bf16[32,2048]{1,0:T(8,128)(2,1)S(1)} %get-tuple-element.37.refs_0_), channel_id=1, source_target_pairs={{0,1},{1,2},{2,3},{3,0},{4,5},{5,6},{6,7},{7,4},{8,9},{9,10},{10,1... | collective-permute-start | bytes 393224 | tf_op jit(solution)/shard_map/ppermute | solution.py:296
  69.3 2.3 %collective-permute-done.11.refs_3_ = bf16[32,2048]{1,0:T(8,128)(2,1)S(1)} collective-permute-done((bf16[32,2048]{1,0:T(8,128)(2,1)S(1)}, bf16[32,2048]{1,0:T(8,128)(2,1)S(1)}, u32[]{:S(2)}, u32[]{:S(2)}) %collective-permute-start.11) | collective-permute-done | bytes 131104 | tf_op jit(solution)/shard_map/ppermute | solution.py:296
  71.7 2.1 %collective-permute-done.10.refs_2_ = bf16[32,2048]{1,0:T(8,128)(2,1)S(1)} collective-permute-done((bf16[32,2048]{1,0:T(8,128)(2,1)S(1)}, bf16[32,2048]{1,0:T(8,128)(2,1)S(1)}, u32[]{:S(2)}, u32[]{:S(2)}) %collective-permute-start.10) | collective-permute-done | bytes 131104 | tf_op jit(solution)/shard_map/ppermute | solution.py:296
  73.8 3.6 %collective-permute-done.9.refs_1_ = bf16[32,2048]{1,0:T(8,128)(2,1)S(1)} collective-permute-done((bf16[32,2048]{1,0:T(8,128)(2,1)S(1)}, bf16[32,2048]{1,0:T(8,128)(2,1)S(1)}, u32[]{:S(2)}, u32[]{:S(2)}) %collective-permute-start.9) | collective-permute-done | bytes 131104 | tf_op jit(solution)/shard_map/ppermute | solution.py:296
  77.4 0.5 shard_map.126
  77.8 13.3 %all_to_all.10 = bf16[32,8,512]{2,1,0:T(8,128)(2,1)S(1)} all-to-all(bf16[32,8,512]{2,1,0:T(8,128)(2,1)S(1)} %bitcast.10), channel_id=1, replica_groups=mesh['req'=32,'tp'=4] {'req'}, dimensions={0} | all-to-all | bytes 524288 | tf_op jit(solution)/shard_map/all_to_all | solution.py:413
  91.1 0.8 shard_map.127
Async XLA Ops:
  2.0 18.4 %all-to-all-start = ((bf16[32,8,512]{2,1,0:T(8,128)(2,1)}), bf16[32,8,512]{2,1,0:T(8,128)(2,1)S(1)}, u32[]{:S(2)}, u32[]{:S(2)}) async-start(bf16[32,8,512]{2,1,0:T(8,128)(2,1)} %bitcast.1), calls=%async_computation | async-start | bytes 524288 | tf_op jit(solution)/shard_map/all_to_all | solution.py:413
  11.5 0.7 copy-start.2
  12.2 0.7 copy-start.3
  12.9 0.7 copy-start.4
  28.4 12.6 %copy-start = (f32[2,2048]{1,0:T(2,128)S(1)}, f32[2,2048]{1,0:T(2,128)}, u32[]{:S(2)}) copy-start(f32[2,2048]{1,0:T(2,128)} %refs_5_.6) | copy-start | bytes 49156
  28.4 8.9 %collective-permute-start.2 = (bf16[32,2048]{1,0:T(8,128)(2,1)S(1)}, bf16[32,2048]{1,0:T(8,128)(2,1)S(1)}, u32[]{:S(2)}, u32[]{:S(2)}) collective-permute-start(bf16[32,2048]{1,0:T(8,128)(2,1)S(1)} %get-tuple-element.26.refs_0_), channel_id=1, source_target_pairs={{0,3},{1,0},{2,1},{3,2},{4,7},{5,4},{6,5},{7,6},{8,11},{9,8},{10,9... | collective-permute-start | bytes 393224 | tf_op jit(solution)/shard_map/ppermute | solution.py:296
  31.2 6.1 %collective-permute-start.1 = (bf16[32,2048]{1,0:T(8,128)(2,1)S(1)}, bf16[32,2048]{1,0:T(8,128)(2,1)S(1)}, u32[]{:S(2)}, u32[]{:S(2)}) collective-permute-start(bf16[32,2048]{1,0:T(8,128)(2,1)S(1)} %get-tuple-element.26.refs_0_), channel_id=1, source_target_pairs={{0,2},{1,3},{2,0},{3,1},{4,6},{5,7},{6,4},{7,5},{8,10},{9,11},{10,... | collective-permute-start | bytes 393224 | tf_op jit(solution)/shard_map/ppermute | solution.py:296
  31.6 9.4 %collective-permute-start = (bf16[32,2048]{1,0:T(8,128)(2,1)S(1)}, bf16[32,2048]{1,0:T(8,128)(2,1)S(1)}, u32[]{:S(2)}, u32[]{:S(2)}) collective-permute-start(bf16[32,2048]{1,0:T(8,128)(2,1)S(1)} %get-tuple-element.26.refs_0_), channel_id=1, source_target_pairs={{0,1},{1,2},{2,3},{3,0},{4,5},{5,6},{6,7},{7,4},{8,9},{9,10},{10,1... | collective-permute-start | bytes 393224 | tf_op jit(solution)/shard_map/ppermute | solution.py:296
  42.8 9.9 %copy-start.1 = (f32[2,2048]{1,0:T(2,128)S(1)}, f32[2,2048]{1,0:T(2,128)}, u32[]{:S(2)}) copy-start(f32[2,2048]{1,0:T(2,128)} %refs_5_.7) | copy-start | bytes 49156
  42.8 4.7 %collective-permute-start.5 = (bf16[32,2048]{1,0:T(8,128)(2,1)S(1)}, bf16[32,2048]{1,0:T(8,128)(2,1)S(1)}, u32[]{:S(2)}, u32[]{:S(2)}) collective-permute-start(bf16[32,2048]{1,0:T(8,128)(2,1)S(1)} %get-tuple-element.30.after_ref.refs_0_), channel_id=1, source_target_pairs={{0,3},{1,0},{2,1},{3,2},{4,7},{5,4},{6,5},{7,6},{8,11},{9,8},{10,9... | collective-permute-start | bytes 393224 | tf_op jit(solution)/shard_map/ppermute | solution.py:296
  42.9 5.5 %collective-permute-start.4 = (bf16[32,2048]{1,0:T(8,128)(2,1)S(1)}, bf16[32,2048]{1,0:T(8,128)(2,1)S(1)}, u32[]{:S(2)}, u32[]{:S(2)}) collective-permute-start(bf16[32,2048]{1,0:T(8,128)(2,1)S(1)} %get-tuple-element.30.after_ref.refs_0_), channel_id=1, source_target_pairs={{0,2},{1,3},{2,0},{3,1},{4,6},{5,7},{6,4},{7,5},{8,10},{9,11},{10,... | collective-permute-start | bytes 393224 | tf_op jit(solution)/shard_map/ppermute | solution.py:296
  43.2 9.5 %collective-permute-start.3 = (bf16[32,2048]{1,0:T(8,128)(2,1)S(1)}, bf16[32,2048]{1,0:T(8,128)(2,1)S(1)}, u32[]{:S(2)}, u32[]{:S(2)}) collective-permute-start(bf16[32,2048]{1,0:T(8,128)(2,1)S(1)} %get-tuple-element.30.after_ref.refs_0_), channel_id=1, source_target_pairs={{0,1},{1,2},{2,3},{3,0},{4,5},{5,6},{6,7},{7,4},{8,9},{9,10},{10,1... | collective-permute-start | bytes 393224 | tf_op jit(solution)/shard_map/ppermute | solution.py:296
  56.7 4.6 %collective-permute-start.8 = (bf16[32,2048]{1,0:T(8,128)(2,1)S(1)}, bf16[32,2048]{1,0:T(8,128)(2,1)S(1)}, u32[]{:S(2)}, u32[]{:S(2)}) collective-permute-start(bf16[32,2048]{1,0:T(8,128)(2,1)S(1)} %get-tuple-element.35.refs_0_), channel_id=1, source_target_pairs={{0,3},{1,0},{2,1},{3,2},{4,7},{5,4},{6,5},{7,6},{8,11},{9,8},{10,9... | collective-permute-start | bytes 393224 | tf_op jit(solution)/shard_map/ppermute | solution.py:296
  56.8 5.5 %collective-permute-start.7 = (bf16[32,2048]{1,0:T(8,128)(2,1)S(1)}, bf16[32,2048]{1,0:T(8,128)(2,1)S(1)}, u32[]{:S(2)}, u32[]{:S(2)}) collective-permute-start(bf16[32,2048]{1,0:T(8,128)(2,1)S(1)} %get-tuple-element.35.refs_0_), channel_id=1, source_target_pairs={{0,2},{1,3},{2,0},{3,1},{4,6},{5,7},{6,4},{7,5},{8,10},{9,11},{10,... | collective-permute-start | bytes 393224 | tf_op jit(solution)/shard_map/ppermute | solution.py:296
  56.9 9.2 %collective-permute-start.6 = (bf16[32,2048]{1,0:T(8,128)(2,1)S(1)}, bf16[32,2048]{1,0:T(8,128)(2,1)S(1)}, u32[]{:S(2)}, u32[]{:S(2)}) collective-permute-start(bf16[32,2048]{1,0:T(8,128)(2,1)S(1)} %get-tuple-element.35.refs_0_), channel_id=1, source_target_pairs={{0,1},{1,2},{2,3},{3,0},{4,5},{5,6},{6,7},{7,4},{8,9},{9,10},{10,1... | collective-permute-start | bytes 393224 | tf_op jit(solution)/shard_map/ppermute | solution.py:296
  67.9 3.8 %collective-permute-start.11 = (bf16[32,2048]{1,0:T(8,128)(2,1)S(1)}, bf16[32,2048]{1,0:T(8,128)(2,1)S(1)}, u32[]{:S(2)}, u32[]{:S(2)}) collective-permute-start(bf16[32,2048]{1,0:T(8,128)(2,1)S(1)} %get-tuple-element.37.refs_0_), channel_id=1, source_target_pairs={{0,3},{1,0},{2,1},{3,2},{4,7},{5,4},{6,5},{7,6},{8,11},{9,8},{10,9... | collective-permute-start | bytes 393224 | tf_op jit(solution)/shard_map/ppermute | solution.py:296
  68.3 5.4 %collective-permute-start.10 = (bf16[32,2048]{1,0:T(8,128)(2,1)S(1)}, bf16[32,2048]{1,0:T(8,128)(2,1)S(1)}, u32[]{:S(2)}, u32[]{:S(2)}) collective-permute-start(bf16[32,2048]{1,0:T(8,128)(2,1)S(1)} %get-tuple-element.37.refs_0_), channel_id=1, source_target_pairs={{0,2},{1,3},{2,0},{3,1},{4,6},{5,7},{6,4},{7,5},{8,10},{9,11},{10,... | collective-permute-start | bytes 393224 | tf_op jit(solution)/shard_map/ppermute | solution.py:296
  68.3 9.0 %collective-permute-start.9 = (bf16[32,2048]{1,0:T(8,128)(2,1)S(1)}, bf16[32,2048]{1,0:T(8,128)(2,1)S(1)}, u32[]{:S(2)}, u32[]{:S(2)}) collective-permute-start(bf16[32,2048]{1,0:T(8,128)(2,1)S(1)} %get-tuple-element.37.refs_0_), channel_id=1, source_target_pairs={{0,1},{1,2},{2,3},{3,0},{4,5},{5,6},{6,7},{7,4},{8,9},{9,10},{10,1... | collective-permute-start | bytes 393224 | tf_op jit(solution)/shard_map/ppermute | solution.py:296

commit v6 on v5

--- a/solution.py
+++ b/solution.py
@@ -13,8 +13,9 @@
 BF = jnp.bfloat16
 F32 = jnp.float32
 MIB = 1 << 20
-DEPTH = 3
+DEPTH = 4
 STEP = 7
+SPLIT = 1
 VMEM_SPEC = pl.BlockSpec(memory_space=pltpu.VMEM)
 HBM_SPEC = pl.BlockSpec(memory_space=pltpu.HBM)
 
@@ -45,18 +46,13 @@
     return (centered * lax.rsqrt(row_var + EPS) * gain_bias[0:1, :] + gain_bias[1:2, :]).astype(BF)
 
 
-def attend(x, wait, w_qkv, score, v_ref, w_out, bias, s_ref, step):
+def attend(x, wait, project, share, score, v_ref, w_out, bias, s_ref, step):
     rows = x.shape[0]
-    share = w_qkv.shape[2]
     heads = share // HD
     pages, page_len = v_ref.shape[:2]
     span = step * page_len
-    scale = 1.0 / math.sqrt(HD)
-    projected = []
-    for i in range(3):
-        wait("qkv", i)
-        projected.append(jnp.dot(x, w_qkv[i], preferred_element_type=F32).astype(BF))
-    query, fresh_key, fresh_value = projected
+    scale = math.log2(math.e) / math.sqrt(HD)
+    query, fresh_key, fresh_value = (project(x, i).astype(BF) for i in range(3))
     lane_head = lax.broadcasted_iota(jnp.int32, (rows, share), 1) // HD
     wide = jnp.concatenate(
         [jnp.where(lane_head == h, query.astype(F32), 0.0) for h in range(heads)], axis=0
@@ -76,13 +72,13 @@
     sums = jnp.zeros((heads * rows, HD), F32)
     mixed = jnp.zeros((heads * rows, share), F32)
     for c in range(pages // step):
-        weight = jnp.exp((s_ref[:, c * span : (c + 1) * span] - peak) * scale)
+        weight = jnp.exp2((s_ref[:, c * span : (c + 1) * span] - peak) * scale)
         for i in range(span // HD):
             sums = sums + weight[:, i * HD : (i + 1) * HD]
         wait("value", c * step)
         values = v_ref[c * step : (c + 1) * step].reshape(span, share)
         mixed = mixed + jnp.dot(weight.astype(BF), values, preferred_element_type=F32)
-    own_weight = jnp.exp((own - peak) * scale)
+    own_weight = jnp.exp2((own - peak) * scale)
     total = jnp.sum(sums, axis=-1, keepdims=True) + own_weight
     fresh_value = fresh_value.astype(F32)
     own_weight = own_weight.astype(BF).astype(F32)
@@ -92,7 +88,6 @@
         f = slice(h * HD, (h + 1) * HD)
         attended.append((mixed[r, f] + own_weight[r] * fresh_value[:, f]) / total[r])
     attended = jnp.concatenate(attended, axis=1).astype(BF)
-    wait("out", 0)
     return jnp.dot(attended, w_out[...], preferred_element_type=F32).astype(BF)
 
 
@@ -175,20 +170,23 @@
     pages, page_len = key_cache.shape[1:3]
     step = k_step(pages)
     parts = pages // step
-    span = step * page_len
-
-    def body(in_ref, take_ref, b_ref, wq_hbm, wo_hbm, k_hbm, v_hbm, x_ref, out_ref, wq_ref, wo_ref,
-             s_ref, k_ref, turned_ref, v_ref, k_sems, v_sems, w_sems):
+    piece = w_qkv.shape[1] // SPLIT
+
+    def body(in_ref, take_ref, b_ref, wo_ref, wq_hbm, k_hbm, v_hbm, x_ref, out_ref, wq_ref,
+             s_ref, k_ref, v_ref, k_sems, v_sems, w_sems):
         copies = {}
+        for i in range(3):
+            for c in range(SPLIT):
+                at = pl.ds(c * piece, piece)
+                copies["qkv", i, c] = pltpu.make_async_copy(
+                    wq_hbm.at[i, at], wq_ref.at[i, at], w_sems.at[i * SPLIT + c]
+                )
         for c in range(parts):
             at = pl.ds(c * step, step)
-            copies["key", c] = pltpu.make_async_copy(k_hbm.at[0, at], k_ref.at[at], k_sems.at[c])
-        for i in range(3):
-            copies["qkv", i] = pltpu.make_async_copy(wq_hbm.at[i], wq_ref.at[i], w_sems.at[i])
+            copies["key", c * step] = pltpu.make_async_copy(k_hbm.at[0, at], k_ref.at[at], k_sems.at[c])
         for c in range(parts):
             at = pl.ds(c * step, step)
             copies["value", c * step] = pltpu.make_async_copy(v_hbm.at[0, at], v_ref.at[at], v_sems.at[c])
-        copies["out", 0] = pltpu.make_async_copy(wo_hbm, wo_ref, w_sems.at[3])
         order = list(copies)
         for key in order[:DEPTH]:
             copies[key].start()
@@ -202,34 +200,40 @@
                 copies[order[later]].start()
 
         def score(wide, at):
-            return jnp.dot(wide, turned_ref[:, at], preferred_element_type=F32)
+            wait("key", at.start // page_len)
+            keys = k_ref[at.start // page_len : at.stop // page_len].reshape(at.stop - at.start, share)
+            return lax.dot_general(wide, keys, (((1,), (1,)), ((), ())), preferred_element_type=F32)
+
+        def project(x, i):
+            total = None
+            for c in range(SPLIT):
+                wait("qkv", i, c)
+                at = slice(c * piece, (c + 1) * piece)
+                term = jnp.dot(x[:, at], wq_ref[i, at], preferred_element_type=F32)
+                total = term if total is None else total + term
+            return total
 
         stacked = jnp.dot(take_ref[...], in_ref[...], preferred_element_type=F32).astype(BF)
         x = jnp.concatenate([stacked[c * rows : (c + 1) * rows] for c in range(cols)], axis=1)
         x_ref[...] = x
-        for c in range(parts):
-            wait("key", c)
-            keys = k_ref[c * step : (c + 1) * step].reshape(span, share)
-            turned_ref[:, c * span : (c + 1) * span] = jnp.transpose(keys)
-        out_ref[...] = attend(x, wait, wq_ref, score, v_ref, wo_ref, b_ref, s_ref, math.gcd(step, STEP))
+        out_ref[...] = attend(x, wait, project, share, score, v_ref, wo_ref, b_ref, s_ref, math.gcd(step, STEP))
 
     shape = jax.ShapeDtypeStruct((rows, share * cols), BF)
     return pl.pallas_call(
         body,
-        out_shape=(shape, shape, pltpu.VMEM(w_qkv.shape, BF), pltpu.VMEM(w_out.shape, BF)),
-        in_specs=[VMEM_SPEC] * 3 + [HBM_SPEC] * 4,
-        out_specs=(VMEM_SPEC,) * 4,
+        out_shape=(shape, shape, pltpu.VMEM(w_qkv.shape, BF)),
+        in_specs=[VMEM_SPEC] * 4 + [HBM_SPEC] * 3,
+        out_specs=(VMEM_SPEC,) * 3,
         scratch_shapes=[
             score_scratch(rows, pages, page_len, share),
             pltpu.VMEM(key_cache.shape[1:], BF),
-            pltpu.VMEM((share, pages * page_len), BF),
             pltpu.VMEM(value_cache.shape[1:], BF),
             pltpu.SemaphoreType.DMA((parts,)),
             pltpu.SemaphoreType.DMA((parts,)),
-            pltpu.SemaphoreType.DMA((4,)),
+            pltpu.SemaphoreType.DMA((3 * SPLIT,)),
         ],
         compiler_params=pltpu.CompilerParams(vmem_limit_bytes=24 * MIB),
-    )(incoming, take, bias, *map(in_place, (w_qkv, w_out, key_cache, value_cache)))
+    )(incoming, take, bias, w_out, *map(in_place, (w_qkv, key_cache, value_cache)))
 
 
 def norm_attention(parts, residual, gain_bias, w_qkv, w_out, keys, values, bias):
@@ -245,7 +249,10 @@
         def score(wide, at):
             return jnp.dot(wide, k_ref[:, at], preferred_element_type=F32)
 
-        out_ref[...] = attend(x, lambda *key: None, wq_ref, score, v_ref, wo_ref, b_ref, s_ref, step)
+        def project(x, i):
+            return jnp.dot(x, wq_ref[i], preferred_element_type=F32)
+
+        out_ref[...] = attend(x, lambda *key: None, project, wq_ref.shape[2], score, v_ref, wo_ref, b_ref, s_ref, step)
 
     shape = jax.ShapeDtypeStruct(residual.shape, BF)
     scratch = [score_scratch(residual.shape[0], *values.shape)]
@@ -350,11 +357,13 @@
     )(in_place(order), in_place(tokens))
 
 
-def deal_take(order, table, lengths, blocks, cols, pages, page_len):
+def deal_take(order, table, lengths, w_out, blocks, cols, pages, page_len):
     rows = lengths.shape[1]
     lines, stack = blocks * CAP * cols, cols * rows
 
-    def body(order_ref, table_ref, len_ref, take_ref, send_ref, bias_ref):
+    def body(order_ref, table_ref, len_ref, wo_hbm, take_ref, send_ref, bias_ref, wo_ref, sem):
+        copy = pltpu.make_async_copy(wo_hbm, wo_ref, sem)
+        copy.start()
         req = lax.axis_index("req")
         slot = req * rows + iota((stack, order.shape[1]), 0) % rows
         mine = jnp.zeros((stack, order.shape[1]), F32)
@@ -388,13 +397,22 @@
             bias_ref[:, p * page_len : (p + 1) * page_len] = jnp.where(
                 offset < room[:, p : p + 1], 0.0, -jnp.inf
             ).astype(F32)
+        copy.wait()
 
     out = (
         jax.ShapeDtypeStruct((stack, lines), BF),
         jax.ShapeDtypeStruct((lines, stack), BF),
         jax.ShapeDtypeStruct((rows, pages * page_len), F32),
+        pltpu.VMEM(w_out.shape, BF),
     )
-    return kernel_call(body, out, [], 8, order, table, lengths)
+    return pl.pallas_call(
+        body,
+        out_shape=out,
+        in_specs=[VMEM_SPEC] * 3 + [HBM_SPEC],
+        out_specs=(VMEM_SPEC,) * 4,
+        scratch_shapes=[pltpu.SemaphoreType.DMA],
+        compiler_params=pltpu.CompilerParams(vmem_limit_bytes=8 * MIB),
+    )(order, table, lengths, in_place(w_out))
 
 
 def settle(incoming, back, rows):
@@ -434,13 +452,11 @@
     order = deal_order.reshape(-1, HD)
     outgoing, back = deal_send(order, tokens, blocks, cols)
     incoming = swap(outgoing, blocks)
-    take, send, bias = deal_take(
-        order, page_table.T, lengths.reshape(1, -1), blocks, cols, pool_pages, page_len
+    take, send, bias, w_out = deal_take(
+        order, page_table.T, lengths.reshape(1, -1), out_weight, blocks, cols, pool_pages, page_len
     )
     w_qkv = jnp.transpose(qkv_weight, (1, 0, 2))
-    current, partial, w_qkv, w_out = first_attention(
-        incoming, take, w_qkv, out_weight, key_cache, value_cache, bias
-    )
+    current, partial, w_qkv = first_attention(incoming, take, w_qkv, w_out, key_cache, value_cache, bias)
     w_up, w_down, values = load(partial, (up_weight, None), (down_weight, None), (value_cache, 1))
     for layer in range(layers):
         hidden, partial = norm_mlp(gather_parts(partial), current, attn_norm, w_up, w_down)

time: 92.3 us -> 91.8 us (level)
    pallas_call x0 -> x1, Pallas kernels: none -> 1.6 us  [deal_take(): pl.pallas_call(body, out_shape=out, in_specs=[VMEM_SPEC] * 3 + [HBM_SPEC]...]
    pallas_call x6 -> x5, Pallas kernels: 9.72 us -> 8.93 us  [kernel_call(): pl.pallas_call(body, out_shape=out_shape, in_specs=[VMEM_SPEC] * len(oper...]
  transfers between devices with their start and end apart: 13 -> 13, of which waited for: 10 -> 10; matrix products, arithmetic and copies ran while one was open for 0% -> 0% of each run, Pallas kernels for 10% -> 11%
where the time goes in v6:
time: 91.8 us; the launch traced here: 91.4 us
  waiting for transfers between devices  29.9 us (33%)
  Pallas kernels  28.3 us (31%)
  starting transfers between devices  17.8 us (19%)
  blocking collectives  13.3 us (14%)
  local copies, waits for them, and re-layouts  2.04 us (2%)
    ppermute x12, waiting for transfers between devices, gather_parts(): lax.ppermute(part, 'tp', [(i, (i + step) % size) for i in range(size)])  24.6 us
    all_to_all x1, blocking collectives, swap(): lax.all_to_all(lines_out.reshape(blocks, lines // blocks, share), 'req',...  13.3 us
    all_to_all x1, starting transfers between devices, swap(): lax.all_to_all(lines_out.reshape(blocks, lines // blocks, share), 'req',...  9.45 us
    pallas_call x5, Pallas kernels, kernel_call(): pl.pallas_call(body, out_shape=out_shape, in_specs=[VMEM_SPEC] * len(oper...  8.93 us
    ppermute x12, starting transfers between devices, gather_parts(): lax.ppermute(part, 'tp', [(i, (i + step) % size) for i in range(size)])  8.35 us
    pallas_call x1, Pallas kernels, first_attention(): pl.pallas_call(body, out_shape=(shape, shape, pltpu.VMEM(w_qkv.shape, BF)...  7.49 us
    all_to_all x1, waiting for transfers between devices, swap(): lax.all_to_all(lines_out.reshape(blocks, lines // blocks, share), 'req',...  5.35 us
    pallas_call x1, Pallas kernels, load(): pl.pallas_call(body, out_shape=tuple((pltpu.VMEM(shape, BF) for shape in...  5.06 us
  transfers between devices with their start and end apart: 13, of which 10 were waited for; matrix products, arithmetic and copies ran while one was open for 0% of the time, Pallas kernels for 11%

profile of v6, /device:TPU:1, one launch (start us, length us, event | category | flops | bytes accessed | tf_op | source)
XLA Modules:
  0.0 91.4 jit_solution(16360601979468557904)
XLA Ops:
  0.0 2.0 %shard_map.118 = (bf16[256,512]{1,0:T(8,128)(2,1)}, bf16[128,256]{1,0:T(8,128)(2,1)S(1)}) custom-call(s32[8,128]{1,0:T(8,128)} %bitcast.11, bf16[32,2048]{1,0:T(8,128)(2,1)} %tok_hbm.1), custom_call_target="tpu_custom_call" | custom-call | tf_op jit(solution)/shard_map/pallas_call | solution.py:343
  2.0 9.4 %all-to-all-start = ((bf16[32,8,512]{2,1,0:T(8,128)(2,1)}), bf16[32,8,512]{2,1,0:T(8,128)(2,1)S(1)}, u32[]{:S(2)}, u32[]{:S(2)}) async-start(bf16[32,8,512]{2,1,0:T(8,128)(2,1)} %bitcast.1), calls=%async_computation | async-start | bytes 524288 | tf_op jit(solution)/shard_map/all_to_all | solution.py:431
  11.5 0.0 copy-start.2
  11.5 0.7 copy-done.2
  12.2 0.0 copy-start.3
  12.2 0.7 copy-done.3
  12.9 0.0 copy-start.4
  12.9 0.7 copy-done.4
  13.5 1.6 %shard_map.119 = (bf16[128,256]{1,0:T(8,128)(2,1)S(1)}, bf16[256,128]{1,0:T(8,128)(2,1)S(1)}, f32[32,5376]{1,0:T(8,128)S(1)}, bf16[512,2048]{1,0:T(8,128)(2,1)S(1)}) custom-call(s32[8,128]{1,0:T(8,128)S(1)} %bitcast.12, s32[6,32]{1,0:T(8,128)S(1)} %bitcast.13, s32[1,32]{1,0:T(1,128)S(1)} %bitcast.14, bf16[512,2048]{1,0:T(8,128)(2,1)} %wo_hbm.1), custom_call_target="tpu_custom_call" | custom-call | tf_op jit(solution)/shard_map/pallas_call | solution.py:408
  15.1 5.3 %all-to-all-done = bf16[32,8,512]{2,1,0:T(8,128)(2,1)S(1)} async-done(((bf16[32,8,512]{2,1,0:T(8,128)(2,1)}), bf16[32,8,512]{2,1,0:T(8,128)(2,1)S(1)}, u32[]{:S(2)}, u32[]{:S(2)}) %all-to-all-start) | async-done | bytes 262176 | tf_op jit(solution)/shard_map/all_to_all | solution.py:431
  20.5 7.5 %shard_map.120 = (bf16[32,2048]{1,0:T(8,128)(2,1)S(1)}, bf16[32,2048]{1,0:T(8,128)(2,1)S(1)}, bf16[3,2048,512]{2,1,0:T(8,128)(2,1)S(1)}) custom-call(bf16[256,512]{1,0:T(8,128)(2,1)S(1)} %bitcast.8, bf16[128,256]{1,0:T(8,128)(2,1)S(1)} %get-tuple-element.24.take_ref, f32[32,5376]{1,0:T(8,128)S(1)} %get-tuple-element.25.b_ref.refs_10_, ...), custom_call_target="tpu_custom_call" | custom-call | tf_op jit(solution)/shard_map/pallas_call | solution.py:222
  28.0 0.0 copy-start
  28.0 2.8 %collective-permute-start.2 = (bf16[32,2048]{1,0:T(8,128)(2,1)S(1)}, bf16[32,2048]{1,0:T(8,128)(2,1)S(1)}, u32[]{:S(2)}, u32[]{:S(2)}) collective-permute-start(bf16[32,2048]{1,0:T(8,128)(2,1)S(1)} %get-tuple-element.27.refs_0_), channel_id=1, source_target_pairs={{0,3},{1,0},{2,1},{3,2},{4,7},{5,4},{6,5},{7,6},{8,11},{9,8},{10,9... | collective-permute-start | bytes 393224 | tf_op jit(solution)/shard_map/ppermute | solution.py:303
  30.8 0.3 collective-permute-start.1
  31.1 0.7 collective-permute-start
  31.8 5.1 %shard_map.121 = (bf16[2048,1024]{1,0:T(8,128)(2,1)S(1)}, bf16[1024,2048]{1,0:T(8,128)(2,1)S(1)}, bf16[42,128,512]{2,1,0:T(8,128)(2,1)S(1)}) custom-call(bf16[32,2048]{1,0:T(8,128)(2,1)S(1)} %get-tuple-element.27.refs_0_, bf16[2048,1024]{1,0:T(8,128)(2,1)} %refs_1_.1, bf16[1024,2048]{1,0:T(8,128)(2,1)} %refs_2_.1, bf16[2,42,128,512]{3,2,1,0:T(8,128)(2,1)} %refs_3_.1), custom_call_target="tpu_custom_call" | custom-call | bytes 27787264 | tf_op jit(solution)/shard_map/pallas_call | solution.py:118
  36.9 0.0 collective-permute-done.2.refs_3_
  36.9 0.0 collective-permute-done.1.refs_2_
  36.9 3.6 %collective-permute-done.refs_1_ = bf16[32,2048]{1,0:T(8,128)(2,1)S(1)} collective-permute-done((bf16[32,2048]{1,0:T(8,128)(2,1)S(1)}, bf16[32,2048]{1,0:T(8,128)(2,1)S(1)}, u32[]{:S(2)}, u32[]{:S(2)}) %collective-permute-start) | collective-permute-done | bytes 131104 | tf_op jit(solution)/shard_map/ppermute | solution.py:303
  40.5 0.0 copy-done
  40.5 1.8 %shard_map.122 = (bf16[32,2048]{1,0:T(8,128)(2,1)S(1)}, bf16[32,2048]{1,0:T(8,128)(2,1)S(1)}) custom-call(bf16[32,2048]{1,0:T(8,128)(2,1)S(1)} %get-tuple-element.27.refs_0_, bf16[32,2048]{1,0:T(8,128)(2,1)S(1)} %collective-permute-done.refs_1_, bf16[32,2048]{1,0:T(8,128)(2,1)S(1)} %collective-permute-done.1.refs_2_, ...), custom_call_target="tpu_custom_call" | custom-call | tf_op jit(solution)/shard_map/pallas_call | solution.py:24
  42.3 0.0 copy-start.1
  42.3 0.1 collective-permute-start.5
  42.4 0.3 collective-permute-start.4
  42.7 1.2 %collective-permute-start.3 = (bf16[32,2048]{1,0:T(8,128)(2,1)S(1)}, bf16[32,2048]{1,0:T(8,128)(2,1)S(1)}, u32[]{:S(2)}, u32[]{:S(2)}) collective-permute-start(bf16[32,2048]{1,0:T(8,128)(2,1)S(1)} %get-tuple-element.31.after_ref.refs_0_), channel_id=1, source_target_pairs={{0,1},{1,2},{2,3},{3,0},{4,5},{5,6},{6,7},{7,4},{8,9},{9,10},{10,1... | collective-permute-start | bytes 393224 | tf_op jit(solution)/shard_map/ppermute | solution.py:303
  43.9 3.2 %shard_map.123.refs_8_ = bf16[512,5376]{1,0:T(8,128)(2,1)S(1)} custom-call(bf16[32,2048]{1,0:T(8,128)(2,1)S(1)} %get-tuple-element.31.after_ref.refs_0_, bf16[2,42,128,512]{3,2,1,0:T(8,128)(2,1)} %k_hbm.3), custom_call_target="tpu_custom_call" | custom-call | bytes 11010048 | tf_op jit(solution)/shard_map/pallas_call | solution.py:154
  47.0 0.0 collective-permute-done.5.refs_3_
  47.0 0.8 collective-permute-done.4.refs_2_
  47.9 4.3 %collective-permute-done.3.refs_1_ = bf16[32,2048]{1,0:T(8,128)(2,1)S(1)} collective-permute-done((bf16[32,2048]{1,0:T(8,128)(2,1)S(1)}, bf16[32,2048]{1,0:T(8,128)(2,1)S(1)}, u32[]{:S(2)}, u32[]{:S(2)}) %collective-permute-start.3) | collective-permute-done | bytes 131104 | tf_op jit(solution)/shard_map/ppermute | solution.py:303
  52.2 0.0 copy-done.1
  52.2 4.0 %shard_map.124 = (bf16[32,2048]{1,0:T(8,128)(2,1)S(1)}, bf16[32,2048]{1,0:T(8,128)(2,1)S(1)}) custom-call(bf16[32,2048]{1,0:T(8,128)(2,1)S(1)} %get-tuple-element.31.after_ref.refs_0_, bf16[32,2048]{1,0:T(8,128)(2,1)S(1)} %collective-permute-done.3.refs_1_, bf16[32,2048]{1,0:T(8,128)(2,1)S(1)} %collective-permute-done.4.refs_2_, ...), custom_call_target="tpu_custom_call" | custom-call | tf_op jit(solution)/shard_map/pallas_call | solution.py:24
  56.2 0.0 collective-permute-start.8
  56.3 0.1 collective-permute-start.7
  56.4 1.4 %collective-permute-start.6 = (bf16[32,2048]{1,0:T(8,128)(2,1)S(1)}, bf16[32,2048]{1,0:T(8,128)(2,1)S(1)}, u32[]{:S(2)}, u32[]{:S(2)}) collective-permute-start(bf16[32,2048]{1,0:T(8,128)(2,1)S(1)} %get-tuple-element.35.refs_0_), channel_id=1, source_target_pairs={{0,1},{1,2},{2,3},{3,0},{4,5},{5,6},{6,7},{7,4},{8,9},{9,10},{10,1... | collective-permute-start | bytes 393224 | tf_op jit(solution)/shard_map/ppermute | solution.py:303
  57.7 3.1 %collective-permute-done.8.refs_3_ = bf16[32,2048]{1,0:T(8,128)(2,1)S(1)} collective-permute-done((bf16[32,2048]{1,0:T(8,128)(2,1)S(1)}, bf16[32,2048]{1,0:T(8,128)(2,1)S(1)}, u32[]{:S(2)}, u32[]{:S(2)}) %collective-permute-start.8) | collective-permute-done | bytes 131104 | tf_op jit(solution)/shard_map/ppermute | solution.py:303
  60.8 0.9 %collective-permute-done.7.refs_2_ = bf16[32,2048]{1,0:T(8,128)(2,1)S(1)} collective-permute-done((bf16[32,2048]{1,0:T(8,128)(2,1)S(1)}, bf16[32,2048]{1,0:T(8,128)(2,1)S(1)}, u32[]{:S(2)}, u32[]{:S(2)}) %collective-permute-start.7) | collective-permute-done | bytes 131104 | tf_op jit(solution)/shard_map/ppermute | solution.py:303
  61.7 3.8 %collective-permute-done.6.refs_1_ = bf16[32,2048]{1,0:T(8,128)(2,1)S(1)} collective-permute-done((bf16[32,2048]{1,0:T(8,128)(2,1)S(1)}, bf16[32,2048]{1,0:T(8,128)(2,1)S(1)}, u32[]{:S(2)}, u32[]{:S(2)}) %collective-permute-start.6) | collective-permute-done | bytes 131104 | tf_op jit(solution)/shard_map/ppermute | solution.py:303
  65.6 1.8 %shard_map.125 = (bf16[32,2048]{1,0:T(8,128)(2,1)S(1)}, bf16[32,2048]{1,0:T(8,128)(2,1)S(1)}) custom-call(bf16[32,2048]{1,0:T(8,128)(2,1)S(1)} %get-tuple-element.35.refs_0_, bf16[32,2048]{1,0:T(8,128)(2,1)S(1)} %collective-permute-done.6.refs_1_, bf16[32,2048]{1,0:T(8,128)(2,1)S(1)} %collective-permute-done.7.refs_2_, ...), custom_call_target="tpu_custom_call" | custom-call | tf_op jit(solution)/shard_map/pallas_call | solution.py:24
  67.3 0.5 collective-permute-start.11
  67.8 0.0 collective-permute-start.10
  67.8 1.0 %collective-permute-start.9 = (bf16[32,2048]{1,0:T(8,128)(2,1)S(1)}, bf16[32,2048]{1,0:T(8,128)(2,1)S(1)}, u32[]{:S(2)}, u32[]{:S(2)}) collective-permute-start(bf16[32,2048]{1,0:T(8,128)(2,1)S(1)} %get-tuple-element.37.refs_0_), channel_id=1, source_target_pairs={{0,1},{1,2},{2,3},{3,0},{4,5},{5,6},{6,7},{7,4},{8,9},{9,10},{10,1... | collective-permute-start | bytes 393224 | tf_op jit(solution)/shard_map/ppermute | solution.py:303
  68.8 2.3 %collective-permute-done.11.refs_3_ = bf16[32,2048]{1,0:T(8,128)(2,1)S(1)} collective-permute-done((bf16[32,2048]{1,0:T(8,128)(2,1)S(1)}, bf16[32,2048]{1,0:T(8,128)(2,1)S(1)}, u32[]{:S(2)}, u32[]{:S(2)}) %collective-permute-start.11) | collective-permute-done | bytes 131104 | tf_op jit(solution)/shard_map/ppermute | solution.py:303
  71.2 2.1 %collective-permute-done.10.refs_2_ = bf16[32,2048]{1,0:T(8,128)(2,1)S(1)} collective-permute-done((bf16[32,2048]{1,0:T(8,128)(2,1)S(1)}, bf16[32,2048]{1,0:T(8,128)(2,1)S(1)}, u32[]{:S(2)}, u32[]{:S(2)}) %collective-permute-start.10) | collective-permute-done | bytes 131104 | tf_op jit(solution)/shard_map/ppermute | solution.py:303
  73.2 3.6 %collective-permute-done.9.refs_1_ = bf16[32,2048]{1,0:T(8,128)(2,1)S(1)} collective-permute-done((bf16[32,2048]{1,0:T(8,128)(2,1)S(1)}, bf16[32,2048]{1,0:T(8,128)(2,1)S(1)}, u32[]{:S(2)}, u32[]{:S(2)}) %collective-permute-start.9) | collective-permute-done | bytes 131104 | tf_op jit(solution)/shard_map/ppermute | solution.py:303
  76.8 0.5 shard_map.126
  77.3 13.3 %all_to_all.10 = bf16[32,8,512]{2,1,0:T(8,128)(2,1)S(1)} all-to-all(bf16[32,8,512]{2,1,0:T(8,128)(2,1)S(1)} %bitcast.10), channel_id=1, replica_groups=mesh['req'=32,'tp'=4] {'req'}, dimensions={0} | all-to-all | bytes 524288 | tf_op jit(solution)/shard_map/all_to_all | solution.py:431
  90.6 0.8 shard_map.127
Async XLA Ops:
  2.0 18.4 %all-to-all-start = ((bf16[32,8,512]{2,1,0:T(8,128)(2,1)}), bf16[32,8,512]{2,1,0:T(8,128)(2,1)S(1)}, u32[]{:S(2)}, u32[]{:S(2)}) async-start(bf16[32,8,512]{2,1,0:T(8,128)(2,1)} %bitcast.1), calls=%async_computation | async-start | bytes 524288 | tf_op jit(solution)/shard_map/all_to_all | solution.py:431
  11.5 0.7 copy-start.2
  12.2 0.7 copy-start.3
  12.9 0.7 copy-start.4
  28.0 12.5 %copy-start = (f32[2,2048]{1,0:T(2,128)S(1)}, f32[2,2048]{1,0:T(2,128)}, u32[]{:S(2)}) copy-start(f32[2,2048]{1,0:T(2,128)} %refs_5_.6) | copy-start | bytes 49156
  28.0 8.9 %collective-permute-start.2 = (bf16[32,2048]{1,0:T(8,128)(2,1)S(1)}, bf16[32,2048]{1,0:T(8,128)(2,1)S(1)}, u32[]{:S(2)}, u32[]{:S(2)}) collective-permute-start(bf16[32,2048]{1,0:T(8,128)(2,1)S(1)} %get-tuple-element.27.refs_0_), channel_id=1, source_target_pairs={{0,3},{1,0},{2,1},{3,2},{4,7},{5,4},{6,5},{7,6},{8,11},{9,8},{10,9... | collective-permute-start | bytes 393224 | tf_op jit(solution)/shard_map/ppermute | solution.py:303
  30.8 6.2 %collective-permute-start.1 = (bf16[32,2048]{1,0:T(8,128)(2,1)S(1)}, bf16[32,2048]{1,0:T(8,128)(2,1)S(1)}, u32[]{:S(2)}, u32[]{:S(2)}) collective-permute-start(bf16[32,2048]{1,0:T(8,128)(2,1)S(1)} %get-tuple-element.27.refs_0_), channel_id=1, source_target_pairs={{0,2},{1,3},{2,0},{3,1},{4,6},{5,7},{6,4},{7,5},{8,10},{9,11},{10,... | collective-permute-start | bytes 393224 | tf_op jit(solution)/shard_map/ppermute | solution.py:303
  31.1 9.4 %collective-permute-start = (bf16[32,2048]{1,0:T(8,128)(2,1)S(1)}, bf16[32,2048]{1,0:T(8,128)(2,1)S(1)}, u32[]{:S(2)}, u32[]{:S(2)}) collective-permute-start(bf16[32,2048]{1,0:T(8,128)(2,1)S(1)} %get-tuple-element.27.refs_0_), channel_id=1, source_target_pairs={{0,1},{1,2},{2,3},{3,0},{4,5},{5,6},{6,7},{7,4},{8,9},{9,10},{10,1... | collective-permute-start | bytes 393224 | tf_op jit(solution)/shard_map/ppermute | solution.py:303
  42.3 9.9 %copy-start.1 = (f32[2,2048]{1,0:T(2,128)S(1)}, f32[2,2048]{1,0:T(2,128)}, u32[]{:S(2)}) copy-start(f32[2,2048]{1,0:T(2,128)} %refs_5_.7) | copy-start | bytes 49156
  42.3 4.7 %collective-permute-start.5 = (bf16[32,2048]{1,0:T(8,128)(2,1)S(1)}, bf16[32,2048]{1,0:T(8,128)(2,1)S(1)}, u32[]{:S(2)}, u32[]{:S(2)}) collective-permute-start(bf16[32,2048]{1,0:T(8,128)(2,1)S(1)} %get-tuple-element.31.after_ref.refs_0_), channel_id=1, source_target_pairs={{0,3},{1,0},{2,1},{3,2},{4,7},{5,4},{6,5},{7,6},{8,11},{9,8},{10,9... | collective-permute-start | bytes 393224 | tf_op jit(solution)/shard_map/ppermute | solution.py:303
  42.4 5.5 %collective-permute-start.4 = (bf16[32,2048]{1,0:T(8,128)(2,1)S(1)}, bf16[32,2048]{1,0:T(8,128)(2,1)S(1)}, u32[]{:S(2)}, u32[]{:S(2)}) collective-permute-start(bf16[32,2048]{1,0:T(8,128)(2,1)S(1)} %get-tuple-element.31.after_ref.refs_0_), channel_id=1, source_target_pairs={{0,2},{1,3},{2,0},{3,1},{4,6},{5,7},{6,4},{7,5},{8,10},{9,11},{10,... | collective-permute-start | bytes 393224 | tf_op jit(solution)/shard_map/ppermute | solution.py:303
  42.7 9.5 %collective-permute-start.3 = (bf16[32,2048]{1,0:T(8,128)(2,1)S(1)}, bf16[32,2048]{1,0:T(8,128)(2,1)S(1)}, u32[]{:S(2)}, u32[]{:S(2)}) collective-permute-start(bf16[32,2048]{1,0:T(8,128)(2,1)S(1)} %get-tuple-element.31.after_ref.refs_0_), channel_id=1, source_target_pairs={{0,1},{1,2},{2,3},{3,0},{4,5},{5,6},{6,7},{7,4},{8,9},{9,10},{10,1... | collective-permute-start | bytes 393224 | tf_op jit(solution)/shard_map/ppermute | solution.py:303
  56.2 4.6 %collective-permute-start.8 = (bf16[32,2048]{1,0:T(8,128)(2,1)S(1)}, bf16[32,2048]{1,0:T(8,128)(2,1)S(1)}, u32[]{:S(2)}, u32[]{:S(2)}) collective-permute-start(bf16[32,2048]{1,0:T(8,128)(2,1)S(1)} %get-tuple-element.35.refs_0_), channel_id=1, source_target_pairs={{0,3},{1,0},{2,1},{3,2},{4,7},{5,4},{6,5},{7,6},{8,11},{9,8},{10,9... | collective-permute-start | bytes 393224 | tf_op jit(solution)/shard_map/ppermute | solution.py:303
  56.3 5.5 %collective-permute-start.7 = (bf16[32,2048]{1,0:T(8,128)(2,1)S(1)}, bf16[32,2048]{1,0:T(8,128)(2,1)S(1)}, u32[]{:S(2)}, u32[]{:S(2)}) collective-permute-start(bf16[32,2048]{1,0:T(8,128)(2,1)S(1)} %get-tuple-element.35.refs_0_), channel_id=1, source_target_pairs={{0,2},{1,3},{2,0},{3,1},{4,6},{5,7},{6,4},{7,5},{8,10},{9,11},{10,... | collective-permute-start | bytes 393224 | tf_op jit(solution)/shard_map/ppermute | solution.py:303
  56.4 9.2 %collective-permute-start.6 = (bf16[32,2048]{1,0:T(8,128)(2,1)S(1)}, bf16[32,2048]{1,0:T(8,128)(2,1)S(1)}, u32[]{:S(2)}, u32[]{:S(2)}) collective-permute-start(bf16[32,2048]{1,0:T(8,128)(2,1)S(1)} %get-tuple-element.35.refs_0_), channel_id=1, source_target_pairs={{0,1},{1,2},{2,3},{3,0},{4,5},{5,6},{6,7},{7,4},{8,9},{9,10},{10,1... | collective-permute-start | bytes 393224 | tf_op jit(solution)/shard_map/ppermute | solution.py:303
  67.3 3.8 %collective-permute-start.11 = (bf16[32,2048]{1,0:T(8,128)(2,1)S(1)}, bf16[32,2048]{1,0:T(8,128)(2,1)S(1)}, u32[]{:S(2)}, u32[]{:S(2)}) collective-permute-start(bf16[32,2048]{1,0:T(8,128)(2,1)S(1)} %get-tuple-element.37.refs_0_), channel_id=1, source_target_pairs={{0,3},{1,0},{2,1},{3,2},{4,7},{5,4},{6,5},{7,6},{8,11},{9,8},{10,9... | collective-permute-start | bytes 393224 | tf_op jit(solution)/shard_map/ppermute | solution.py:303
  67.8 5.4 %collective-permute-start.10 = (bf16[32,2048]{1,0:T(8,128)(2,1)S(1)}, bf16[32,2048]{1,0:T(8,128)(2,1)S(1)}, u32[]{:S(2)}, u32[]{:S(2)}) collective-permute-start(bf16[32,2048]{1,0:T(8,128)(2,1)S(1)} %get-tuple-element.37.refs_0_), channel_id=1, source_target_pairs={{0,2},{1,3},{2,0},{3,1},{4,6},{5,7},{6,4},{7,5},{8,10},{9,11},{10,... | collective-permute-start | bytes 393224 | tf_op jit(solution)/shard_map/ppermute | solution.py:303
  67.8 9.0 %collective-permute-start.9 = (bf16[32,2048]{1,0:T(8,128)(2,1)S(1)}, bf16[32,2048]{1,0:T(8,128)(2,1)S(1)}, u32[]{:S(2)}, u32[]{:S(2)}) collective-permute-start(bf16[32,2048]{1,0:T(8,128)(2,1)S(1)} %get-tuple-element.37.refs_0_), channel_id=1, source_target_pairs={{0,1},{1,2},{2,3},{3,0},{4,5},{5,6},{6,7},{7,4},{8,9},{9,10},{10,1... | collective-permute-start | bytes 393224 | tf_op jit(solution)/shard_map/ppermute | solution.py:303

commit v7 on v6

--- a/solution.py
+++ b/solution.py
@@ -301,7 +301,7 @@
     size = lax.axis_size("tp")
     return [part] + [
         lax.ppermute(part, "tp", [(i, (i + step) % size) for i in range(size)])
-        for step in range(1, size)
+        for step in range(size - 1, 0, -1)
     ]
 
 

time: 91.8 us -> 88.6 us (0.965)
  waiting for transfers between devices: 29.9 us -> 13.9 us
  starting transfers between devices: 17.8 us -> 27.7 us
  blocking collectives: 13.3 us -> 16.2 us
    ppermute x12, waiting for transfers between devices: 24.6 us -> 8.56 us  [gather_parts(): lax.ppermute(part, 'tp', [(i, (i + step) % size) for i in range(size)])]
    ppermute x12, starting transfers between devices: 8.35 us -> 18.3 us  [gather_parts(): lax.ppermute(part, 'tp', [(i, (i + step) % size) for i in range(size)])]
    all_to_all x1, blocking collectives: 13.3 us -> 16.2 us  [swap(): lax.all_to_all(lines_out.reshape(blocks, lines // blocks, share), 'req',...]
  transfers between devices with their start and end apart: 13 -> 13, of which waited for: 10 -> 9; matrix products, arithmetic and copies ran while one was open for 0% -> 0% of each run, Pallas kernels for 11% -> 11%
where the time goes in v7:
time: 88.6 us; the launch traced here: 88.3 us
  Pallas kernels  28.3 us (32%)
  starting transfers between devices  27.7 us (31%)
  blocking collectives  16.2 us (18%)
  waiting for transfers between devices  13.9 us (16%)
  local copies, waits for them, and re-layouts  2.04 us (2%)
    ppermute x12, starting transfers between devices, gather_parts(): lax.ppermute(part, 'tp', [(i, (i + step) % size) for i in range(size)])  18.3 us
    all_to_all x1, blocking collectives, swap(): lax.all_to_all(lines_out.reshape(blocks, lines // blocks, share), 'req',...  16.2 us
    all_to_all x1, starting transfers between devices, swap(): lax.all_to_all(lines_out.reshape(blocks, lines // blocks, share), 'req',...  9.45 us
    pallas_call x5, Pallas kernels, kernel_call(): pl.pallas_call(body, out_shape=out_shape, in_specs=[VMEM_SPEC] * len(oper...  8.92 us
    ppermute x12, waiting for transfers between devices, gather_parts(): lax.ppermute(part, 'tp', [(i, (i + step) % size) for i in range(size)])  8.56 us
    pallas_call x1, Pallas kernels, first_attention(): pl.pallas_call(body, out_shape=(shape, shape, pltpu.VMEM(w_qkv.shape, BF)...  7.49 us
    all_to_all x1, waiting for transfers between devices, swap(): lax.all_to_all(lines_out.reshape(blocks, lines // blocks, share), 'req',...  5.35 us
    pallas_call x1, Pallas kernels, load(): pl.pallas_call(body, out_shape=tuple((pltpu.VMEM(shape, BF) for shape in...  5.06 us
  transfers between devices with their start and end apart: 13, of which 9 were waited for; matrix products, arithmetic and copies ran while one was open for 0% of the time, Pallas kernels for 11%

profile of v7, /device:TPU:1, one launch (start us, length us, event | category | flops | bytes accessed | tf_op | source)
XLA Modules:
  0.0 88.3 jit_solution(7097166834378264229)
XLA Ops:
  0.0 2.0 %shard_map.118 = (bf16[256,512]{1,0:T(8,128)(2,1)}, bf16[128,256]{1,0:T(8,128)(2,1)S(1)}) custom-call(s32[8,128]{1,0:T(8,128)} %bitcast.11, bf16[32,2048]{1,0:T(8,128)(2,1)} %tok_hbm.1), custom_call_target="tpu_custom_call" | custom-call | tf_op jit(solution)/shard_map/pallas_call | solution.py:343
  2.0 9.4 %all-to-all-start = ((bf16[32,8,512]{2,1,0:T(8,128)(2,1)}), bf16[32,8,512]{2,1,0:T(8,128)(2,1)S(1)}, u32[]{:S(2)}, u32[]{:S(2)}) async-start(bf16[32,8,512]{2,1,0:T(8,128)(2,1)} %bitcast.1), calls=%async_computation | async-start | bytes 524288 | tf_op jit(solution)/shard_map/all_to_all | solution.py:431
  11.5 0.0 copy-start.2
  11.5 0.7 copy-done.2
  12.2 0.0 copy-start.3
  12.2 0.7 copy-done.3
  12.9 0.0 copy-start.4
  12.9 0.7 copy-done.4
  13.5 1.6 %shard_map.119 = (bf16[128,256]{1,0:T(8,128)(2,1)S(1)}, bf16[256,128]{1,0:T(8,128)(2,1)S(1)}, f32[32,5376]{1,0:T(8,128)S(1)}, bf16[512,2048]{1,0:T(8,128)(2,1)S(1)}) custom-call(s32[8,128]{1,0:T(8,128)S(1)} %bitcast.12, s32[6,32]{1,0:T(8,128)S(1)} %bitcast.13, s32[1,32]{1,0:T(1,128)S(1)} %bitcast.14, bf16[512,2048]{1,0:T(8,128)(2,1)} %wo_hbm.1), custom_call_target="tpu_custom_call" | custom-call | tf_op jit(solution)/shard_map/pallas_call | solution.py:408
  15.1 5.3 %all-to-all-done = bf16[32,8,512]{2,1,0:T(8,128)(2,1)S(1)} async-done(((bf16[32,8,512]{2,1,0:T(8,128)(2,1)}), bf16[32,8,512]{2,1,0:T(8,128)(2,1)S(1)}, u32[]{:S(2)}, u32[]{:S(2)}) %all-to-all-start) | async-done | bytes 262176 | tf_op jit(solution)/shard_map/all_to_all | solution.py:431
  20.5 7.5 %shard_map.120 = (bf16[32,2048]{1,0:T(8,128)(2,1)S(1)}, bf16[32,2048]{1,0:T(8,128)(2,1)S(1)}, bf16[3,2048,512]{2,1,0:T(8,128)(2,1)S(1)}) custom-call(bf16[256,512]{1,0:T(8,128)(2,1)S(1)} %bitcast.8, bf16[128,256]{1,0:T(8,128)(2,1)S(1)} %get-tuple-element.24.take_ref, f32[32,5376]{1,0:T(8,128)S(1)} %get-tuple-element.25.b_ref.refs_10_, ...), custom_call_target="tpu_custom_call" | custom-call | tf_op jit(solution)/shard_map/pallas_call | solution.py:222
  28.0 0.0 copy-start
  28.0 1.4 %collective-permute-start.2 = (bf16[32,2048]{1,0:T(8,128)(2,1)S(1)}, bf16[32,2048]{1,0:T(8,128)(2,1)S(1)}, u32[]{:S(2)}, u32[]{:S(2)}) collective-permute-start(bf16[32,2048]{1,0:T(8,128)(2,1)S(1)} %get-tuple-element.27.refs_0_), channel_id=1, source_target_pairs={{0,1},{1,2},{2,3},{3,0},{4,5},{5,6},{6,7},{7,4},{8,9},{9,10},{10,1... | collective-permute-start | bytes 393224 | tf_op jit(solution)/shard_map/ppermute | solution.py:303
  29.3 2.6 %collective-permute-start.1 = (bf16[32,2048]{1,0:T(8,128)(2,1)S(1)}, bf16[32,2048]{1,0:T(8,128)(2,1)S(1)}, u32[]{:S(2)}, u32[]{:S(2)}) collective-permute-start(bf16[32,2048]{1,0:T(8,128)(2,1)S(1)} %get-tuple-element.27.refs_0_), channel_id=1, source_target_pairs={{0,2},{1,3},{2,0},{3,1},{4,6},{5,7},{6,4},{7,5},{8,10},{9,11},{10,... | collective-permute-start | bytes 393224 | tf_op jit(solution)/shard_map/ppermute | solution.py:303
  32.0 1.1 %collective-permute-start = (bf16[32,2048]{1,0:T(8,128)(2,1)S(1)}, bf16[32,2048]{1,0:T(8,128)(2,1)S(1)}, u32[]{:S(2)}, u32[]{:S(2)}) collective-permute-start(bf16[32,2048]{1,0:T(8,128)(2,1)S(1)} %get-tuple-element.27.refs_0_), channel_id=1, source_target_pairs={{0,3},{1,0},{2,1},{3,2},{4,7},{5,4},{6,5},{7,6},{8,11},{9,8},{10,9... | collective-permute-start | bytes 393224 | tf_op jit(solution)/shard_map/ppermute | solution.py:303
  33.0 5.1 %shard_map.121 = (bf16[2048,1024]{1,0:T(8,128)(2,1)S(1)}, bf16[1024,2048]{1,0:T(8,128)(2,1)S(1)}, bf16[42,128,512]{2,1,0:T(8,128)(2,1)S(1)}) custom-call(bf16[32,2048]{1,0:T(8,128)(2,1)S(1)} %get-tuple-element.27.refs_0_, bf16[2048,1024]{1,0:T(8,128)(2,1)} %refs_1_.1, bf16[1024,2048]{1,0:T(8,128)(2,1)} %refs_2_.1, bf16[2,42,128,512]{3,2,1,0:T(8,128)(2,1)} %refs_3_.1), custom_call_target="tpu_custom_call" | custom-call | bytes 27787264 | tf_op jit(solution)/shard_map/pallas_call | solution.py:118
  38.1 0.0 collective-permute-done.2.refs_3_
  38.1 0.1 collective-permute-done.1.refs_2_
  38.2 0.0 collective-permute-done.refs_1_
  38.2 0.0 copy-done
  38.2 1.8 %shard_map.122 = (bf16[32,2048]{1,0:T(8,128)(2,1)S(1)}, bf16[32,2048]{1,0:T(8,128)(2,1)S(1)}) custom-call(bf16[32,2048]{1,0:T(8,128)(2,1)S(1)} %get-tuple-element.27.refs_0_, bf16[32,2048]{1,0:T(8,128)(2,1)S(1)} %collective-permute-done.refs_1_, bf16[32,2048]{1,0:T(8,128)(2,1)S(1)} %collective-permute-done.1.refs_2_, ...), custom_call_target="tpu_custom_call" | custom-call | tf_op jit(solution)/shard_map/pallas_call | solution.py:24
  40.0 0.0 copy-start.1
  40.0 0.8 collective-permute-start.5
  40.8 2.4 %collective-permute-start.4 = (bf16[32,2048]{1,0:T(8,128)(2,1)S(1)}, bf16[32,2048]{1,0:T(8,128)(2,1)S(1)}, u32[]{:S(2)}, u32[]{:S(2)}) collective-permute-start(bf16[32,2048]{1,0:T(8,128)(2,1)S(1)} %get-tuple-element.31.after_ref.refs_0_), channel_id=1, source_target_pairs={{0,2},{1,3},{2,0},{3,1},{4,6},{5,7},{6,4},{7,5},{8,10},{9,11},{10,... | collective-permute-start | bytes 393224 | tf_op jit(solution)/shard_map/ppermute | solution.py:303
  43.2 0.9 %collective-permute-start.3 = (bf16[32,2048]{1,0:T(8,128)(2,1)S(1)}, bf16[32,2048]{1,0:T(8,128)(2,1)S(1)}, u32[]{:S(2)}, u32[]{:S(2)}) collective-permute-start(bf16[32,2048]{1,0:T(8,128)(2,1)S(1)} %get-tuple-element.31.after_ref.refs_0_), channel_id=1, source_target_pairs={{0,3},{1,0},{2,1},{3,2},{4,7},{5,4},{6,5},{7,6},{8,11},{9,8},{10,9... | collective-permute-start | bytes 393224 | tf_op jit(solution)/shard_map/ppermute | solution.py:303
  44.2 3.2 %shard_map.123.refs_8_ = bf16[512,5376]{1,0:T(8,128)(2,1)S(1)} custom-call(bf16[32,2048]{1,0:T(8,128)(2,1)S(1)} %get-tuple-element.31.after_ref.refs_0_, bf16[2,42,128,512]{3,2,1,0:T(8,128)(2,1)} %k_hbm.3), custom_call_target="tpu_custom_call" | custom-call | bytes 11010048 | tf_op jit(solution)/shard_map/pallas_call | solution.py:154
  47.3 0.0 collective-permute-done.5.refs_3_
  47.3 1.0 %collective-permute-done.4.refs_2_ = bf16[32,2048]{1,0:T(8,128)(2,1)S(1)} collective-permute-done((bf16[32,2048]{1,0:T(8,128)(2,1)S(1)}, bf16[32,2048]{1,0:T(8,128)(2,1)S(1)}, u32[]{:S(2)}, u32[]{:S(2)}) %collective-permute-start.4) | collective-permute-done | bytes 131104 | tf_op jit(solution)/shard_map/ppermute | solution.py:303
  48.4 0.0 collective-permute-done.3.refs_1_
  48.4 0.0 copy-done.1
  48.4 4.0 %shard_map.124 = (bf16[32,2048]{1,0:T(8,128)(2,1)S(1)}, bf16[32,2048]{1,0:T(8,128)(2,1)S(1)}) custom-call(bf16[32,2048]{1,0:T(8,128)(2,1)S(1)} %get-tuple-element.31.after_ref.refs_0_, bf16[32,2048]{1,0:T(8,128)(2,1)S(1)} %collective-permute-done.3.refs_1_, bf16[32,2048]{1,0:T(8,128)(2,1)S(1)} %collective-permute-done.4.refs_2_, ...), custom_call_target="tpu_custom_call" | custom-call | tf_op jit(solution)/shard_map/pallas_call | solution.py:24
  52.4 2.5 %collective-permute-start.8 = (bf16[32,2048]{1,0:T(8,128)(2,1)S(1)}, bf16[32,2048]{1,0:T(8,128)(2,1)S(1)}, u32[]{:S(2)}, u32[]{:S(2)}) collective-permute-start(bf16[32,2048]{1,0:T(8,128)(2,1)S(1)} %get-tuple-element.35.refs_0_), channel_id=1, source_target_pairs={{0,1},{1,2},{2,3},{3,0},{4,5},{5,6},{6,7},{7,4},{8,9},{9,10},{10,1... | collective-permute-start | bytes 393224 | tf_op jit(solution)/shard_map/ppermute | solution.py:303
  54.9 1.7 %collective-permute-start.7 = (bf16[32,2048]{1,0:T(8,128)(2,1)S(1)}, bf16[32,2048]{1,0:T(8,128)(2,1)S(1)}, u32[]{:S(2)}, u32[]{:S(2)}) collective-permute-start(bf16[32,2048]{1,0:T(8,128)(2,1)S(1)} %get-tuple-element.35.refs_0_), channel_id=1, source_target_pairs={{0,2},{1,3},{2,0},{3,1},{4,6},{5,7},{6,4},{7,5},{8,10},{9,11},{10,... | collective-permute-start | bytes 393224 | tf_op jit(solution)/shard_map/ppermute | solution.py:303
  56.6 0.8 collective-permute-start.6
  57.4 0.4 collective-permute-done.8.refs_3_
  57.8 3.2 %collective-permute-done.7.refs_2_ = bf16[32,2048]{1,0:T(8,128)(2,1)S(1)} collective-permute-done((bf16[32,2048]{1,0:T(8,128)(2,1)S(1)}, bf16[32,2048]{1,0:T(8,128)(2,1)S(1)}, u32[]{:S(2)}, u32[]{:S(2)}) %collective-permute-start.7) | collective-permute-done | bytes 131104 | tf_op jit(solution)/shard_map/ppermute | solution.py:303
  61.0 0.6 collective-permute-done.6.refs_1_
  61.6 1.8 %shard_map.125 = (bf16[32,2048]{1,0:T(8,128)(2,1)S(1)}, bf16[32,2048]{1,0:T(8,128)(2,1)S(1)}) custom-call(bf16[32,2048]{1,0:T(8,128)(2,1)S(1)} %get-tuple-element.35.refs_0_, bf16[32,2048]{1,0:T(8,128)(2,1)S(1)} %collective-permute-done.6.refs_1_, bf16[32,2048]{1,0:T(8,128)(2,1)S(1)} %collective-permute-done.7.refs_2_, ...), custom_call_target="tpu_custom_call" | custom-call | tf_op jit(solution)/shard_map/pallas_call | solution.py:24
  63.4 0.4 collective-permute-start.11
  63.8 2.4 %collective-permute-start.10 = (bf16[32,2048]{1,0:T(8,128)(2,1)S(1)}, bf16[32,2048]{1,0:T(8,128)(2,1)S(1)}, u32[]{:S(2)}, u32[]{:S(2)}) collective-permute-start(bf16[32,2048]{1,0:T(8,128)(2,1)S(1)} %get-tuple-element.37.refs_0_), channel_id=1, source_target_pairs={{0,2},{1,3},{2,0},{3,1},{4,6},{5,7},{6,4},{7,5},{8,10},{9,11},{10,... | collective-permute-start | bytes 393224 | tf_op jit(solution)/shard_map/ppermute | solution.py:303
  66.2 1.4 %collective-permute-start.9 = (bf16[32,2048]{1,0:T(8,128)(2,1)S(1)}, bf16[32,2048]{1,0:T(8,128)(2,1)S(1)}, u32[]{:S(2)}, u32[]{:S(2)}) collective-permute-start(bf16[32,2048]{1,0:T(8,128)(2,1)S(1)} %get-tuple-element.37.refs_0_), channel_id=1, source_target_pairs={{0,3},{1,0},{2,1},{3,2},{4,7},{5,4},{6,5},{7,6},{8,11},{9,8},{10,9... | collective-permute-start | bytes 393224 | tf_op jit(solution)/shard_map/ppermute | solution.py:303
  67.5 0.9 %collective-permute-done.11.refs_3_ = bf16[32,2048]{1,0:T(8,128)(2,1)S(1)} collective-permute-done((bf16[32,2048]{1,0:T(8,128)(2,1)S(1)}, bf16[32,2048]{1,0:T(8,128)(2,1)S(1)}, u32[]{:S(2)}, u32[]{:S(2)}) %collective-permute-start.11) | collective-permute-done | bytes 131104 | tf_op jit(solution)/shard_map/ppermute | solution.py:303
  68.4 1.5 %collective-permute-done.10.refs_2_ = bf16[32,2048]{1,0:T(8,128)(2,1)S(1)} collective-permute-done((bf16[32,2048]{1,0:T(8,128)(2,1)S(1)}, bf16[32,2048]{1,0:T(8,128)(2,1)S(1)}, u32[]{:S(2)}, u32[]{:S(2)}) %collective-permute-start.10) | collective-permute-done | bytes 131104 | tf_op jit(solution)/shard_map/ppermute | solution.py:303
  69.9 0.8 collective-permute-done.9.refs_1_
  70.7 0.5 shard_map.126
  71.2 16.2 %all_to_all.10 = bf16[32,8,512]{2,1,0:T(8,128)(2,1)S(1)} all-to-all(bf16[32,8,512]{2,1,0:T(8,128)(2,1)S(1)} %bitcast.10), channel_id=1, replica_groups=mesh['req'=32,'tp'=4] {'req'}, dimensions={0} | all-to-all | bytes 524288 | tf_op jit(solution)/shard_map/all_to_all | solution.py:431
  87.4 0.8 shard_map.127
Async XLA Ops:
  2.0 18.4 %all-to-all-start = ((bf16[32,8,512]{2,1,0:T(8,128)(2,1)}), bf16[32,8,512]{2,1,0:T(8,128)(2,1)S(1)}, u32[]{:S(2)}, u32[]{:S(2)}) async-start(bf16[32,8,512]{2,1,0:T(8,128)(2,1)} %bitcast.1), calls=%async_computation | async-start | bytes 524288 | tf_op jit(solution)/shard_map/all_to_all | solution.py:431
  11.5 0.7 copy-start.2
  12.2 0.7 copy-start.3
  12.9 0.7 copy-start.4
  28.0 10.3 %copy-start = (f32[2,2048]{1,0:T(2,128)S(1)}, f32[2,2048]{1,0:T(2,128)}, u32[]{:S(2)}) copy-start(f32[2,2048]{1,0:T(2,128)} %refs_5_.6) | copy-start | bytes 49156
  28.0 10.1 %collective-permute-start.2 = (bf16[32,2048]{1,0:T(8,128)(2,1)S(1)}, bf16[32,2048]{1,0:T(8,128)(2,1)S(1)}, u32[]{:S(2)}, u32[]{:S(2)}) collective-permute-start(bf16[32,2048]{1,0:T(8,128)(2,1)S(1)} %get-tuple-element.27.refs_0_), channel_id=1, source_target_pairs={{0,1},{1,2},{2,3},{3,0},{4,5},{5,6},{6,7},{7,4},{8,9},{9,10},{10,1... | collective-permute-start | bytes 393224 | tf_op jit(solution)/shard_map/ppermute | solution.py:303
  29.3 8.9 %collective-permute-start.1 = (bf16[32,2048]{1,0:T(8,128)(2,1)S(1)}, bf16[32,2048]{1,0:T(8,128)(2,1)S(1)}, u32[]{:S(2)}, u32[]{:S(2)}) collective-permute-start(bf16[32,2048]{1,0:T(8,128)(2,1)S(1)} %get-tuple-element.27.refs_0_), channel_id=1, source_target_pairs={{0,2},{1,3},{2,0},{3,1},{4,6},{5,7},{6,4},{7,5},{8,10},{9,11},{10,... | collective-permute-start | bytes 393224 | tf_op jit(solution)/shard_map/ppermute | solution.py:303
  32.0 6.3 %collective-permute-start = (bf16[32,2048]{1,0:T(8,128)(2,1)S(1)}, bf16[32,2048]{1,0:T(8,128)(2,1)S(1)}, u32[]{:S(2)}, u32[]{:S(2)}) collective-permute-start(bf16[32,2048]{1,0:T(8,128)(2,1)S(1)} %get-tuple-element.27.refs_0_), channel_id=1, source_target_pairs={{0,3},{1,0},{2,1},{3,2},{4,7},{5,4},{6,5},{7,6},{8,11},{9,8},{10,9... | collective-permute-start | bytes 393224 | tf_op jit(solution)/shard_map/ppermute | solution.py:303
  40.0 8.3 %copy-start.1 = (f32[2,2048]{1,0:T(2,128)S(1)}, f32[2,2048]{1,0:T(2,128)}, u32[]{:S(2)}) copy-start(f32[2,2048]{1,0:T(2,128)} %refs_5_.7) | copy-start | bytes 49156
  40.0 7.3 %collective-permute-start.5 = (bf16[32,2048]{1,0:T(8,128)(2,1)S(1)}, bf16[32,2048]{1,0:T(8,128)(2,1)S(1)}, u32[]{:S(2)}, u32[]{:S(2)}) collective-permute-start(bf16[32,2048]{1,0:T(8,128)(2,1)S(1)} %get-tuple-element.31.after_ref.refs_0_), channel_id=1, source_target_pairs={{0,1},{1,2},{2,3},{3,0},{4,5},{5,6},{6,7},{7,4},{8,9},{9,10},{10,1... | collective-permute-start | bytes 393224 | tf_op jit(solution)/shard_map/ppermute | solution.py:303
  40.8 7.5 %collective-permute-start.4 = (bf16[32,2048]{1,0:T(8,128)(2,1)S(1)}, bf16[32,2048]{1,0:T(8,128)(2,1)S(1)}, u32[]{:S(2)}, u32[]{:S(2)}) collective-permute-start(bf16[32,2048]{1,0:T(8,128)(2,1)S(1)} %get-tuple-element.31.after_ref.refs_0_), channel_id=1, source_target_pairs={{0,2},{1,3},{2,0},{3,1},{4,6},{5,7},{6,4},{7,5},{8,10},{9,11},{10,... | collective-permute-start | bytes 393224 | tf_op jit(solution)/shard_map/ppermute | solution.py:303
  43.2 5.1 %collective-permute-start.3 = (bf16[32,2048]{1,0:T(8,128)(2,1)S(1)}, bf16[32,2048]{1,0:T(8,128)(2,1)S(1)}, u32[]{:S(2)}, u32[]{:S(2)}) collective-permute-start(bf16[32,2048]{1,0:T(8,128)(2,1)S(1)} %get-tuple-element.31.after_ref.refs_0_), channel_id=1, source_target_pairs={{0,3},{1,0},{2,1},{3,2},{4,7},{5,4},{6,5},{7,6},{8,11},{9,8},{10,9... | collective-permute-start | bytes 393224 | tf_op jit(solution)/shard_map/ppermute | solution.py:303
  52.4 5.4 %collective-permute-start.8 = (bf16[32,2048]{1,0:T(8,128)(2,1)S(1)}, bf16[32,2048]{1,0:T(8,128)(2,1)S(1)}, u32[]{:S(2)}, u32[]{:S(2)}) collective-permute-start(bf16[32,2048]{1,0:T(8,128)(2,1)S(1)} %get-tuple-element.35.refs_0_), channel_id=1, source_target_pairs={{0,1},{1,2},{2,3},{3,0},{4,5},{5,6},{6,7},{7,4},{8,9},{9,10},{10,1... | collective-permute-start | bytes 393224 | tf_op jit(solution)/shard_map/ppermute | solution.py:303
  54.9 6.1 %collective-permute-start.7 = (bf16[32,2048]{1,0:T(8,128)(2,1)S(1)}, bf16[32,2048]{1,0:T(8,128)(2,1)S(1)}, u32[]{:S(2)}, u32[]{:S(2)}) collective-permute-start(bf16[32,2048]{1,0:T(8,128)(2,1)S(1)} %get-tuple-element.35.refs_0_), channel_id=1, source_target_pairs={{0,2},{1,3},{2,0},{3,1},{4,6},{5,7},{6,4},{7,5},{8,10},{9,11},{10,... | collective-permute-start | bytes 393224 | tf_op jit(solution)/shard_map/ppermute | solution.py:303
  56.6 5.0 %collective-permute-start.6 = (bf16[32,2048]{1,0:T(8,128)(2,1)S(1)}, bf16[32,2048]{1,0:T(8,128)(2,1)S(1)}, u32[]{:S(2)}, u32[]{:S(2)}) collective-permute-start(bf16[32,2048]{1,0:T(8,128)(2,1)S(1)} %get-tuple-element.35.refs_0_), channel_id=1, source_target_pairs={{0,3},{1,0},{2,1},{3,2},{4,7},{5,4},{6,5},{7,6},{8,11},{9,8},{10,9... | collective-permute-start | bytes 393224 | tf_op jit(solution)/shard_map/ppermute | solution.py:303
  63.4 5.0 %collective-permute-start.11 = (bf16[32,2048]{1,0:T(8,128)(2,1)S(1)}, bf16[32,2048]{1,0:T(8,128)(2,1)S(1)}, u32[]{:S(2)}, u32[]{:S(2)}) collective-permute-start(bf16[32,2048]{1,0:T(8,128)(2,1)S(1)} %get-tuple-element.37.refs_0_), channel_id=1, source_target_pairs={{0,1},{1,2},{2,3},{3,0},{4,5},{5,6},{6,7},{7,4},{8,9},{9,10},{10,1... | collective-permute-start | bytes 393224 | tf_op jit(solution)/shard_map/ppermute | solution.py:303
  63.8 6.1 %collective-permute-start.10 = (bf16[32,2048]{1,0:T(8,128)(2,1)S(1)}, bf16[32,2048]{1,0:T(8,128)(2,1)S(1)}, u32[]{:S(2)}, u32[]{:S(2)}) collective-permute-start(bf16[32,2048]{1,0:T(8,128)(2,1)S(1)} %get-tuple-element.37.refs_0_), channel_id=1, source_target_pairs={{0,2},{1,3},{2,0},{3,1},{4,6},{5,7},{6,4},{7,5},{8,10},{9,11},{10,... | collective-permute-start | bytes 393224 | tf_op jit(solution)/shard_map/ppermute | solution.py:303
  66.2 4.5 %collective-permute-start.9 = (bf16[32,2048]{1,0:T(8,128)(2,1)S(1)}, bf16[32,2048]{1,0:T(8,128)(2,1)S(1)}, u32[]{:S(2)}, u32[]{:S(2)}) collective-permute-start(bf16[32,2048]{1,0:T(8,128)(2,1)S(1)} %get-tuple-element.37.refs_0_), channel_id=1, source_target_pairs={{0,3},{1,0},{2,1},{3,2},{4,7},{5,4},{6,5},{7,6},{8,11},{9,8},{10,9... | collective-permute-start | bytes 393224 | tf_op jit(solution)/shard_map/ppermute | solution.py:303

commit v8 on v7

--- a/solution.py
+++ b/solution.py
@@ -46,10 +46,9 @@
     return (centered * lax.rsqrt(row_var + EPS) * gain_bias[0:1, :] + gain_bias[1:2, :]).astype(BF)
 
 
-def attend(x, wait, project, share, score, v_ref, w_out, bias, s_ref, step):
+def attend(x, wait, project, share, score, pages, page_len, value, w_out, bias, s_ref, step):
     rows = x.shape[0]
     heads = share // HD
-    pages, page_len = v_ref.shape[:2]
     span = step * page_len
     scale = math.log2(math.e) / math.sqrt(HD)
     query, fresh_key, fresh_value = (project(x, i).astype(BF) for i in range(3))
@@ -76,7 +75,7 @@
         for i in range(span // HD):
             sums = sums + weight[:, i * HD : (i + 1) * HD]
         wait("value", c * step)
-        values = v_ref[c * step : (c + 1) * step].reshape(span, share)
+        values = value(c * step, step).reshape(span, share)
         mixed = mixed + jnp.dot(weight.astype(BF), values, preferred_element_type=F32)
     own_weight = jnp.exp2((own - peak) * scale)
     total = jnp.sum(sums, axis=-1, keepdims=True) + own_weight
@@ -105,16 +104,16 @@
     def body(*refs):
         copies = [
             pltpu.make_async_copy(
-                refs[1 + i] if layer is None else refs[1 + i].at[layer], refs[1 + count + i], refs[-1].at[i]
+                refs[1 + i] if at is None else refs[1 + i].at[at[0], pl.ds(0, at[1])], refs[1 + count + i], refs[-1].at[i]
             )
-            for i, (_, layer) in enumerate(sources)
+            for i, (_, at) in enumerate(sources)
         ]
         for copy in copies:
             copy.start()
         for copy in copies:
             copy.wait()
 
-    shapes = [a.shape if layer is None else a.shape[1:] for a, layer in sources]
+    shapes = [a.shape if at is None else (at[1], *a.shape[2:]) for a, at in sources]
     return pl.pallas_call(
         body,
         out_shape=tuple(pltpu.VMEM(shape, BF) for shape in shapes),
@@ -131,13 +130,14 @@
     return pl.CostEstimate(flops=0, transcendentals=0, bytes_accessed=2 * size)
 
 
-def load_turned(after, key_cache, layer):
+def load_turned(after, key_cache, value_cache, layer, cut):
     pages, page_len, share = key_cache.shape[1:]
     step = math.gcd(pages, 14)
     parts = pages // step
     span = step * page_len
 
-    def body(after_ref, k_hbm, out_ref, k_ref, sems):
+    def body(after_ref, k_hbm, v_hbm, out_ref, late_ref, k_ref, sems):
+        late = pltpu.make_async_copy(v_hbm.at[layer, pl.ds(cut, pages - cut)], late_ref, sems.at[parts])
         copies = [
             pltpu.make_async_copy(k_hbm.at[layer, pl.ds(c * step, step)], k_ref.at[pl.ds(c * step, step)], sems.at[c])
             for c in range(parts)
@@ -148,18 +148,21 @@
             copies[c].wait()
             if c + 3 < parts:
                 copies[c + 3].start()
+            if c == 0:
+                late.start()
             keys = k_ref[c * step : (c + 1) * step].reshape(span, share)
             out_ref[:, c * span : (c + 1) * span] = jnp.transpose(keys)
+        late.wait()
 
     return pl.pallas_call(
         body,
-        out_shape=pltpu.VMEM((share, pages * page_len), BF),
-        in_specs=[HBM_SPEC] * 2,
-        out_specs=VMEM_SPEC,
-        scratch_shapes=[pltpu.VMEM((pages, page_len, share), BF), pltpu.SemaphoreType.DMA((parts,))],
+        out_shape=(pltpu.VMEM((share, pages * page_len), BF), pltpu.VMEM((pages - cut, page_len, share), BF)),
+        in_specs=[HBM_SPEC] * 3,
+        out_specs=(VMEM_SPEC,) * 2,
+        scratch_shapes=[pltpu.VMEM((pages, page_len, share), BF), pltpu.SemaphoreType.DMA((parts + 1,))],
         compiler_params=pltpu.CompilerParams(vmem_limit_bytes=10 * MIB),
         cost_estimate=load_cost([key_cache.shape[1:]]),
-    )(after, in_place(key_cache))
+    )(after, in_place(key_cache), in_place(value_cache))
 
 
 def first_attention(incoming, take, w_qkv, w_out, key_cache, value_cache, bias):
@@ -216,7 +219,12 @@
         stacked = jnp.dot(take_ref[...], in_ref[...], preferred_element_type=F32).astype(BF)
         x = jnp.concatenate([stacked[c * rows : (c + 1) * rows] for c in range(cols)], axis=1)
         x_ref[...] = x
-        out_ref[...] = attend(x, wait, project, share, score, v_ref, wo_ref, b_ref, s_ref, math.gcd(step, STEP))
+        def value(first, count):
+            return v_ref[first : first + count]
+
+        out_ref[...] = attend(
+            x, wait, project, share, score, pages, page_len, value, wo_ref, b_ref, s_ref, math.gcd(step, STEP)
+        )
 
     shape = jax.ShapeDtypeStruct((rows, share * cols), BF)
     return pl.pallas_call(
@@ -236,13 +244,15 @@
     )(incoming, take, bias, w_out, *map(in_place, (w_qkv, key_cache, value_cache)))
 
 
-def norm_attention(parts, residual, gain_bias, w_qkv, w_out, keys, values, bias):
+def norm_attention(parts, residual, gain_bias, w_qkv, w_out, keys, early, late, bias):
     count = len(parts)
-    step = math.gcd(values.shape[0], 6)
+    cut, page_len, share = early.shape
+    pages = cut + late.shape[0]
+    step = math.gcd(cut, late.shape[0])
 
     def body(*refs):
-        part_refs, (res_ref, norm_ref, wq_ref, wo_ref, k_ref, v_ref, b_ref) = refs[:count], refs[count : count + 7]
-        x_ref, out_ref, s_ref = refs[count + 7 :]
+        part_refs, (res_ref, norm_ref, wq_ref, wo_ref, k_ref, v0_ref, v1_ref, b_ref) = refs[:count], refs[count : count + 8]
+        x_ref, out_ref, s_ref = refs[count + 8 :]
         x = add_norm([r[...] for r in part_refs], res_ref[...], norm_ref[...])
         x_ref[...] = x
 
@@ -252,12 +262,19 @@
         def project(x, i):
             return jnp.dot(x, wq_ref[i], preferred_element_type=F32)
 
-        out_ref[...] = attend(x, lambda *key: None, project, wq_ref.shape[2], score, v_ref, wo_ref, b_ref, s_ref, step)
+        def value(first, number):
+            if first < cut:
+                return v0_ref[first : first + number]
+            return v1_ref[first - cut : first - cut + number]
+
+        out_ref[...] = attend(
+            x, lambda *key: None, project, share, score, pages, page_len, value, wo_ref, b_ref, s_ref, step
+        )
 
     shape = jax.ShapeDtypeStruct(residual.shape, BF)
-    scratch = [score_scratch(residual.shape[0], *values.shape)]
+    scratch = [score_scratch(residual.shape[0], pages, page_len, share)]
     return kernel_call(
-        body, (shape, shape), scratch, 12, *parts, residual, gain_bias, w_qkv, w_out, keys, values, bias
+        body, (shape, shape), scratch, 12, *parts, residual, gain_bias, w_qkv, w_out, keys, early, late, bias
     )
 
 
@@ -457,16 +474,17 @@
     )
     w_qkv = jnp.transpose(qkv_weight, (1, 0, 2))
     current, partial, w_qkv = first_attention(incoming, take, w_qkv, w_out, key_cache, value_cache, bias)
-    w_up, w_down, values = load(partial, (up_weight, None), (down_weight, None), (value_cache, 1))
+    cut = pool_pages * 4 // 7
+    w_up, w_down, early = load(partial, (up_weight, None), (down_weight, None), (value_cache, (1, cut)))
     for layer in range(layers):
         hidden, partial = norm_mlp(gather_parts(partial), current, attn_norm, w_up, w_down)
         if layer + 1 < layers:
-            keys = load_turned(partial, key_cache, layer + 1)
+            keys, late = load_turned(partial, key_cache, value_cache, layer + 1, cut)
             current, partial = norm_attention(
-                gather_parts(partial), hidden, mlp_norm, w_qkv, w_out, keys, values, bias
+                gather_parts(partial), hidden, mlp_norm, w_qkv, w_out, keys, early, late, bias
             )
             if layer + 2 < layers:
-                (values,) = load(partial, (value_cache, layer + 2))
+                (early,) = load(partial, (value_cache, (layer + 2, cut)))
     leaving = norm_send(gather_parts(partial), hidden, mlp_norm, send)
     return settle(swap(leaving, blocks), back, req_rows)
 

time: 88.6 us -> 88.6 us (level)
  no operation moved by 1% of the time
where the time goes in v8:
time: 88.6 us; the launch traced here: 88.3 us
  Pallas kernels  28 us (32%)
  starting transfers between devices  27.8 us (31%)
  blocking collectives  16.3 us (18%)
  waiting for transfers between devices  14 us (16%)
  local copies, waits for them, and re-layouts  2.04 us (2%)
    ppermute x12, starting transfers between devices, gather_parts(): lax.ppermute(part, 'tp', [(i, (i + step) % size) for i in range(size)])  18.3 us
    all_to_all x1, blocking collectives, swap(): lax.all_to_all(lines_out.reshape(blocks, lines // blocks, share), 'req',...  16.3 us
    all_to_all x1, starting transfers between devices, swap(): lax.all_to_all(lines_out.reshape(blocks, lines // blocks, share), 'req',...  9.45 us
    pallas_call x5, Pallas kernels, kernel_call(): pl.pallas_call(body, out_shape=out_shape, in_specs=[VMEM_SPEC] * len(oper...  8.92 us
    ppermute x12, waiting for transfers between devices, gather_parts(): lax.ppermute(part, 'tp', [(i, (i + step) % size) for i in range(size)])  8.69 us
    pallas_call x1, Pallas kernels, first_attention(): pl.pallas_call(body, out_shape=(shape, shape, pltpu.VMEM(w_qkv.shape, BF)...  7.49 us
    all_to_all x1, waiting for transfers between devices, swap(): lax.all_to_all(lines_out.reshape(blocks, lines // blocks, share), 'req',...  5.35 us
    pallas_call x1, Pallas kernels, load(): pl.pallas_call(body, out_shape=tuple((pltpu.VMEM(shape, BF) for shape in...  4.39 us
  transfers between devices with their start and end apart: 13, of which 9 were waited for; matrix products, arithmetic and copies ran while one was open for 0% of the time, Pallas kernels for 11%

profile of v8, /device:TPU:1, one launch (start us, length us, event | category | flops | bytes accessed | tf_op | source)
XLA Modules:
  0.0 88.3 jit_solution(16522804772334998322)
XLA Ops:
  0.0 2.0 %shard_map.118 = (bf16[256,512]{1,0:T(8,128)(2,1)}, bf16[128,256]{1,0:T(8,128)(2,1)S(1)}) custom-call(s32[8,128]{1,0:T(8,128)} %bitcast.11, bf16[32,2048]{1,0:T(8,128)(2,1)} %tok_hbm.1), custom_call_target="tpu_custom_call" | custom-call | tf_op jit(solution)/shard_map/pallas_call | solution.py:360
  2.0 9.4 %all-to-all-start = ((bf16[32,8,512]{2,1,0:T(8,128)(2,1)}), bf16[32,8,512]{2,1,0:T(8,128)(2,1)S(1)}, u32[]{:S(2)}, u32[]{:S(2)}) async-start(bf16[32,8,512]{2,1,0:T(8,128)(2,1)} %bitcast.1), calls=%async_computation | async-start | bytes 524288 | tf_op jit(solution)/shard_map/all_to_all | solution.py:448
  11.5 0.0 copy-start.2
  11.5 0.7 copy-done.2
  12.2 0.0 copy-start.3
  12.2 0.7 copy-done.3
  12.9 0.0 copy-start.4
  12.9 0.7 copy-done.4
  13.5 1.6 %shard_map.119 = (bf16[128,256]{1,0:T(8,128)(2,1)S(1)}, bf16[256,128]{1,0:T(8,128)(2,1)S(1)}, f32[32,5376]{1,0:T(8,128)S(1)}, bf16[512,2048]{1,0:T(8,128)(2,1)S(1)}) custom-call(s32[8,128]{1,0:T(8,128)S(1)} %bitcast.12, s32[6,32]{1,0:T(8,128)S(1)} %bitcast.13, s32[1,32]{1,0:T(1,128)S(1)} %bitcast.14, bf16[512,2048]{1,0:T(8,128)(2,1)} %wo_hbm.1), custom_call_target="tpu_custom_call" | custom-call | tf_op jit(solution)/shard_map/pallas_call | solution.py:425
  15.1 5.3 %all-to-all-done = bf16[32,8,512]{2,1,0:T(8,128)(2,1)S(1)} async-done(((bf16[32,8,512]{2,1,0:T(8,128)(2,1)}), bf16[32,8,512]{2,1,0:T(8,128)(2,1)S(1)}, u32[]{:S(2)}, u32[]{:S(2)}) %all-to-all-start) | async-done | bytes 262176 | tf_op jit(solution)/shard_map/all_to_all | solution.py:448
  20.5 7.5 %shard_map.120 = (bf16[32,2048]{1,0:T(8,128)(2,1)S(1)}, bf16[32,2048]{1,0:T(8,128)(2,1)S(1)}, bf16[3,2048,512]{2,1,0:T(8,128)(2,1)S(1)}) custom-call(bf16[256,512]{1,0:T(8,128)(2,1)S(1)} %bitcast.8, bf16[128,256]{1,0:T(8,128)(2,1)S(1)} %get-tuple-element.26.take_ref, f32[32,5376]{1,0:T(8,128)S(1)} %get-tuple-element.27.b_ref.refs_11_, ...), custom_call_target="tpu_custom_call" | custom-call | tf_op jit(solution)/shard_map/pallas_call | solution.py:230
  28.0 0.0 copy-start
  28.0 1.4 %collective-permute-start.2 = (bf16[32,2048]{1,0:T(8,128)(2,1)S(1)}, bf16[32,2048]{1,0:T(8,128)(2,1)S(1)}, u32[]{:S(2)}, u32[]{:S(2)}) collective-permute-start(bf16[32,2048]{1,0:T(8,128)(2,1)S(1)} %get-tuple-element.29.refs_0_), channel_id=1, source_target_pairs={{0,1},{1,2},{2,3},{3,0},{4,5},{5,6},{6,7},{7,4},{8,9},{9,10},{10,1... | collective-permute-start | bytes 393224 | tf_op jit(solution)/shard_map/ppermute | solution.py:320
  29.3 2.6 %collective-permute-start.1 = (bf16[32,2048]{1,0:T(8,128)(2,1)S(1)}, bf16[32,2048]{1,0:T(8,128)(2,1)S(1)}, u32[]{:S(2)}, u32[]{:S(2)}) collective-permute-start(bf16[32,2048]{1,0:T(8,128)(2,1)S(1)} %get-tuple-element.29.refs_0_), channel_id=1, source_target_pairs={{0,2},{1,3},{2,0},{3,1},{4,6},{5,7},{6,4},{7,5},{8,10},{9,11},{10,... | collective-permute-start | bytes 393224 | tf_op jit(solution)/shard_map/ppermute | solution.py:320
  32.0 1.1 %collective-permute-start = (bf16[32,2048]{1,0:T(8,128)(2,1)S(1)}, bf16[32,2048]{1,0:T(8,128)(2,1)S(1)}, u32[]{:S(2)}, u32[]{:S(2)}) collective-permute-start(bf16[32,2048]{1,0:T(8,128)(2,1)S(1)} %get-tuple-element.29.refs_0_), channel_id=1, source_target_pairs={{0,3},{1,0},{2,1},{3,2},{4,7},{5,4},{6,5},{7,6},{8,11},{9,8},{10,9... | collective-permute-start | bytes 393224 | tf_op jit(solution)/shard_map/ppermute | solution.py:320
  33.0 4.4 %shard_map.121 = (bf16[2048,1024]{1,0:T(8,128)(2,1)S(1)}, bf16[1024,2048]{1,0:T(8,128)(2,1)S(1)}, bf16[24,128,512]{2,1,0:T(8,128)(2,1)S(1)}) custom-call(bf16[32,2048]{1,0:T(8,128)(2,1)S(1)} %get-tuple-element.29.refs_0_, bf16[2048,1024]{1,0:T(8,128)(2,1)} %refs_1_.1, bf16[1024,2048]{1,0:T(8,128)(2,1)} %refs_2_.1, bf16[2,42,128,512]{3,2,1,0:T(8,128)(2,1)} %v_hbm.3), custom_call_target="tpu_custom_call" | custom-call | bytes 23068672 | tf_op jit(solution)/shard_map/pallas_call | solution.py:117
  37.4 0.0 collective-permute-done.2.refs_3_
  37.4 0.8 collective-permute-done.1.refs_2_
  38.2 0.0 collective-permute-done.refs_1_
  38.2 0.0 copy-done
  38.2 1.8 %shard_map.122 = (bf16[32,2048]{1,0:T(8,128)(2,1)S(1)}, bf16[32,2048]{1,0:T(8,128)(2,1)S(1)}) custom-call(bf16[32,2048]{1,0:T(8,128)(2,1)S(1)} %get-tuple-element.29.refs_0_, bf16[32,2048]{1,0:T(8,128)(2,1)S(1)} %collective-permute-done.refs_1_, bf16[32,2048]{1,0:T(8,128)(2,1)S(1)} %collective-permute-done.1.refs_2_, ...), custom_call_target="tpu_custom_call" | custom-call | tf_op jit(solution)/shard_map/pallas_call | solution.py:24
  40.0 0.0 copy-start.1
  40.0 0.8 collective-permute-start.5
  40.8 2.4 %collective-permute-start.4 = (bf16[32,2048]{1,0:T(8,128)(2,1)S(1)}, bf16[32,2048]{1,0:T(8,128)(2,1)S(1)}, u32[]{:S(2)}, u32[]{:S(2)}) collective-permute-start(bf16[32,2048]{1,0:T(8,128)(2,1)S(1)} %get-tuple-element.33.after_ref.refs_0_), channel_id=1, source_target_pairs={{0,2},{1,3},{2,0},{3,1},{4,6},{5,7},{6,4},{7,5},{8,10},{9,11},{10,... | collective-permute-start | bytes 393224 | tf_op jit(solution)/shard_map/ppermute | solution.py:320
  43.2 0.9 %collective-permute-start.3 = (bf16[32,2048]{1,0:T(8,128)(2,1)S(1)}, bf16[32,2048]{1,0:T(8,128)(2,1)S(1)}, u32[]{:S(2)}, u32[]{:S(2)}) collective-permute-start(bf16[32,2048]{1,0:T(8,128)(2,1)S(1)} %get-tuple-element.33.after_ref.refs_0_), channel_id=1, source_target_pairs={{0,3},{1,0},{2,1},{3,2},{4,7},{5,4},{6,5},{7,6},{8,11},{9,8},{10,9... | collective-permute-start | bytes 393224 | tf_op jit(solution)/shard_map/ppermute | solution.py:320
  44.1 3.6 %shard_map.123 = (bf16[512,5376]{1,0:T(8,128)(2,1)S(1)}, bf16[18,128,512]{2,1,0:T(8,128)(2,1)S(1)}) custom-call(bf16[32,2048]{1,0:T(8,128)(2,1)S(1)} %get-tuple-element.33.after_ref.refs_0_, bf16[2,42,128,512]{3,2,1,0:T(8,128)(2,1)} %k_hbm.3, bf16[2,42,128,512]{3,2,1,0:T(8,128)(2,1)} %v_hbm.3), custom_call_target="tpu_custom_call" | custom-call | bytes 11010048 | tf_op jit(solution)/shard_map/pallas_call | solution.py:157
  47.7 0.0 collective-permute-done.5.refs_3_
  47.7 0.6 collective-permute-done.4.refs_2_
  48.3 0.0 collective-permute-done.3.refs_1_
  48.3 0.0 copy-done.1
  48.3 4.0 %shard_map.124 = (bf16[32,2048]{1,0:T(8,128)(2,1)S(1)}, bf16[32,2048]{1,0:T(8,128)(2,1)S(1)}) custom-call(bf16[32,2048]{1,0:T(8,128)(2,1)S(1)} %get-tuple-element.33.after_ref.refs_0_, bf16[32,2048]{1,0:T(8,128)(2,1)S(1)} %collective-permute-done.3.refs_1_, bf16[32,2048]{1,0:T(8,128)(2,1)S(1)} %collective-permute-done.4.refs_2_, ...), custom_call_target="tpu_custom_call" | custom-call | tf_op jit(solution)/shard_map/pallas_call | solution.py:24
  52.4 2.5 %collective-permute-start.8 = (bf16[32,2048]{1,0:T(8,128)(2,1)S(1)}, bf16[32,2048]{1,0:T(8,128)(2,1)S(1)}, u32[]{:S(2)}, u32[]{:S(2)}) collective-permute-start(bf16[32,2048]{1,0:T(8,128)(2,1)S(1)} %get-tuple-element.39.refs_0_), channel_id=1, source_target_pairs={{0,1},{1,2},{2,3},{3,0},{4,5},{5,6},{6,7},{7,4},{8,9},{9,10},{10,1... | collective-permute-start | bytes 393224 | tf_op jit(solution)/shard_map/ppermute | solution.py:320
  54.9 1.7 %collective-permute-start.7 = (bf16[32,2048]{1,0:T(8,128)(2,1)S(1)}, bf16[32,2048]{1,0:T(8,128)(2,1)S(1)}, u32[]{:S(2)}, u32[]{:S(2)}) collective-permute-start(bf16[32,2048]{1,0:T(8,128)(2,1)S(1)} %get-tuple-element.39.refs_0_), channel_id=1, source_target_pairs={{0,2},{1,3},{2,0},{3,1},{4,6},{5,7},{6,4},{7,5},{8,10},{9,11},{10,... | collective-permute-start | bytes 393224 | tf_op jit(solution)/shard_map/ppermute | solution.py:320
  56.6 0.8 collective-permute-start.6
  57.3 0.4 collective-permute-done.8.refs_3_
  57.7 3.2 %collective-permute-done.7.refs_2_ = bf16[32,2048]{1,0:T(8,128)(2,1)S(1)} collective-permute-done((bf16[32,2048]{1,0:T(8,128)(2,1)S(1)}, bf16[32,2048]{1,0:T(8,128)(2,1)S(1)}, u32[]{:S(2)}, u32[]{:S(2)}) %collective-permute-start.7) | collective-permute-done | bytes 131104 | tf_op jit(solution)/shard_map/ppermute | solution.py:320
  60.9 0.6 collective-permute-done.6.refs_1_
  61.5 1.8 %shard_map.125 = (bf16[32,2048]{1,0:T(8,128)(2,1)S(1)}, bf16[32,2048]{1,0:T(8,128)(2,1)S(1)}) custom-call(bf16[32,2048]{1,0:T(8,128)(2,1)S(1)} %get-tuple-element.39.refs_0_, bf16[32,2048]{1,0:T(8,128)(2,1)S(1)} %collective-permute-done.6.refs_1_, bf16[32,2048]{1,0:T(8,128)(2,1)S(1)} %collective-permute-done.7.refs_2_, ...), custom_call_target="tpu_custom_call" | custom-call | tf_op jit(solution)/shard_map/pallas_call | solution.py:24
  63.3 0.3 collective-permute-start.11
  63.6 2.5 %collective-permute-start.10 = (bf16[32,2048]{1,0:T(8,128)(2,1)S(1)}, bf16[32,2048]{1,0:T(8,128)(2,1)S(1)}, u32[]{:S(2)}, u32[]{:S(2)}) collective-permute-start(bf16[32,2048]{1,0:T(8,128)(2,1)S(1)} %get-tuple-element.41.refs_0_), channel_id=1, source_target_pairs={{0,2},{1,3},{2,0},{3,1},{4,6},{5,7},{6,4},{7,5},{8,10},{9,11},{10,... | collective-permute-start | bytes 393224 | tf_op jit(solution)/shard_map/ppermute | solution.py:320
  66.1 1.4 %collective-permute-start.9 = (bf16[32,2048]{1,0:T(8,128)(2,1)S(1)}, bf16[32,2048]{1,0:T(8,128)(2,1)S(1)}, u32[]{:S(2)}, u32[]{:S(2)}) collective-permute-start(bf16[32,2048]{1,0:T(8,128)(2,1)S(1)} %get-tuple-element.41.refs_0_), channel_id=1, source_target_pairs={{0,3},{1,0},{2,1},{3,2},{4,7},{5,4},{6,5},{7,6},{8,11},{9,8},{10,9... | collective-permute-start | bytes 393224 | tf_op jit(solution)/shard_map/ppermute | solution.py:320
  67.5 0.9 collective-permute-done.11.refs_3_
  68.3 1.5 %collective-permute-done.10.refs_2_ = bf16[32,2048]{1,0:T(8,128)(2,1)S(1)} collective-permute-done((bf16[32,2048]{1,0:T(8,128)(2,1)S(1)}, bf16[32,2048]{1,0:T(8,128)(2,1)S(1)}, u32[]{:S(2)}, u32[]{:S(2)}) %collective-permute-start.10) | collective-permute-done | bytes 131104 | tf_op jit(solution)/shard_map/ppermute | solution.py:320
  69.8 0.8 collective-permute-done.9.refs_1_
  70.6 0.5 shard_map.126
  71.1 16.3 %all_to_all.10 = bf16[32,8,512]{2,1,0:T(8,128)(2,1)S(1)} all-to-all(bf16[32,8,512]{2,1,0:T(8,128)(2,1)S(1)} %bitcast.10), channel_id=1, replica_groups=mesh['req'=32,'tp'=4] {'req'}, dimensions={0} | all-to-all | bytes 524288 | tf_op jit(solution)/shard_map/all_to_all | solution.py:448
  87.4 0.8 shard_map.127
Async XLA Ops:
  2.0 18.4 %all-to-all-start = ((bf16[32,8,512]{2,1,0:T(8,128)(2,1)}), bf16[32,8,512]{2,1,0:T(8,128)(2,1)S(1)}, u32[]{:S(2)}, u32[]{:S(2)}) async-start(bf16[32,8,512]{2,1,0:T(8,128)(2,1)} %bitcast.1), calls=%async_computation | async-start | bytes 524288 | tf_op jit(solution)/shard_map/all_to_all | solution.py:448
  11.5 0.7 copy-start.2
  12.2 0.7 copy-start.3
  12.9 0.7 copy-start.4
  28.0 10.2 %copy-start = (f32[2,2048]{1,0:T(2,128)S(1)}, f32[2,2048]{1,0:T(2,128)}, u32[]{:S(2)}) copy-start(f32[2,2048]{1,0:T(2,128)} %refs_5_.6) | copy-start | bytes 49156
  28.0 9.4 %collective-permute-start.2 = (bf16[32,2048]{1,0:T(8,128)(2,1)S(1)}, bf16[32,2048]{1,0:T(8,128)(2,1)S(1)}, u32[]{:S(2)}, u32[]{:S(2)}) collective-permute-start(bf16[32,2048]{1,0:T(8,128)(2,1)S(1)} %get-tuple-element.29.refs_0_), channel_id=1, source_target_pairs={{0,1},{1,2},{2,3},{3,0},{4,5},{5,6},{6,7},{7,4},{8,9},{9,10},{10,1... | collective-permute-start | bytes 393224 | tf_op jit(solution)/shard_map/ppermute | solution.py:320
  29.3 8.9 %collective-permute-start.1 = (bf16[32,2048]{1,0:T(8,128)(2,1)S(1)}, bf16[32,2048]{1,0:T(8,128)(2,1)S(1)}, u32[]{:S(2)}, u32[]{:S(2)}) collective-permute-start(bf16[32,2048]{1,0:T(8,128)(2,1)S(1)} %get-tuple-element.29.refs_0_), channel_id=1, source_target_pairs={{0,2},{1,3},{2,0},{3,1},{4,6},{5,7},{6,4},{7,5},{8,10},{9,11},{10,... | collective-permute-start | bytes 393224 | tf_op jit(solution)/shard_map/ppermute | solution.py:320
  32.0 6.3 %collective-permute-start = (bf16[32,2048]{1,0:T(8,128)(2,1)S(1)}, bf16[32,2048]{1,0:T(8,128)(2,1)S(1)}, u32[]{:S(2)}, u32[]{:S(2)}) collective-permute-start(bf16[32,2048]{1,0:T(8,128)(2,1)S(1)} %get-tuple-element.29.refs_0_), channel_id=1, source_target_pairs={{0,3},{1,0},{2,1},{3,2},{4,7},{5,4},{6,5},{7,6},{8,11},{9,8},{10,9... | collective-permute-start | bytes 393224 | tf_op jit(solution)/shard_map/ppermute | solution.py:320
  40.0 8.3 %copy-start.1 = (f32[2,2048]{1,0:T(2,128)S(1)}, f32[2,2048]{1,0:T(2,128)}, u32[]{:S(2)}) copy-start(f32[2,2048]{1,0:T(2,128)} %refs_5_.7) | copy-start | bytes 49156
  40.0 7.7 %collective-permute-start.5 = (bf16[32,2048]{1,0:T(8,128)(2,1)S(1)}, bf16[32,2048]{1,0:T(8,128)(2,1)S(1)}, u32[]{:S(2)}, u32[]{:S(2)}) collective-permute-start(bf16[32,2048]{1,0:T(8,128)(2,1)S(1)} %get-tuple-element.33.after_ref.refs_0_), channel_id=1, source_target_pairs={{0,1},{1,2},{2,3},{3,0},{4,5},{5,6},{6,7},{7,4},{8,9},{9,10},{10,1... | collective-permute-start | bytes 393224 | tf_op jit(solution)/shard_map/ppermute | solution.py:320
  40.8 7.5 %collective-permute-start.4 = (bf16[32,2048]{1,0:T(8,128)(2,1)S(1)}, bf16[32,2048]{1,0:T(8,128)(2,1)S(1)}, u32[]{:S(2)}, u32[]{:S(2)}) collective-permute-start(bf16[32,2048]{1,0:T(8,128)(2,1)S(1)} %get-tuple-element.33.after_ref.refs_0_), channel_id=1, source_target_pairs={{0,2},{1,3},{2,0},{3,1},{4,6},{5,7},{6,4},{7,5},{8,10},{9,11},{10,... | collective-permute-start | bytes 393224 | tf_op jit(solution)/shard_map/ppermute | solution.py:320
  43.2 5.1 %collective-permute-start.3 = (bf16[32,2048]{1,0:T(8,128)(2,1)S(1)}, bf16[32,2048]{1,0:T(8,128)(2,1)S(1)}, u32[]{:S(2)}, u32[]{:S(2)}) collective-permute-start(bf16[32,2048]{1,0:T(8,128)(2,1)S(1)} %get-tuple-element.33.after_ref.refs_0_), channel_id=1, source_target_pairs={{0,3},{1,0},{2,1},{3,2},{4,7},{5,4},{6,5},{7,6},{8,11},{9,8},{10,9... | collective-permute-start | bytes 393224 | tf_op jit(solution)/shard_map/ppermute | solution.py:320
  52.4 5.4 %collective-permute-start.8 = (bf16[32,2048]{1,0:T(8,128)(2,1)S(1)}, bf16[32,2048]{1,0:T(8,128)(2,1)S(1)}, u32[]{:S(2)}, u32[]{:S(2)}) collective-permute-start(bf16[32,2048]{1,0:T(8,128)(2,1)S(1)} %get-tuple-element.39.refs_0_), channel_id=1, source_target_pairs={{0,1},{1,2},{2,3},{3,0},{4,5},{5,6},{6,7},{7,4},{8,9},{9,10},{10,1... | collective-permute-start | bytes 393224 | tf_op jit(solution)/shard_map/ppermute | solution.py:320
  54.9 6.1 %collective-permute-start.7 = (bf16[32,2048]{1,0:T(8,128)(2,1)S(1)}, bf16[32,2048]{1,0:T(8,128)(2,1)S(1)}, u32[]{:S(2)}, u32[]{:S(2)}) collective-permute-start(bf16[32,2048]{1,0:T(8,128)(2,1)S(1)} %get-tuple-element.39.refs_0_), channel_id=1, source_target_pairs={{0,2},{1,3},{2,0},{3,1},{4,6},{5,7},{6,4},{7,5},{8,10},{9,11},{10,... | collective-permute-start | bytes 393224 | tf_op jit(solution)/shard_map/ppermute | solution.py:320
  56.6 4.9 %collective-permute-start.6 = (bf16[32,2048]{1,0:T(8,128)(2,1)S(1)}, bf16[32,2048]{1,0:T(8,128)(2,1)S(1)}, u32[]{:S(2)}, u32[]{:S(2)}) collective-permute-start(bf16[32,2048]{1,0:T(8,128)(2,1)S(1)} %get-tuple-element.39.refs_0_), channel_id=1, source_target_pairs={{0,3},{1,0},{2,1},{3,2},{4,7},{5,4},{6,5},{7,6},{8,11},{9,8},{10,9... | collective-permute-start | bytes 393224 | tf_op jit(solution)/shard_map/ppermute | solution.py:320
  63.3 5.0 %collective-permute-start.11 = (bf16[32,2048]{1,0:T(8,128)(2,1)S(1)}, bf16[32,2048]{1,0:T(8,128)(2,1)S(1)}, u32[]{:S(2)}, u32[]{:S(2)}) collective-permute-start(bf16[32,2048]{1,0:T(8,128)(2,1)S(1)} %get-tuple-element.41.refs_0_), channel_id=1, source_target_pairs={{0,1},{1,2},{2,3},{3,0},{4,5},{5,6},{6,7},{7,4},{8,9},{9,10},{10,1... | collective-permute-start | bytes 393224 | tf_op jit(solution)/shard_map/ppermute | solution.py:320
  63.6 6.2 %collective-permute-start.10 = (bf16[32,2048]{1,0:T(8,128)(2,1)S(1)}, bf16[32,2048]{1,0:T(8,128)(2,1)S(1)}, u32[]{:S(2)}, u32[]{:S(2)}) collective-permute-start(bf16[32,2048]{1,0:T(8,128)(2,1)S(1)} %get-tuple-element.41.refs_0_), channel_id=1, source_target_pairs={{0,2},{1,3},{2,0},{3,1},{4,6},{5,7},{6,4},{7,5},{8,10},{9,11},{10,... | collective-permute-start | bytes 393224 | tf_op jit(solution)/shard_map/ppermute | solution.py:320
  66.1 4.5 %collective-permute-start.9 = (bf16[32,2048]{1,0:T(8,128)(2,1)S(1)}, bf16[32,2048]{1,0:T(8,128)(2,1)S(1)}, u32[]{:S(2)}, u32[]{:S(2)}) collective-permute-start(bf16[32,2048]{1,0:T(8,128)(2,1)S(1)} %get-tuple-element.41.refs_0_), channel_id=1, source_target_pairs={{0,3},{1,0},{2,1},{3,2},{4,7},{5,4},{6,5},{7,6},{8,11},{9,8},{10,9... | collective-permute-start | bytes 393224 | tf_op jit(solution)/shard_map/ppermute | solution.py:320
